TPU v7x, 32 devices: a whole 2x2x4 slice. The times are simulated.
32 devices in a mesh: gx: 2 (over y), gy: 4 (over z), gz: 4 (over x, core).
Axes of the slice: x: 2, y: 2, z: 4, core: 2. Of those that a mesh axis runs over, the one named last changes fastest.
Arguments:
- source_term: float32 [32, 8, 32, 512], P(None, 'gx', 'gy', 'gz'), may hold values from -16 to 16
- labels: int32 [8, 32, 512], P('gx', 'gy', 'gz'), may hold values from 0 to 5
- conductivity_table: float32 [6], replicated, may hold values from 0.05 to 1
- send_map: int32 [2, 4, 4, 256], P('gx', 'gy', 'gz'), may hold values from -1 to 4095, as said below
- owner_slots: int32 [4096], P(('gx', 'gy', 'gz')), may hold values from 0 to 255, as said below
- sensor_data: float32 [32, 128], replicated, may hold values from -6 to 6
Outputs:
- projections: float32 [3, 128, 4096], P(None, None, ('gx', 'gy', 'gz'))
- gram_blocks: float32 [6, 4096], P(None, ('gx', 'gy', 'gz'))
Inputs may be any that keep to these rules, and one draw needn't show every extreme that they name: `send_map`: entries q * 32 to q * 32 + 31 of row (sx, sy, iz) hold, in their first slots, the brick-local voxels (i * 8 + j) * 128 + k of the positions that this brick sends to owner q = ix * 4 + iy of the same iz, and -1 in the others; no voxel appears twice in a row; some brick fills all 32 slots of some owner. `owner_slots`: the 128 entries of owner d = (ix * 4 + iy) * 4 + iz name, each once, exactly the slots src * 32 + slot that the bricks src = sx * 4 + sy with the same iz fill for it.
All inputs are finite; a program needn't handle non-finite values.
Results may differ from a plain program's by a relative error of at most 0.00012.
Values sent between devices are 32-bit elements; how exact they have to be, the bound alone decides.
No kernel may reach another device: no remote copies, remote signals or barrier semaphores. Data moves between devices by JAX's collectives and lax.ppermute only.
A program may use at most 64 MiB of HBM per device.

v0:
```python
import jax
import jax.numpy as jnp
from jax import lax
from jax.sharding import PartitionSpec as P

mass_term = 0.25


def extended(block, sides, width):
    for axis, dim in sides:
        count = lax.axis_size(axis)
        forward = [(i, i + 1) for i in range(count - 1)]
        backward = [(target, source) for source, target in forward]
        low = lax.ppermute(
            lax.slice_in_dim(block, block.shape[dim] - width, None, axis=dim), axis, forward
        )
        high = lax.ppermute(lax.slice_in_dim(block, 0, width, axis=dim), axis, backward)
        block = jnp.concatenate([low, block, high], axis=dim)
    return block


def tissue(shifted, table):
    conductivity = jnp.zeros(shifted.shape, table.dtype)
    for tissue_level in range(table.shape[0]):
        conductivity = conductivity + jnp.where(
            shifted == tissue_level + 1, table[tissue_level], 0.0
        )
    inside = (shifted > 0).astype(table.dtype)
    return (conductivity, inside)


def neighbour_slices(dim_index, offset):
    selection = [slice(1, -1), slice(1, -1), slice(1, -1)]
    selection[dim_index] = slice(2, None) if offset > 0 else slice(0, -2)
    return tuple(selection)


def stencil(padded, conductivity, inside):
    leading = (slice(None),) * (padded.ndim - 3)
    middle = (slice(1, -1), slice(1, -1), slice(1, -1))
    centre = padded[leading + middle]
    own_cond = conductivity[middle]
    own_in = inside[middle]
    accumulated = mass_term * centre
    for dim_index in range(3):
        for offset in (-1, 1):
            beside_all = neighbour_slices(dim_index, offset)
            weight = 0.5 * (own_cond + conductivity[beside_all]) * own_in * inside[beside_all]
            accumulated = accumulated + weight * (centre - padded[leading + beside_all])
    return accumulated


def gram_rows(leadfield):
    entry_pairs = ((0, 0), (1, 1), (2, 2), (0, 1), (0, 2), (1, 2))
    return jnp.stack(
        [jnp.sum(leadfield[first] * leadfield[second], axis=0) for first, second in entry_pairs]
    )


def local_inner(first, second):
    return jnp.sum(first * second, axis=(1, 2, 3))


def per_sensor(values):
    return values[:, None, None, None]


def per_device(source_term, labels, conductivity_table, send_map, owner_slots, sensor_data):
    sensors, size_x, size_y, size_z = source_term.shape
    shifted = labels + 1
    label_pad = extended(shifted, (("gx", 0), ("gy", 1), ("gz", 2)), 2)
    conductivity, inside = tissue(label_pad, conductivity_table)
    source_pad = extended(source_term, (("gx", 1), ("gy", 2), ("gz", 3)), 2)
    applied = stencil(source_pad, conductivity, inside)
    inner_cond = conductivity[1:-1, 1:-1, 1:-1]
    inner_in = inside[1:-1, 1:-1, 1:-1]
    twice_applied = stencil(applied, inner_cond, inner_in)
    applied_core = applied[:, 1:-1, 1:-1, 1:-1]
    moment_zero, moment_one, moment_two, moment_three = lax.psum(
        (
            local_inner(source_term, source_term),
            local_inner(source_term, applied_core),
            local_inner(applied_core, applied_core),
            local_inner(applied_core, twice_applied),
        ),
        ("gx", "gy", "gz"),
    )
    first_step = moment_zero / moment_one
    residue = first_step * first_step * moment_two - moment_zero
    growth = 1.0 + residue / moment_zero
    curvature = (
        growth * growth * moment_one
        - 2.0 * growth * first_step * moment_two
        + first_step * first_step * moment_three
    )
    second_step = residue / curvature
    source_coef = first_step + second_step * growth
    applied_coef = second_step * first_step
    solution_pad = (
        per_sensor(source_coef) * source_pad[:, 1:-1, 1:-1, 1:-1]
        - per_sensor(applied_coef) * applied
    )
    cond_inner = conductivity[2:-2, 2:-2, 2:-2]
    voxel_local = jnp.maximum(send_map.reshape(-1), 0)
    index_x = voxel_local // (size_y * size_z)
    index_y = voxel_local // size_z % size_y
    index_z = voxel_local % size_z
    stride_y = size_z + 2
    stride_x = (size_y + 2) * (size_z + 2)
    centre = (index_x + 1) * stride_x + (index_y + 1) * stride_y + (index_z + 1)
    flattened = solution_pad.reshape(sensors, -1)
    cond_here = jnp.take(cond_inner.reshape(-1), voxel_local)

    def gradient(stride):
        upper = jnp.take(flattened, centre + stride, axis=1)
        lower = jnp.take(flattened, centre - stride, axis=1)
        return cond_here * ((upper - lower) * 0.5)

    columns = jnp.stack([gradient(stride_x), gradient(stride_y), gradient(1)])
    received = lax.all_to_all(columns, ("gx", "gy"), split_axis=2, concat_axis=2, tiled=True)
    owned = jnp.take(received, owner_slots, axis=2)
    projections = jnp.einsum("csp,st->ctp", owned, sensor_data, precision=lax.Precision.HIGHEST)
    return (projections, gram_rows(owned))


def solution(mesh):
    in_specs = (
        P(None, "gx", "gy", "gz"),
        P("gx", "gy", "gz"),
        P(),
        P("gx", "gy", "gz", None),
        P(("gx", "gy", "gz")),
        P(),
    )
    out_specs = (P(None, None, ("gx", "gy", "gz")), P(None, ("gx", "gy", "gz")))
    return jax.shard_map(
        per_device, mesh=mesh, in_specs=in_specs, out_specs=out_specs, check_vma=False
    )
```

profile of v0, /device:TPU:0, one launch (start us, length us, event | category | flops | bytes accessed | tf_op | source)
XLA Modules:
  0.0 188.7 jit_solution(1903327529436321746)
XLA Ops:
  0.6 0.7 broadcast_add_fusion
  1.4 4.9 %collective-permute-start.6 = (s32[2,8,128]{2,1,0:T(8,128)S(1)}, s32[2,8,128]{2,1,0:T(8,128)S(1)}, u32[]{:S(2)}, u32[]{:S(2)}) collective-permute-start(s32[2,8,128]{2,1,0:T(8,128)S(1)} %get-tuple-element.58), channel_id=1, source_target_pairs={{0,16},{1,17},{2,18},{3,19},{4,20},{5,21},{6,22},{7,23},{8,24},{9,... | collective-permute-start | bytes 24584 | tf_op jit(solution)/shard_map/ppermute | solution.py:14
  6.3 1.3 collective-permute-start.7
  7.6 1.1 fusion.70
  8.7 4.6 %collective-permute-start = (f32[32,2,8,128]{3,2,1,0:T(8,128)S(1)}, f32[32,2,8,128]{3,2,1,0:T(8,128)S(1)}, u32[]{:S(2)}, u32[]{:S(2)}) collective-permute-start(f32[32,2,8,128]{3,2,1,0:T(8,128)S(1)} %get-tuple-element.39), channel_id=1, source_target_pairs={{0,16},{1,17},{2,18},{3,19},{4,20},{5,21},{6,22},{7,23},{8,24},{9,... | collective-permute-start | bytes 786440 | tf_op jit(solution)/shard_map/ppermute | solution.py:14
  13.2 1.3 collective-permute-start.1
  14.5 1.9 multiply_reduce_fusion.2
  16.4 0.7 compare_reduce_fusion
  17.1 0.7 broadcast_maximum_fusion
  18.3 0.6 compare_and_fusion.4
  19.0 0.7 compare_select_fusion.6
  19.6 1.5 fusion.73
  23.0 3.5 %collective-permute-start.8 = (s32[8,2,128]{2,1,0:T(2,128)S(1)}, s32[8,2,128]{2,1,0:T(2,128)S(1)}, u32[]{:S(2)}, u32[]{:S(2)}) collective-permute-start(s32[8,2,128]{2,1,0:T(2,128)S(1)} %get-tuple-element.56), channel_id=1, source_target_pairs={{0,4},{4,8},{8,12},{1,5},{5,9},{9,13},{2,6},{6,10},{10,14},{3,7},{... | collective-permute-start | bytes 24584 | tf_op jit(solution)/shard_map/ppermute | solution.py:14
  26.4 1.3 collective-permute-start.9
  28.3 3.6 %collective-permute-done.9 = s32[8,2,128]{2,1,0:T(2,128)S(1)} collective-permute-done((s32[8,2,128]{2,1,0:T(2,128)S(1)}, s32[8,2,128]{2,1,0:T(2,128)S(1)}, u32[]{:S(2)}, u32[]{:S(2)}) %collective-permute-start.9) | collective-permute-done | bytes 8224 | tf_op jit(solution)/shard_map/ppermute | solution.py:17
  32.1 1.3 collective-permute-start.10
  33.4 1.3 collective-permute-start.11
  34.7 1.2 copy.105
  35.9 2.4 %collective-permute-done.11 = s32[8,12,2]{2,1,0:T(8,128)S(1)} collective-permute-done((s32[8,12,2]{2,1,0:T(8,128)S(1)}, s32[8,12,2]{2,1,0:T(8,128)S(1)}, u32[]{:S(2)}, u32[]{:S(2)}) %collective-permute-start.11) | collective-permute-done | bytes 800 | tf_op jit(solution)/shard_map/ppermute | solution.py:17
  38.4 3.8 %select_add_fusion = f32[8,12,132]{2,1,0:T(8,128)S(1)} fusion(f32[]{:T(128)} %bitcast.8, f32[]{:T(128)} %bitcast.7, f32[]{:T(128)} %bitcast.6, f32[]{:T(128)} %bitcast.5, f32[]{:T(128)} %bitcast.4, f32[]{:T(128)} %bitcast.3, s32[8,12,2]{2,1,0:T(8,128)S(1)} %collective-permute-done.11, s32[8,2,128]{2,1,0:T(2,128)S(1)} %collective-permute-done.9, ...), kind=kLoop, calls=%fused_computation.79 | loop fusion | flops 291456 | bytes 101400 | tf_op jit(solution)/shard_map/add | solution.py:25
  42.2 0.7 slice_multiply_fusion.11
  43.7 3.5 %collective-permute-start.2 = (f32[32,8,2,128]{3,1,2,0:T(8,128)S(1)}, f32[32,8,2,128]{3,1,2,0:T(8,128)S(1)}, u32[]{:S(2)}, u32[]{:S(2)}) collective-permute-start(f32[32,8,2,128]{3,1,2,0:T(8,128)S(1)} %get-tuple-element.37), channel_id=1, source_target_pairs={{0,4},{4,8},{8,12},{1,5},{5,9},{9,13},{2,6},{6,10},{10,14},{3,7},{... | collective-permute-start | bytes 786440 | tf_op jit(solution)/shard_map/ppermute | solution.py:14
  47.2 1.3 collective-permute-start.3
  48.5 0.7 slice_multiply_fusion.7
  49.2 1.7 gather_fusion
  51.2 0.7 collective-permute-done.2
  51.9 4.7 %collective-permute-done.3 = f32[32,8,2,128]{3,1,2,0:T(8,128)S(1)} collective-permute-done((f32[32,8,2,128]{3,1,2,0:T(8,128)S(1)}, f32[32,8,2,128]{3,1,2,0:T(8,128)S(1)}, u32[]{:S(2)}, u32[]{:S(2)}) %collective-permute-start.3) | collective-permute-done | bytes 262176 | tf_op jit(solution)/shard_map/ppermute | solution.py:17
  56.6 0.7 copy-done.11
  57.6 1.8 fusion.69
  59.4 2.2 %copy.93 = f32[32,8,12,2]{0,1,3,2:T(8,128)S(1)} copy(f32[32,8,12,2]{3,1,2,0:T(8,128)} %get-tuple-element.35) | data formatting | bytes 49152 | tf_op jit(solution)/shard_map/slice | solution.py:15
  61.6 0.9 copy.94
  62.5 1.3 collective-permute-start.5
  63.8 4.2 %collective-permute-start.4 = (f32[32,8,12,2]{0,1,3,2:T(8,128)S(1)}, f32[32,8,12,2]{0,1,3,2:T(8,128)S(1)}, u32[]{:S(2)}, u32[]{:S(2)}) collective-permute-start(f32[32,8,12,2]{0,1,3,2:T(8,128)S(1)} %copy.93), channel_id=1, source_target_pairs={{0,1},{1,2},{2,3},{4,5},{5,6},{6,7},{8,9},{9,10},{10,11},{12,13},{... | collective-permute-start | bytes 73736 | tf_op jit(solution)/shard_map/ppermute | solution.py:14
  68.6 0.6 copy.106
  69.2 0.6 copy.109
  71.1 0.7 copy.98
  71.7 0.7 copy.99
  72.4 0.7 copy.97
  73.1 0.7 copy.101
  73.8 0.7 copy.100
  74.5 2.4 %copy.95 = f32[32,8,12,2]{3,1,2,0:T(8,128)} copy(f32[32,8,12,2]{0,1,3,2:T(8,128)S(1)} %collective-permute-done.4) | data formatting | bytes 49152 | tf_op jit(solution)/shard_map/ppermute | solution.py:14
  76.8 2.4 %copy.96 = f32[32,8,12,2]{3,1,2,0:T(8,128)} copy(f32[32,8,12,2]{0,1,3,2:T(8,128)S(1)} %collective-permute-done.5) | data formatting | bytes 49152 | tf_op jit(solution)/shard_map/ppermute | solution.py:17
  79.3 4.8 %pad_maximum_fusion = f32[32,8,12,132]{3,1,2,0:T(8,128)S(1)} fusion(f32[32,8,12,2]{3,1,2,0:T(8,128)} %copy.96, f32[32,8,2,128]{3,1,2,0:T(8,128)} %copy-done.11, f32[32,2,8,128]{3,1,2,0:T(2,128)} %copy-done.7, f32[32,4,8,128]{3,1,2,0:T(4,128)} %copy-done.4, f32[32,2,8,128]{3,1,2,0:T(2,128)S(1)} %copy.90, f32[32,8,2,128]{3,1,2,0:T(8,128)} %copy-done.9, ...), kind=kLoop, calls=%fused_computation.8 | loop fusion | flops 2433024 | bytes 3244032 | tf_op jit(solution)/shard_map/concatenate | solution.py:18
  84.3 7.2 %fusion.2 = f32[32,6,10,130]{3,1,2,0:T(8,128)S(1)} fusion(f32[32,8,12,2]{3,1,2,0:T(8,128)S(1)} %copy-done.3, f32[32,8,2,128]{3,1,2,0:T(8,128)S(1)} %copy-done.12, f32[32,8,2,128]{3,1,2,0:T(8,128)S(1)} %copy-done.10, f32[32,2,8,128]{3,1,2,0:T(2,128)S(1)} %copy-done.8, f32[32,4,8,128]{3,1,2,0:T(4,128)S(1)} %copy-done.5, f32[32,2,8,128]{3,1,2,0:T(2,128)S(1)} %copy.90, ...), kind=kLoop, calls=%fused_computation.12 | loop fusion | flops 7238400 | bytes 7799616 | tf_op jit(solution)/shard_map/add | solution.py:49
  91.5 1.5 copy-done.1
  93.1 2.4 %multiply_reduce_fusion.1 = (f32[32]{0:T(128)S(1)}, f32[32]{0:T(128)S(1)}, f32[32]{0:T(128)S(1)}) fusion(f32[32,6,10,130]{3,1,2,0:T(8,128)S(1)} %fusion.2, f32[32,4,8,128]{3,2,1,0:T(8,128)S(1)} %copy-done.6, f32[4,8,128]{2,0,1:T(4,128)S(1)} %copy.111, f32[4,8,128]{2,0,1:T(4,128)S(1)} %copy.110, f32[4,8,128]{2,0,1:T(4,128)S(1)} %copy-done.19, ...), kind=kLoop, calls=%fused_computation.60 | loop fusion | flops 3276704 | bytes 4292992 | tf_op jit(solution)/shard_map/reduce_sum | solution.py:61
  95.4 41.9 %all-reduce = (f32[32]{0:T(128)S(1)}, f32[32]{0:T(128)S(1)}, f32[32]{0:T(128)S(1)}, f32[32]{0:T(128)S(1)}) all-reduce(f32[32]{0:T(128)S(1)} %get-tuple-element.15, f32[32]{0:T(128)S(1)} %get-tuple-element.14, f32[32]{0:T(128)S(1)} %copy-done.32, f32[32]{0:T(128)S(1)} %get-tuple-element.13), channel_id=1, replica_groups=mesh['gx'=2,'gy'=4,'gz'=4] {'gx','gy','gz'}, use_global_device_ids=true, to_apply=%region_7.8 | all-reduce | flops 128 | bytes 1024 | tf_op jit(solution)/shard_map/psum | solution.py:79
  137.4 4.1 %multiply_subtract_fusion = f32[32,6,10,130]{3,1,2,0:T(8,128)} fusion(f32[32,6,10,130]{3,1,2,0:T(8,128)} %copy-done.1, f32[32,8,12,132]{3,1,2,0:T(8,128)S(1)} %pad_maximum_fusion, f32[32]{0:T(128)S(1)} %mul.415, f32[32]{0:T(128)S(1)} %get-tuple-element.31), kind=kLoop, calls=%fused_computation.37 | loop fusion | flops 748800 | bytes 2995456 | tf_op jit(solution)/shard_map/sub | solution.py:100
  141.5 4.8 %copy.122 = f32[32,6,10,130]{0,3,2,1:T(8,128)} copy(f32[32,6,10,130]{3,1,2,0:T(8,128)} %multiply_subtract_fusion) | data formatting | bytes 1996800 | tf_op jit(solution)/shard_map/reshape | solution.py:111
  146.3 4.8 %reshape.172 = f32[32,7800]{0,1:T(8,128)} reshape(f32[32,6,10,130]{0,3,2,1:T(8,128)} %copy.122) | data formatting | bytes 1996800 | tf_op jit(solution)/shard_map/reshape | solution.py:111
  151.1 3.0 %gather_fusion.7 = f32[256,32]{1,0:T(8,128)S(1)} fusion(f32[32,7800]{0,1:T(8,128)} %reshape.172, s32[1024]{0:T(1024)} %get-tuple-element.84), kind=kCustom, calls=%fused_computation.5.clone | custom fusion | bytes 66560 | tf_op jit(solution)/shard_map/jit(_take)/gather | solution.py:116
  154.1 3.0 %gather_fusion.6 = f32[256,32]{1,0:T(8,128)S(1)} fusion(f32[32,7800]{0,1:T(8,128)} %reshape.172, s32[1024]{0:T(1024)} %get-tuple-element.85), kind=kCustom, calls=%fused_computation.4.clone | custom fusion | bytes 66560 | tf_op jit(solution)/shard_map/jit(_take)/gather | solution.py:115
  157.1 3.0 %gather_fusion.5 = f32[256,32]{1,0:T(8,128)S(1)} fusion(f32[32,7800]{0,1:T(8,128)} %reshape.172, s32[1024]{0:T(1024)} %get-tuple-element.86), kind=kCustom, calls=%fused_computation.3.clone | custom fusion | bytes 66560 | tf_op jit(solution)/shard_map/jit(_take)/gather | solution.py:116
  160.1 3.0 %gather_fusion.4 = f32[256,32]{1,0:T(8,128)S(1)} fusion(f32[32,7800]{0,1:T(8,128)} %reshape.172, s32[1024]{0:T(1024)} %get-tuple-element.87), kind=kCustom, calls=%fused_computation.2.clone | custom fusion | bytes 66560 | tf_op jit(solution)/shard_map/jit(_take)/gather | solution.py:115
  163.1 3.0 %gather_fusion.3 = f32[256,32]{1,0:T(8,128)S(1)} fusion(f32[32,7800]{0,1:T(8,128)} %reshape.172, s32[1024]{0:T(1024)} %get-tuple-element.88), kind=kCustom, calls=%fused_computation.1.clone | custom fusion | bytes 66560 | tf_op jit(solution)/shard_map/jit(_take)/gather | solution.py:116
  166.1 3.0 %gather_fusion.2 = f32[256,32]{1,0:T(8,128)S(1)} fusion(f32[32,7800]{0,1:T(8,128)} %reshape.172, s32[1024]{0:T(1024)} %get-tuple-element.89), kind=kCustom, calls=%fused_computation.clone | custom fusion | bytes 66560 | tf_op jit(solution)/shard_map/jit(_take)/gather | solution.py:115
  169.8 1.0 reshape.176
  170.8 4.5 %all-to-all-start = ((f32[8,1,3072]{2,1,0:T(1,128)}), f32[8,1,3072]{2,1,0:T(1,128)S(1)}, u32[]{:S(2)}, u32[]{:S(2)}) async-start(f32[8,1,3072]{2,1,0:T(1,128)} %reshape.176), calls=%async_computation | async-start | bytes 196608 | tf_op jit(solution)/shard_map/all_to_all | solution.py:120
  175.3 7.2 %all-to-all-done = f32[8,1,3072]{2,1,0:T(1,128)S(1)} async-done(((f32[8,1,3072]{2,1,0:T(1,128)}), f32[8,1,3072]{2,1,0:T(1,128)S(1)}, u32[]{:S(2)}, u32[]{:S(2)}) %all-to-all-start) | async-done | bytes 98336 | tf_op jit(solution)/shard_map/all_to_all | solution.py:120
  183.0 0.9 reduce.12
  184.3 0.9 gather_fusion.1
  185.3 1.6 multiply_reduce_fusion.3
  187.3 0.8 copy.121
  188.1 0.6 stack.43
  (111 shorter events, 8.5 us)
Async XLA Ops:
  0.6 186.3 %copy-start = (f32[32,128]{1,0:T(8,128)S(1)}, f32[32,128]{1,0:T(8,128)}, u32[]{:S(2)}) copy-start(f32[32,128]{1,0:T(8,128)} %param.13) | copy-start | bytes 49156
  1.4 21.6 %collective-permute-start.6 = (s32[2,8,128]{2,1,0:T(8,128)S(1)}, s32[2,8,128]{2,1,0:T(8,128)S(1)}, u32[]{:S(2)}, u32[]{:S(2)}) collective-permute-start(s32[2,8,128]{2,1,0:T(8,128)S(1)} %get-tuple-element.58), channel_id=1, source_target_pairs={{0,16},{1,17},{2,18},{3,19},{4,20},{5,21},{6,22},{7,23},{8,24},{9,... | collective-permute-start | bytes 24584 | tf_op jit(solution)/shard_map/ppermute | solution.py:14
  6.3 16.7 %collective-permute-start.7 = (s32[2,8,128]{2,1,0:T(8,128)S(1)}, s32[2,8,128]{2,1,0:T(8,128)S(1)}, u32[]{:S(2)}, u32[]{:S(2)}) collective-permute-start(s32[2,8,128]{2,1,0:T(8,128)S(1)} %get-tuple-element.59), channel_id=1, source_target_pairs={{16,0},{17,1},{18,2},{19,3},{20,4},{21,5},{22,6},{23,7},{24,8},{25... | collective-permute-start | bytes 24584 | tf_op jit(solution)/shard_map/ppermute | solution.py:17
  8.7 34.5 %collective-permute-start = (f32[32,2,8,128]{3,2,1,0:T(8,128)S(1)}, f32[32,2,8,128]{3,2,1,0:T(8,128)S(1)}, u32[]{:S(2)}, u32[]{:S(2)}) collective-permute-start(f32[32,2,8,128]{3,2,1,0:T(8,128)S(1)} %get-tuple-element.39), channel_id=1, source_target_pairs={{0,16},{1,17},{2,18},{3,19},{4,20},{5,21},{6,22},{7,23},{8,24},{9,... | collective-permute-start | bytes 786440 | tf_op jit(solution)/shard_map/ppermute | solution.py:14
  13.2 30.1 %collective-permute-start.1 = (f32[32,2,8,128]{3,2,1,0:T(8,128)S(1)}, f32[32,2,8,128]{3,2,1,0:T(8,128)S(1)}, u32[]{:S(2)}, u32[]{:S(2)}) collective-permute-start(f32[32,2,8,128]{3,2,1,0:T(8,128)S(1)} %get-tuple-element.40), channel_id=1, source_target_pairs={{16,0},{17,1},{18,2},{19,3},{20,4},{21,5},{22,6},{23,7},{24,8},{25... | collective-permute-start | bytes 786440 | tf_op jit(solution)/shard_map/ppermute | solution.py:17
  23.0 5.4 %collective-permute-start.8 = (s32[8,2,128]{2,1,0:T(2,128)S(1)}, s32[8,2,128]{2,1,0:T(2,128)S(1)}, u32[]{:S(2)}, u32[]{:S(2)}) collective-permute-start(s32[8,2,128]{2,1,0:T(2,128)S(1)} %get-tuple-element.56), channel_id=1, source_target_pairs={{0,4},{4,8},{8,12},{1,5},{5,9},{9,13},{2,6},{6,10},{10,14},{3,7},{... | collective-permute-start | bytes 24584 | tf_op jit(solution)/shard_map/ppermute | solution.py:14
  26.4 5.5 %collective-permute-start.9 = (s32[8,2,128]{2,1,0:T(2,128)S(1)}, s32[8,2,128]{2,1,0:T(2,128)S(1)}, u32[]{:S(2)}, u32[]{:S(2)}) collective-permute-start(s32[8,2,128]{2,1,0:T(2,128)S(1)} %get-tuple-element.57), channel_id=1, source_target_pairs={{4,0},{8,4},{12,8},{5,1},{9,5},{13,9},{6,2},{10,6},{14,10},{7,3},{... | collective-permute-start | bytes 24584 | tf_op jit(solution)/shard_map/ppermute | solution.py:17
  32.1 3.8 %collective-permute-start.10 = (s32[8,12,2]{2,1,0:T(8,128)S(1)}, s32[8,12,2]{2,1,0:T(8,128)S(1)}, u32[]{:S(2)}, u32[]{:S(2)}) collective-permute-start(s32[8,12,2]{2,1,0:T(8,128)S(1)} %get-tuple-element.54), channel_id=1, source_target_pairs={{0,1},{1,2},{2,3},{4,5},{5,6},{6,7},{8,9},{9,10},{10,11},{12,13},{... | collective-permute-start | bytes 2312 | tf_op jit(solution)/shard_map/ppermute | solution.py:14
  33.4 4.9 %collective-permute-start.11 = (s32[8,12,2]{2,1,0:T(8,128)S(1)}, s32[8,12,2]{2,1,0:T(8,128)S(1)}, u32[]{:S(2)}, u32[]{:S(2)}) collective-permute-start(s32[8,12,2]{2,1,0:T(8,128)S(1)} %get-tuple-element.55), channel_id=1, source_target_pairs={{1,0},{2,1},{3,2},{5,4},{6,5},{7,6},{9,8},{10,9},{11,10},{13,12},{... | collective-permute-start | bytes 2312 | tf_op jit(solution)/shard_map/ppermute | solution.py:17
  35.9 20.7 %copy-start.4 = (f32[32,4,8,128]{3,1,2,0:T(4,128)}, f32[32,4,8,128]{3,1,2,0:T(4,128)S(1)}, u32[]{:S(2)}) copy-start(f32[32,4,8,128]{3,1,2,0:T(4,128)S(1)} %copy.105) | copy-start | bytes 1572868
  43.5 14.2 %copy-start.7 = (f32[32,2,8,128]{3,1,2,0:T(2,128)}, f32[32,2,8,128]{3,1,2,0:T(2,128)S(1)}, u32[]{:S(2)}) copy-start(f32[32,2,8,128]{3,1,2,0:T(2,128)S(1)} %copy.92) | copy-start | bytes 786436
  43.7 8.2 %collective-permute-start.2 = (f32[32,8,2,128]{3,1,2,0:T(8,128)S(1)}, f32[32,8,2,128]{3,1,2,0:T(8,128)S(1)}, u32[]{:S(2)}, u32[]{:S(2)}) collective-permute-start(f32[32,8,2,128]{3,1,2,0:T(8,128)S(1)} %get-tuple-element.37), channel_id=1, source_target_pairs={{0,4},{4,8},{8,12},{1,5},{5,9},{9,13},{2,6},{6,10},{10,14},{3,7},{... | collective-permute-start | bytes 786440 | tf_op jit(solution)/shard_map/ppermute | solution.py:14
  47.2 9.4 %collective-permute-start.3 = (f32[32,8,2,128]{3,1,2,0:T(8,128)S(1)}, f32[32,8,2,128]{3,1,2,0:T(8,128)S(1)}, u32[]{:S(2)}, u32[]{:S(2)}) collective-permute-start(f32[32,8,2,128]{3,1,2,0:T(8,128)S(1)} %get-tuple-element.38), channel_id=1, source_target_pairs={{4,0},{8,4},{12,8},{5,1},{9,5},{13,9},{6,2},{10,6},{14,10},{7,3},{... | collective-permute-start | bytes 786440 | tf_op jit(solution)/shard_map/ppermute | solution.py:17
  51.9 4.7 %copy-start.9 = (f32[32,8,2,128]{3,1,2,0:T(8,128)}, f32[32,8,2,128]{3,1,2,0:T(8,128)S(1)}, u32[]{:S(2)}) copy-start(f32[32,8,2,128]{3,1,2,0:T(8,128)S(1)} %collective-permute-done.2) | copy-start | bytes 786436
  56.6 0.7 copy-start.11
  59.4 9.2 %copy-start.25 = (f32[4,8,128]{2,1,0:T(8,128)S(1)}, f32[4,8,128]{2,1,0:T(8,128)}, u32[]{:S(2)}) copy-start(f32[4,8,128]{2,1,0:T(8,128)} %get-tuple-element.46) | copy-start | bytes 49156
  59.4 9.2 %copy-start.24 = (f32[4,8,128]{2,1,0:T(8,128)S(1)}, f32[4,8,128]{2,1,0:T(8,128)}, u32[]{:S(2)}) copy-start(f32[4,8,128]{2,1,0:T(8,128)} %get-tuple-element.41) | copy-start | bytes 49156
  59.4 9.8 %copy-start.23 = (f32[4,8,128]{2,1,0:T(8,128)S(1)}, f32[4,8,128]{2,1,0:T(8,128)}, u32[]{:S(2)}) copy-start(f32[4,8,128]{2,1,0:T(8,128)} %get-tuple-element.42) | copy-start | bytes 49156
  59.4 10.4 %copy-start.22 = (f32[4,8,128]{2,1,0:T(8,128)S(1)}, f32[4,8,128]{2,1,0:T(8,128)}, u32[]{:S(2)}) copy-start(f32[4,8,128]{2,1,0:T(8,128)} %get-tuple-element.43) | copy-start | bytes 49156
  62.5 14.3 %collective-permute-start.5 = (f32[32,8,12,2]{0,1,3,2:T(8,128)S(1)}, f32[32,8,12,2]{0,1,3,2:T(8,128)S(1)}, u32[]{:S(2)}, u32[]{:S(2)}) collective-permute-start(f32[32,8,12,2]{0,1,3,2:T(8,128)S(1)} %copy.94), channel_id=1, source_target_pairs={{1,0},{2,1},{3,2},{5,4},{6,5},{7,6},{9,8},{10,9},{11,10},{13,12},{... | collective-permute-start | bytes 73736 | tf_op jit(solution)/shard_map/ppermute | solution.py:17
  63.8 10.7 %collective-permute-start.4 = (f32[32,8,12,2]{0,1,3,2:T(8,128)S(1)}, f32[32,8,12,2]{0,1,3,2:T(8,128)S(1)}, u32[]{:S(2)}, u32[]{:S(2)}) collective-permute-start(f32[32,8,12,2]{0,1,3,2:T(8,128)S(1)} %copy.93), channel_id=1, source_target_pairs={{0,1},{1,2},{2,3},{4,5},{5,6},{6,7},{8,9},{9,10},{10,11},{12,13},{... | collective-permute-start | bytes 73736 | tf_op jit(solution)/shard_map/ppermute | solution.py:14
  79.2 4.9 %copy-start.2 = (f32[32,8,12,2]{3,1,2,0:T(8,128)S(1)}, f32[32,8,12,2]{3,1,2,0:T(8,128)}, u32[]{:S(2)}) copy-start(f32[32,8,12,2]{3,1,2,0:T(8,128)} %copy.95) | copy-start | bytes 73732
  79.2 4.9 %copy-start.3 = (f32[32,8,12,2]{3,1,2,0:T(8,128)S(1)}, f32[32,8,12,2]{3,1,2,0:T(8,128)}, u32[]{:S(2)}) copy-start(f32[32,8,12,2]{3,1,2,0:T(8,128)} %copy.96) | copy-start | bytes 73732
  79.2 4.9 %copy-start.5 = (f32[32,4,8,128]{3,1,2,0:T(4,128)S(1)}, f32[32,4,8,128]{3,1,2,0:T(4,128)}, u32[]{:S(2)}) copy-start(f32[32,4,8,128]{3,1,2,0:T(4,128)} %copy-done.4) | copy-start | bytes 1572868
  79.2 4.9 %copy-start.8 = (f32[32,2,8,128]{3,1,2,0:T(2,128)S(1)}, f32[32,2,8,128]{3,1,2,0:T(2,128)}, u32[]{:S(2)}) copy-start(f32[32,2,8,128]{3,1,2,0:T(2,128)} %copy-done.7) | copy-start | bytes 786436
  79.2 4.9 %copy-start.10 = (f32[32,8,2,128]{3,1,2,0:T(8,128)S(1)}, f32[32,8,2,128]{3,1,2,0:T(8,128)}, u32[]{:S(2)}) copy-start(f32[32,8,2,128]{3,1,2,0:T(8,128)} %copy-done.9) | copy-start | bytes 786436
  79.2 4.9 %copy-start.12 = (f32[32,8,2,128]{3,1,2,0:T(8,128)S(1)}, f32[32,8,2,128]{3,1,2,0:T(8,128)}, u32[]{:S(2)}) copy-start(f32[32,8,2,128]{3,1,2,0:T(8,128)} %copy-done.11) | copy-start | bytes 786436
  79.3 4.9 %copy-start.13 = (f32[6,10,130]{2,0,1:T(8,128)S(1)}, f32[6,10,130]{2,0,1:T(8,128)}, u32[]{:S(2)}) copy-start(f32[6,10,130]{2,0,1:T(8,128)} %copy.98) | copy-start | bytes 93604
  79.3 4.9 %copy-start.14 = (f32[6,10,130]{2,0,1:T(8,128)S(1)}, f32[6,10,130]{2,0,1:T(8,128)}, u32[]{:S(2)}) copy-start(f32[6,10,130]{2,0,1:T(8,128)} %copy.99) | copy-start | bytes 93604
  79.3 4.9 %copy-start.15 = (f32[6,10,130]{2,0,1:T(8,128)S(1)}, f32[6,10,130]{2,0,1:T(8,128)}, u32[]{:S(2)}) copy-start(f32[6,10,130]{2,0,1:T(8,128)} %copy.97) | copy-start | bytes 93604
  79.3 4.9 %copy-start.16 = (f32[6,10,130]{2,0,1:T(8,128)S(1)}, f32[6,10,130]{2,0,1:T(8,128)}, u32[]{:S(2)}) copy-start(f32[6,10,130]{2,0,1:T(8,128)} %copy.101) | copy-start | bytes 93604
  79.3 4.9 %copy-start.17 = (f32[6,10,130]{2,0,1:T(8,128)S(1)}, f32[6,10,130]{2,0,1:T(8,128)}, u32[]{:S(2)}) copy-start(f32[6,10,130]{2,0,1:T(8,128)} %copy.100) | copy-start | bytes 93604
  84.2 8.8 %copy-start.6 = (f32[32,4,8,128]{3,2,1,0:T(8,128)S(1)}, f32[32,4,8,128]{3,2,1,0:T(8,128)}, u32[]{:S(2)}) copy-start(f32[32,4,8,128]{3,2,1,0:T(8,128)} %param.8) | copy-start | bytes 1572868
  84.2 8.8 %copy-start.18 = (f32[4,8,128]{2,0,1:T(4,128)S(1)}, f32[4,8,128]{2,0,1:T(4,128)}, u32[]{:S(2)}) copy-start(f32[4,8,128]{2,0,1:T(4,128)} %copy.106) | copy-start | bytes 49156
  84.2 8.8 %copy-start.19 = (f32[4,8,128]{2,0,1:T(4,128)S(1)}, f32[4,8,128]{2,0,1:T(4,128)}, u32[]{:S(2)}) copy-start(f32[4,8,128]{2,0,1:T(4,128)} %copy.109) | copy-start | bytes 49156
  84.2 8.8 %copy-start.20 = (f32[4,8,128]{2,0,1:T(4,128)S(1)}, f32[4,8,128]{2,0,1:T(4,128)}, u32[]{:S(2)}) copy-start(f32[4,8,128]{2,0,1:T(4,128)} %copy.108) | copy-start | bytes 49156
  84.3 8.8 %copy-start.21 = (f32[4,8,128]{2,0,1:T(4,128)S(1)}, f32[4,8,128]{2,0,1:T(4,128)}, u32[]{:S(2)}) copy-start(f32[4,8,128]{2,0,1:T(4,128)} %copy.107) | copy-start | bytes 49156
  91.5 1.5 copy-start.1
  93.0 2.4 %copy-start.32 = (f32[32]{0:T(128)S(1)}, f32[32]{0:T(128)}, u32[]{:S(2)}) copy-start(f32[32]{0:T(128)} %multiply_reduce_fusion.2) | copy-start | bytes 388
  146.3 22.8 %copy-start.26 = (f32[256]{0:T(256)S(1)}, f32[256]{0:T(256)}, u32[]{:S(2)}) copy-start(f32[256]{0:T(256)} %select_multiply_fusion) | copy-start | bytes 3076
  146.3 22.8 %copy-start.27 = (pred[256]{0:T(512)(128)(4,1)S(1)}, pred[256]{0:T(512)(128)(4,1)}, u32[]{:S(2)}) copy-start(pred[256]{0:T(512)(128)(4,1)} %get-tuple-element.63) | copy-start | bytes 772
  146.3 22.8 %copy-start.28 = (pred[256]{0:T(512)(128)(4,1)S(1)}, pred[256]{0:T(512)(128)(4,1)}, u32[]{:S(2)}) copy-start(pred[256]{0:T(512)(128)(4,1)} %get-tuple-element.64) | copy-start | bytes 772
  146.3 22.8 %copy-start.29 = (pred[256]{0:T(512)(128)(4,1)S(1)}, pred[256]{0:T(512)(128)(4,1)}, u32[]{:S(2)}) copy-start(pred[256]{0:T(512)(128)(4,1)} %get-tuple-element.65) | copy-start | bytes 772
  146.3 22.8 %copy-start.30 = (pred[256]{0:T(512)(128)(4,1)S(1)}, pred[256]{0:T(512)(128)(4,1)}, u32[]{:S(2)}) copy-start(pred[256]{0:T(512)(128)(4,1)} %get-tuple-element.66) | copy-start | bytes 772
  146.3 22.8 %copy-start.31 = (pred[256]{0:T(512)(128)(4,1)S(1)}, pred[256]{0:T(512)(128)(4,1)}, u32[]{:S(2)}) copy-start(pred[256]{0:T(512)(128)(4,1)} %get-tuple-element.67) | copy-start | bytes 772
  146.3 22.8 %copy-start.33 = (pred[256]{0:T(512)(128)(4,1)S(1)}, pred[256]{0:T(512)(128)(4,1)}, u32[]{:S(2)}) copy-start(pred[256]{0:T(512)(128)(4,1)} %get-tuple-element.29) | copy-start | bytes 772
  154.1 21.2 %copy-start.34 = (s32[128]{0:T(128)S(1)}, s32[128]{0:T(128)}, u32[]{:S(2)}) copy-start(s32[128]{0:T(128)} %param.12) | copy-start | bytes 1540
  170.8 11.8 %all-to-all-start = ((f32[8,1,3072]{2,1,0:T(1,128)}), f32[8,1,3072]{2,1,0:T(1,128)S(1)}, u32[]{:S(2)}, u32[]{:S(2)}) async-start(f32[8,1,3072]{2,1,0:T(1,128)} %reshape.176), calls=%async_computation | async-start | bytes 196608 | tf_op jit(solution)/shard_map/all_to_all | solution.py:120
where the time goes:
time: 190 us; the launch traced here: 189 us
  local copies, waits for them, and re-layouts  55.5 us (29%)
  blocking collectives  41.9 us (22%)
  other arithmetic  36.8 us (19%)
  starting transfers between devices  34.2 us (18%)
  waiting for transfers between devices  18.6 us (10%)
    psum x1, blocking collectives, per_device(): lax.psum((local_inner(source_term, source_term), local_inner(source_term,...  41.9 us
    ppermute x6, starting transfers between devices, extended(): lax.ppermute(lax.slice_in_dim(block, block.shape[dim] - width, None, axis...  21.9 us
    ppermute x6, waiting for transfers between devices, extended(): lax.ppermute(lax.slice_in_dim(block, 0, width, axis=dim), axis, backward)  10.7 us
    reshape x2, local copies, waits for them, and re-layouts, per_device(): flattened = solution_pad.reshape(sensors, -1)  9.57 us
    gather x3, local copies, waits for them, and re-layouts, gradient(): upper = jnp.take(flattened, centre + stride, axis=1)  8.98 us
    gather x3, local copies, waits for them, and re-layouts, gradient(): lower = jnp.take(flattened, centre - stride, axis=1)  8.97 us
    ppermute x6, starting transfers between devices, extended(): lax.ppermute(lax.slice_in_dim(block, 0, width, axis=dim), axis, backward)  7.75 us
    all_to_all x1, waiting for transfers between devices, per_device(): lax.all_to_all(columns, ('gx', 'gy'), split_axis=2, concat_axis=2, tiled=...  7.24 us
  transfers between devices with their start and end apart: 13, of which 5 were waited for; matrix products, arithmetic and copies ran while one was open for 15% of the time, Pallas kernels for 0%

commit v1 on v0

v1 whole, which is shorter than its diff:
```python
import functools

import jax
import jax.numpy as jnp
from jax import lax
from jax.experimental import pallas as pl
from jax.experimental.pallas import tpu as pltpu
from jax.sharding import PartitionSpec as P

mass_term = 0.25
lane_tile = 128
entry_pairs = ((0, 0), (1, 1), (2, 2), (0, 1), (0, 2), (1, 2))


def ring(count, step):
    return [(i, (i + step) % count) for i in range(count)]


def exchange(faces, axis):
    count = lax.axis_size(axis)
    if count == 1:
        return faces[0], faces[1]
    if count == 2:
        swapped = lax.ppermute(faces[0], axis, ring(2, 1))
        return swapped, swapped
    low, high = faces
    return lax.ppermute(high, axis, ring(count, 1)), lax.ppermute(low, axis, ring(count, -1))


def faces_per_axis(count):
    return 1 if count == 2 else 2


def lanes_equal(shape, value):
    return lax.broadcasted_iota(jnp.int32, shape, len(shape) - 1) == value


def neighbour_flags():
    flags = []
    for axis in ("gx", "gy", "gz"):
        index = lax.axis_index(axis)
        flags.append((index > 0, index < lax.axis_size(axis) - 1))
    return flags


def write_faces(dims, field, face_refs, extra=None):
    sensors, size_x, size_y, size_z = dims
    x_refs, y_refs, z_refs = face_refs

    def put(refs, axis, write):
        if len(refs) == 2:
            write(refs[0], 0)
            write(refs[1], 1)
            return
        index = lax.axis_index(axis)

        @pl.when(index == 0)
        def _():
            write(refs[0], 1)

        @pl.when(index != 0)
        def _():
            write(refs[0], 0)

    def write_x(ref, end):
        x = (size_x - 1) * end
        for y in range(size_y):
            ref[y * sensors : (y + 1) * sensors, :] = field(x * size_y + y)
        if extra is not None:
            ref[size_y * sensors : size_y * (sensors + 1), :] = extra[x]

    def write_y(ref, end):
        y = (size_y - 1) * end
        for x in range(size_x):
            ref[x * sensors : (x + 1) * sensors, :] = field(x * size_y + y)
        if extra is not None:
            for x in range(size_x):
                ref[size_x * sensors + x : size_x * sensors + x + 1, :] = extra[x][y : y + 1, :]

    def write_z(ref, end):
        z = (size_z - 1) * end
        lanes = ref.shape[1]
        packed = jnp.zeros((sensors, lanes), jnp.float32)
        for r in range(size_x * size_y):
            packed = jnp.where(lanes_equal(packed.shape, r), field(r)[:, z : z + 1], packed)
        ref[0:sensors, :] = packed
        if extra is not None:
            packed = jnp.zeros((size_y, lanes), jnp.float32)
            for x in range(size_x):
                packed = jnp.where(lanes_equal(packed.shape, x), extra[x][:, z : z + 1], packed)
            ref[sensors : sensors + size_y, :] = packed

    put(x_refs, "gx", write_x)
    put(y_refs, "gy", write_y)
    put(z_refs, "gz", write_z)


def split_refs(refs, counts):
    groups, start = [], 0
    for count in counts:
        groups.append(refs[start : start + count])
        start += count
    return groups


def pack_kernel(dims, counts, source_ref, label_ref, rows_ref, *face_refs):
    sensors, size_x, size_y, size_z = dims
    count = size_x * size_y
    for r in range(count):
        rows_ref[r * sensors : (r + 1) * sensors, :] = source_ref[pl.ds(r, sensors, stride=count), :]
    shifted = [(label_ref[x] + 1).astype(jnp.float32) for x in range(size_x)]
    field = lambda r: rows_ref[r * sensors : (r + 1) * sensors, :]
    write_faces(dims, field, split_refs(face_refs, counts), shifted)


def tissue(shifted, table_ref):
    conductivity = jnp.zeros_like(shifted)
    for level in range(table_ref.shape[0]):
        conductivity = jnp.where(shifted == level + 1, table_ref[level], conductivity)
    return conductivity, (shifted > 0).astype(jnp.float32)


def edge_weight(first, second):
    return 0.5 * (first[0] + second[0]) * first[1] * second[1]


def weights(dims, label_ref, table_ref, halo_refs, weight_ref):
    sensors, size_x, size_y, size_z = dims
    flags = neighbour_flags()
    (x_low, x_high), (y_low, y_high), (z_low, z_high) = halo_refs

    def masked(value, flag):
        return jnp.where(flag, value, 0.0)

    own = [(label_ref[x] + 1).astype(jnp.float32) for x in range(size_x)]
    own_tissue = [tissue(plane, table_ref) for plane in own]
    x_rows = slice(size_y * sensors, size_y * (sensors + 1))
    below = tissue(masked(x_low[x_rows, :], flags[0][0]), table_ref)
    above = tissue(masked(x_high[x_rows, :], flags[0][1]), table_ref)
    planes = [below] + own_tissue + [above]
    across_x = [edge_weight(planes[i], planes[i + 1]) for i in range(size_x + 1)]
    row_index = lax.broadcasted_iota(jnp.int32, (size_y, size_z), 0)
    lane_index = lax.broadcasted_iota(jnp.int32, (size_y, size_z), 1)
    for x in range(size_x):
        y_row = size_x * sensors + x
        shifted = own[x]
        y_before = jnp.where(
            row_index == 0,
            masked(y_low[y_row : y_row + 1, :], flags[1][0]),
            pltpu.roll(shifted, 1, 0),
        )
        y_after = jnp.where(
            row_index == size_y - 1,
            masked(y_high[y_row : y_row + 1, :], flags[1][1]),
            pltpu.roll(shifted, size_y - 1, 0),
        )
        z_rows = slice(sensors, sensors + size_y)
        z_before = jnp.where(
            lane_index == 0,
            masked(z_low[z_rows, x : x + 1], flags[2][0]),
            pltpu.roll(shifted, 1, 1),
        )
        z_after = jnp.where(
            lane_index == size_z - 1,
            masked(z_high[z_rows, x : x + 1], flags[2][1]),
            pltpu.roll(shifted, size_z - 1, 1),
        )
        six = [across_x[x], across_x[x + 1]]
        for beside in (y_before, y_after, z_before, z_after):
            six.append(edge_weight(own_tissue[x], tissue(beside, table_ref)))
        for k, weight in enumerate(six):
            weight_ref[k, x] = weight
        weight_ref[6, x] = mass_term + (six[0] + six[1]) + (six[2] + six[3]) + (six[4] + six[5])
        weight_ref[7, x] = 0.5 * own_tissue[x][0]


def around(dims, rows_ref, halo_refs, r, flags=None):
    sensors, size_x, size_y, size_z = dims
    (x_low, x_high), (y_low, y_high), (z_low, z_high) = halo_refs
    x, y = divmod(r, size_y)

    def keep(value, dim, end):
        return value if flags is None else jnp.where(flags[dim][end], value, 0.0)

    def row(index):
        return rows_ref[index * sensors : (index + 1) * sensors, :]

    def part(ref, index):
        return ref[index * sensors : (index + 1) * sensors, :]

    centre = row(r)
    x_before = row(r - size_y) if x > 0 else keep(part(x_low, y), 0, 0)
    x_after = row(r + size_y) if x < size_x - 1 else keep(part(x_high, y), 0, 1)
    y_before = row(r - 1) if y > 0 else keep(part(y_low, x), 1, 0)
    y_after = row(r + 1) if y < size_y - 1 else keep(part(y_high, x), 1, 1)
    lane_index = lax.broadcasted_iota(jnp.int32, centre.shape, 1)
    z_before = jnp.where(
        lane_index == 0, keep(z_low[0:sensors, r : r + 1], 2, 0), pltpu.roll(centre, 1, 1)
    )
    z_after = jnp.where(
        lane_index == size_z - 1,
        keep(z_high[0:sensors, r : r + 1], 2, 1),
        pltpu.roll(centre, size_z - 1, 1),
    )
    return centre, (x_before, x_after, y_before, y_after, z_before, z_after)


def combine(weight_ref, x, y, centre, beside):
    total = weight_ref[6, x, y : y + 1, :] * centre
    for k, value in enumerate(beside):
        total = total - weight_ref[k, x, y : y + 1, :] * value
    return total


def pair_up(refs):
    return [(refs[2 * i], refs[2 * i + 1]) for i in range(3)]


def apply_kernel(dims, counts, rows_ref, label_ref, table_ref, *refs):
    sensors, size_x, size_y, size_z = dims
    halo_refs = pair_up(refs[:6])
    weight_ref, applied_ref = refs[6:8]
    face_refs = refs[8:]
    weights(dims, label_ref, table_ref, halo_refs, weight_ref)
    for r in range(size_x * size_y):
        x, y = divmod(r, size_y)
        centre, beside = around(dims, rows_ref, halo_refs, r)
        applied_ref[r * sensors : (r + 1) * sensors, :] = combine(weight_ref, x, y, centre, beside)
    field = lambda r: applied_ref[r * sensors : (r + 1) * sensors, :]
    write_faces(dims, field, split_refs(face_refs, counts))


def halves(value):
    high = value.astype(jnp.bfloat16)
    return high, (value - high.astype(jnp.float32)).astype(jnp.bfloat16)


def select_kernel(dims, rows_ref, applied_ref, weight_ref, voxel_ref, *refs):
    sensors, size_x, size_y, size_z = dims
    source_halos = pair_up(refs[:6])
    applied_halos = pair_up(refs[6:12])
    column_ref, moment_ref, chosen_ref, high_ref, low_ref = refs[12:]
    flags = neighbour_flags()
    slots = voxel_ref.shape[0]
    sums = [jnp.zeros((sensors, size_z), jnp.float32) for _ in range(4)]
    lane_index = lax.broadcasted_iota(jnp.int32, (slots, size_z), 1)
    voxel = voxel_ref[...]
    for r in range(size_x * size_y):
        x, y = divmod(r, size_y)
        span = slice(r * size_z, (r + 1) * size_z)
        chosen_ref[:, span] = (lane_index == voxel - r * size_z).astype(jnp.float32).astype(jnp.bfloat16)
        scale = weight_ref[7, x, y : y + 1, :]
        source, source_beside = around(dims, rows_ref, source_halos, r, flags)
        applied, applied_beside = around(dims, applied_ref, applied_halos, r, flags)
        twice = combine(weight_ref, x, y, applied, applied_beside)
        for k, product in enumerate(
            (source * source, source * applied, applied * applied, applied * twice)
        ):
            sums[k] = sums[k] + product
        for part, beside in enumerate((source_beside, applied_beside)):
            for c in range(3):
                high, low = halves(scale * (beside[2 * c + 1] - beside[2 * c]))
                first = (part * 3 + c) * sensors
                high_ref[first : first + sensors, span] = high
                low_ref[first : first + sensors, span] = low
    contract = (((1,), (1,)), ((), ()))
    chosen = chosen_ref[...]
    column_ref[...] = lax.dot_general(
        chosen, high_ref[...], contract, preferred_element_type=jnp.float32
    ) + lax.dot_general(chosen, low_ref[...], contract, preferred_element_type=jnp.float32)
    stacked = jnp.concatenate(sums, axis=0)
    moment_ref[...] = lax.dot_general(
        jnp.ones((8, size_z), jnp.float32),
        stacked,
        contract,
        precision=lax.Precision.HIGHEST,
        preferred_element_type=jnp.float32,
    )


def owner_kernel(sensors, slots_each, received_ref, owned_ref, data_ref, projection_ref, gram_ref):
    total, width = received_ref.shape
    base = 6 * sensors
    extra = width - base
    moment_rows = -(-4 * sensors // extra)
    gathered = jnp.zeros((moment_rows, extra), jnp.float32)
    for source in range(total // slots_each):
        first = source * slots_each
        gathered = gathered + received_ref[first : first + moment_rows, base:width]
    moments = []
    sensor_index = lax.broadcasted_iota(jnp.int32, (sensors, extra), 0)
    lane_index = lax.broadcasted_iota(jnp.int32, (sensors, extra), 1)
    for k in range(4):
        row, offset = divmod(k * sensors, extra)
        picked = jnp.where(lane_index == sensor_index + offset, gathered[row : row + 1, :], 0.0)
        moments.append(jnp.sum(picked, axis=1, keepdims=True))
    moment_zero, moment_one, moment_two, moment_three = moments
    first_step = moment_zero / moment_one
    residue = first_step * first_step * moment_two - moment_zero
    growth = 1.0 + residue / moment_zero
    curvature = (
        growth * growth * moment_one
        - 2.0 * growth * first_step * moment_two
        + first_step * first_step * moment_three
    )
    second_step = residue / curvature
    source_coef = first_step + second_step * growth
    applied_coef = second_step * first_step
    positions = owned_ref.shape[1]
    slot_index = lax.broadcasted_iota(jnp.int32, (total, positions), 0)
    chosen = (slot_index == owned_ref[...]).astype(jnp.float32).astype(jnp.bfloat16)
    high, low = halves(received_ref[:, 0:base])
    contract = (((0,), (0,)), ((), ()))
    owned = lax.dot_general(
        high, chosen, contract, preferred_element_type=jnp.float32
    ) + lax.dot_general(low, chosen, contract, preferred_element_type=jnp.float32)
    lead = []
    for c in range(3):
        source_part = owned[c * sensors : (c + 1) * sensors, :]
        applied_part = owned[(3 + c) * sensors : (4 + c) * sensors, :]
        lead.append(source_coef * source_part - applied_coef * applied_part)
        projection_ref[c] = lax.dot_general(
            data_ref[...],
            lead[c],
            contract,
            precision=lax.Precision.HIGHEST,
            preferred_element_type=jnp.float32,
        )
    for k, (first, second) in enumerate(entry_pairs):
        gram_ref[k : k + 1, :] = jnp.sum(lead[first] * lead[second], axis=0, keepdims=True)


def in_vmem(count):
    return [pl.BlockSpec(memory_space=pltpu.VMEM)] * count


def face_shapes(dims, counts, with_labels):
    sensors, size_x, size_y, size_z = dims
    lanes = -(-size_x * size_y // lane_tile) * lane_tile
    shapes = (
        (size_y * (sensors + with_labels), size_z),
        (size_x * sensors + 8 * with_labels * -(-size_x // 8), size_z),
        (sensors + size_y * with_labels, lanes),
    )
    return [
        jax.ShapeDtypeStruct(shape, jnp.float32)
        for shape, count in zip(shapes, counts)
        for _ in range(count)
    ]


def exchange_all(faces, counts):
    halos = []
    for axis, group in zip(("gx", "gy", "gz"), split_refs(faces, counts)):
        halos.extend(exchange(group, axis))
    return halos


def per_device(source_term, labels, conductivity_table, send_map, owner_slots, sensor_data):
    dims = source_term.shape
    sensors, size_x, size_y, size_z = dims
    rows_count = size_x * size_y
    counts = [faces_per_axis(lax.axis_size(axis)) for axis in ("gx", "gy", "gz")]
    owners = lax.axis_size("gx") * lax.axis_size("gy")
    slots = send_map.size
    slots_each = slots // owners
    times = sensor_data.shape[1]
    positions = owner_slots.shape[0]

    field_shape = jax.ShapeDtypeStruct((rows_count * sensors, size_z), jnp.float32)
    packed = pl.pallas_call(
        functools.partial(pack_kernel, dims, counts),
        out_shape=[field_shape] + face_shapes(dims, counts, 1),
        in_specs=in_vmem(2),
        out_specs=in_vmem(1 + sum(counts)),
        name="pack",
    )(source_term.reshape(sensors * rows_count, size_z), labels)
    rows, faces = packed[0], packed[1:]
    source_halos = exchange_all(faces, counts)

    weight_shape = jax.ShapeDtypeStruct((8, size_x, size_y, size_z), jnp.float32)
    result = pl.pallas_call(
        functools.partial(apply_kernel, dims, counts),
        out_shape=[weight_shape, field_shape] + face_shapes(dims, counts, 0),
        in_specs=in_vmem(2) + [pl.BlockSpec(memory_space=pltpu.SMEM)] + in_vmem(6),
        out_specs=in_vmem(2 + sum(counts)),
        name="apply",
    )(rows, labels, conductivity_table, *source_halos)
    weight, applied, faces = result[0], result[1], result[2:]
    applied_halos = exchange_all(faces, counts)

    base = 6 * sensors
    columns, moment = pl.pallas_call(
        functools.partial(select_kernel, dims),
        out_shape=[
            jax.ShapeDtypeStruct((slots, base), jnp.float32),
            jax.ShapeDtypeStruct((8, 4 * sensors), jnp.float32),
        ],
        in_specs=in_vmem(16),
        out_specs=in_vmem(2),
        scratch_shapes=[
            pltpu.VMEM((slots, rows_count * size_z), jnp.bfloat16),
            pltpu.VMEM((base, rows_count * size_z), jnp.bfloat16),
            pltpu.VMEM((base, rows_count * size_z), jnp.bfloat16),
        ],
        name="choose",
    )(rows, applied, weight, send_map.reshape(slots, 1), *source_halos, *applied_halos)

    depth = lax.axis_size("gz")
    moment = moment + sum(lax.ppermute(moment, "gz", ring(depth, d)) for d in range(1, depth))
    extra = -base % lane_tile
    while slots_each * extra < 4 * sensors:
        extra += lane_tile
    spread = jnp.pad(moment[0], (0, slots_each * extra - 4 * sensors)).reshape(1, slots_each, extra)
    spread = jnp.broadcast_to(spread, (owners, slots_each, extra)).reshape(slots, extra)
    outgoing = jnp.concatenate([columns, spread], axis=1)
    received = lax.all_to_all(
        outgoing.reshape(owners, slots_each, base + extra), ("gx", "gy"), 0, 0, tiled=True
    ).reshape(slots, base + extra)
    return pl.pallas_call(
        functools.partial(owner_kernel, sensors, slots_each),
        out_shape=[
            jax.ShapeDtypeStruct((3, times, positions), jnp.float32),
            jax.ShapeDtypeStruct((6, positions), jnp.float32),
        ],
        in_specs=in_vmem(3),
        out_specs=in_vmem(2),
        name="owner",
    )(received, owner_slots.reshape(1, positions), sensor_data)


def solution(mesh):
    in_specs = (
        P(None, "gx", "gy", "gz"),
        P("gx", "gy", "gz"),
        P(),
        P("gx", "gy", "gz", None),
        P(("gx", "gy", "gz")),
        P(),
    )
    out_specs = (P(None, None, ("gx", "gy", "gz")), P(None, ("gx", "gy", "gz")))
    step = jax.shard_map(
        per_device, mesh=mesh, in_specs=in_specs, out_specs=out_specs, check_vma=False
    )
    return lambda *arguments: tuple(step(*arguments))
```

time: 190 us -> 54.5 us (0.29)
  local copies, waits for them, and re-layouts: 55.5 us -> 2.23 us
  other arithmetic: 36.8 us -> 1.75 us
  blocking collectives: 41.9 us -> 12.7 us
  starting transfers between devices: 34.2 us -> 17.9 us
  Pallas kernels: 0 us -> 13.2 us
  waiting for transfers between devices: 18.6 us -> 5.8 us
    psum x1 -> x0, blocking collectives: 41.9 us -> none  [per_device(): lax.psum((local_inner(source_term, source_term), local_inner(source_term,...]
    gather x8 -> x0, local copies, waits for them, and re-layouts: 20.5 us -> none  [the longest x3 8.98 us: gradient(): upper = jnp.take(flattened, centre + stride, axis=1)]
    pallas_call x0 -> x4, Pallas kernels: none -> 13.2 us  [the longest x1 5.63 us: per_device(): pl.pallas_call(functools.partial(select_kernel, dims), out_shape=[jax.Sha...]
    all_to_all x0 -> x1, blocking collectives: none -> 12.7 us  [per_device(): lax.all_to_all(outgoing.reshape(owners, slots_each, base + extra), ('gx',...]
    ppermute x12 -> x13, starting transfers between devices: 29.7 us -> 17.9 us  [the longest x4 7.9 us: exchange(): lax.ppermute(low, axis, ring(count, -1))]
    add x5 -> x1, other arithmetic: 11.8 us -> 0.69 us  [per_device(): moment + sum((lax.ppermute(moment, 'gz', ring(depth, d)) for d in range(1...]
    reshape x2 -> x1, local copies, waits for them, and re-layouts: 9.57 us -> 0.8 us  [per_device(): send_map.reshape(slots, 1)]
    slice x7 -> x0, local copies, waits for them, and re-layouts: 7.5 us -> none  [the longest x5 5.13 us: extended(): lax.slice_in_dim(block, block.shape[dim] - width, None, axis=dim)]
  transfers between devices with their start and end apart: 13 -> 13, of which waited for: 5 -> 4; matrix products, arithmetic and copies ran while one was open for 15% -> 1% of each run, Pallas kernels for 0% -> 0%
where the time goes in v1:
time: 54.5 us; the launch traced here: 54.2 us
  starting transfers between devices  17.9 us (33%)
  Pallas kernels  13.2 us (24%)
  blocking collectives  12.7 us (23%)
  waiting for transfers between devices  5.8 us (11%)
  local copies, waits for them, and re-layouts  2.23 us (4%)
  other arithmetic  1.75 us (3%)
  between operations  0.71 us (1%)
    all_to_all x1, blocking collectives, per_device(): lax.all_to_all(outgoing.reshape(owners, slots_each, base + extra), ('gx',...  12.7 us
    ppermute x4, starting transfers between devices, exchange(): lax.ppermute(low, axis, ring(count, -1))  7.9 us
    pallas_call x1, Pallas kernels, per_device(): pl.pallas_call(functools.partial(select_kernel, dims), out_shape=[jax.Sha...  5.63 us
    ppermute x3, starting transfers between devices, per_device(): lax.ppermute(moment, 'gz', ring(depth, d))  3.43 us
    ppermute x2, starting transfers between devices, exchange(): swapped = lax.ppermute(faces[0], axis, ring(2, 1))  3.28 us
    ppermute x3, waiting for transfers between devices, per_device(): lax.ppermute(moment, 'gz', ring(depth, d))  3.24 us
    ppermute x4, starting transfers between devices, exchange(): lax.ppermute(high, axis, ring(count, 1))  3.24 us
    pallas_call x1, Pallas kernels, per_device(): pl.pallas_call(functools.partial(apply_kernel, dims, counts), out_shape=[...  2.96 us
  transfers between devices with their start and end apart: 13, of which 4 were waited for; matrix products, arithmetic and copies ran while one was open for 1% of the time, Pallas kernels for 0%

profile of v1, /device:TPU:0, one launch (start us, length us, event | category | flops | bytes accessed | tf_op | source)
XLA Modules:
  0.0 54.2 jit_solution(2890562394725452315)
XLA Ops:
  0.6 2.3 %pack.1 = (f32[1024,128]{1,0:T(8,128)}, f32[264,128]{1,0:T(8,128)}, f32[136,128]{1,0:T(8,128)}, f32[136,128]{1,0:T(8,128)}, f32[40,128]{1,0:T(8,128)}, /*index=5*/f32[40,128]{1,0:T(8,128)}) custom-call(f32[1024,128]{1,0:T(8,128)} %bitcast.8, s32[4,8,128]{2,1,0:T(8,128)} %label_ref.3), custom_call_target="tpu_custom_call" | custom-call | tf_op jit(solution)/shard_map/pack/pallas_call | solution.py:371
  2.9 3.0 %collective-permute-start = (f32[264,128]{1,0:T(8,128)}, f32[264,128]{1,0:T(8,128)S(1)}, u32[]{:S(2)}, u32[]{:S(2)}) collective-permute-start(f32[264,128]{1,0:T(8,128)} %get-tuple-element.18), channel_id=1, source_target_pairs={{0,16},{16,0},{1,17},{17,1},{2,18},{18,2},{3,19},{19,3},{4,20},{20... | collective-permute-start | bytes 405512 | tf_op jit(solution)/shard_map/ppermute | solution.py:24
  5.9 1.6 %collective-permute-start.1 = (f32[136,128]{1,0:T(8,128)}, f32[136,128]{1,0:T(8,128)S(1)}, u32[]{:S(2)}, u32[]{:S(2)}) collective-permute-start(f32[136,128]{1,0:T(8,128)} %get-tuple-element.19), channel_id=1, source_target_pairs={{0,4},{4,8},{8,12},{12,0},{1,5},{5,9},{9,13},{13,1},{2,6},{6,10},{... | collective-permute-start | bytes 208904 | tf_op jit(solution)/shard_map/ppermute | solution.py:27
  7.5 2.2 %collective-permute-start.2 = (f32[136,128]{1,0:T(8,128)}, f32[136,128]{1,0:T(8,128)S(1)}, u32[]{:S(2)}, u32[]{:S(2)}) collective-permute-start(f32[136,128]{1,0:T(8,128)} %get-tuple-element.20), channel_id=1, source_target_pairs={{0,12},{4,0},{8,4},{12,8},{1,13},{5,1},{9,5},{13,9},{2,14},{6,2},{... | collective-permute-start | bytes 208904 | tf_op jit(solution)/shard_map/ppermute | solution.py:27
  9.8 0.0 collective-permute-start.3
  9.8 1.7 %collective-permute-start.4 = (f32[40,128]{1,0:T(8,128)}, f32[40,128]{1,0:T(8,128)S(1)}, u32[]{:S(2)}, u32[]{:S(2)}) collective-permute-start(f32[40,128]{1,0:T(8,128)} %get-tuple-element.22), channel_id=1, source_target_pairs={{0,3},{1,0},{2,1},{3,2},{4,7},{5,4},{6,5},{7,6},{8,11},{9,8},{10,9... | collective-permute-start | bytes 61448 | tf_op jit(solution)/shard_map/ppermute | solution.py:27
  11.5 1.7 %collective-permute-done.3.refs_4_ = f32[40,128]{1,0:T(8,128)S(1)} collective-permute-done((f32[40,128]{1,0:T(8,128)}, f32[40,128]{1,0:T(8,128)S(1)}, u32[]{:S(2)}, u32[]{:S(2)}) %collective-permute-start.3) | collective-permute-done | bytes 20512 | tf_op jit(solution)/shard_map/ppermute | solution.py:27
  13.2 0.0 copy-start.4
  13.2 0.0 collective-permute-done.4.refs_5_
  13.2 0.0 copy-start.5
  13.2 0.0 collective-permute-done.1.refs_2_
  13.2 0.0 copy-start.2
  13.2 0.0 collective-permute-done.2.refs_3_
  13.2 0.0 copy-start.3
  13.2 0.0 collective-permute-done.refs_0_.refs_1_
  13.2 0.0 copy-start
  13.3 0.5 copy-done.4
  13.8 0.0 copy-done.5
  13.8 0.0 copy-done.2
  13.8 0.0 copy-done.3
  13.9 0.0 copy-done
  13.9 3.0 %apply.1 = (f32[8,4,8,128]{3,2,1,0:T(8,128)}, f32[1024,128]{1,0:T(8,128)}, f32[256,128]{1,0:T(8,128)}, f32[128,128]{1,0:T(8,128)}, f32[128,128]{1,0:T(8,128)}, /*index=5*/f32[32,128]{1,0:T(8,128)}, f32[32,128]{1,0:T(8,128)}) custom-call(f32[1024,128]{1,0:T(8,128)} %get-tuple-element.17.rows_ref, s32[4,8,128]{2,1,0:T(8,128)} %label_ref.3, f32[6]{0:T(128)} %table_ref.1, ...), custom_call_target="tpu_custom_call" | custom-call | tf_op jit(solution)/shard_map/apply/pallas_call | solution.py:382
  16.9 0.3 collective-permute-start.5
  17.2 0.7 %collective-permute-start.6 = (f32[128,128]{1,0:T(8,128)}, f32[128,128]{1,0:T(8,128)S(1)}, u32[]{:S(2)}, u32[]{:S(2)}) collective-permute-start(f32[128,128]{1,0:T(8,128)} %get-tuple-element.26), channel_id=1, source_target_pairs={{0,4},{4,8},{8,12},{12,0},{1,5},{5,9},{9,13},{13,1},{2,6},{6,10},{... | collective-permute-start | bytes 196616 | tf_op jit(solution)/shard_map/ppermute | solution.py:27
  17.8 3.1 %collective-permute-start.7 = (f32[128,128]{1,0:T(8,128)}, f32[128,128]{1,0:T(8,128)S(1)}, u32[]{:S(2)}, u32[]{:S(2)}) collective-permute-start(f32[128,128]{1,0:T(8,128)} %get-tuple-element.27), channel_id=1, source_target_pairs={{0,12},{4,0},{8,4},{12,8},{1,13},{5,1},{9,5},{13,9},{2,14},{6,2},{... | collective-permute-start | bytes 196616 | tf_op jit(solution)/shard_map/ppermute | solution.py:27
  21.0 1.0 %collective-permute-start.8 = (f32[32,128]{1,0:T(8,128)}, f32[32,128]{1,0:T(8,128)S(1)}, u32[]{:S(2)}, u32[]{:S(2)}) collective-permute-start(f32[32,128]{1,0:T(8,128)} %get-tuple-element.28), channel_id=1, source_target_pairs={{0,1},{1,2},{2,3},{3,0},{4,5},{5,6},{6,7},{7,4},{8,9},{9,10},{10,1... | collective-permute-start | bytes 49160 | tf_op jit(solution)/shard_map/ppermute | solution.py:27
  21.9 0.0 copy-start.10
  21.9 0.8 %collective-permute-start.9 = (f32[32,128]{1,0:T(8,128)}, f32[32,128]{1,0:T(8,128)S(1)}, u32[]{:S(2)}, u32[]{:S(2)}) collective-permute-start(f32[32,128]{1,0:T(8,128)} %get-tuple-element.29), channel_id=1, source_target_pairs={{0,3},{1,0},{2,1},{3,2},{4,7},{5,4},{6,5},{7,6},{8,11},{9,8},{10,9... | collective-permute-start | bytes 49160 | tf_op jit(solution)/shard_map/ppermute | solution.py:27
  22.7 0.0 copy-done.10
  22.7 0.8 %copy.8.voxel_ref = s32[256,1]{1,0:T(8,128)} copy(s32[256,1]{0,1:T(1,128)S(1)} %bitcast.10) | data formatting | bytes 2048 | tf_op jit(solution)/shard_map/reshape | solution.py:407
  23.5 0.8 %collective-permute-done.8.refs_10_ = f32[32,128]{1,0:T(8,128)S(1)} collective-permute-done((f32[32,128]{1,0:T(8,128)}, f32[32,128]{1,0:T(8,128)S(1)}, u32[]{:S(2)}, u32[]{:S(2)}) %collective-permute-start.8) | collective-permute-done | bytes 16416 | tf_op jit(solution)/shard_map/ppermute | solution.py:27
  24.4 0.0 copy-start.8
  24.4 0.0 collective-permute-done.9.refs_11_
  24.4 0.0 copy-start.9
  24.4 0.0 collective-permute-done.6.refs_8_
  24.4 0.0 copy-start.6
  24.4 0.0 collective-permute-done.7.refs_9_
  24.4 0.0 copy-start.7
  24.4 0.0 collective-permute-done.5.refs_6_.refs_7_
  24.4 0.0 copy-start.1
  24.4 0.5 copy-done.8
  25.0 0.0 copy-done.9
  25.0 0.0 copy-done.6
  25.0 0.0 copy-done.7
  25.0 0.0 copy-done.1
  25.1 5.6 %choose.1 = (f32[256,192]{1,0:T(8,128)}, f32[8,128]{1,0:T(8,128)}) custom-call(f32[1024,128]{1,0:T(8,128)} %get-tuple-element.17.rows_ref, f32[1024,128]{1,0:T(8,128)} %get-tuple-element.23.applied_ref, f32[8,4,8,128]{3,2,1,0:T(8,128)} %get-tuple-element.24.weight_ref, s32[256,1]{1,0:T(8,128)} %copy.8.voxel_ref, f32[264,128]{1,0:T(8,128)} %copy-done, ...), custom_call_target="tpu_custom_call" | custom-call | tf_op jit(solution)/shard_map/choose/pallas_call | solution.py:393
  30.7 1.7 %collective-permute-start.12 = (f32[8,128]{1,0:T(8,128)}, f32[8,128]{1,0:T(8,128)S(1)}, u32[]{:S(2)}, u32[]{:S(2)}) collective-permute-start(f32[8,128]{1,0:T(8,128)} %get-tuple-element.31), channel_id=1, source_target_pairs={{0,3},{1,0},{2,1},{3,2},{4,7},{5,4},{6,5},{7,6},{8,11},{9,8},{10,9... | collective-permute-start | bytes 12296 | tf_op jit(solution)/shard_map/ppermute | solution.py:410
  32.4 1.7 %collective-permute-start.11 = (f32[8,128]{1,0:T(8,128)}, f32[8,128]{1,0:T(8,128)S(1)}, u32[]{:S(2)}, u32[]{:S(2)}) collective-permute-start(f32[8,128]{1,0:T(8,128)} %get-tuple-element.31), channel_id=1, source_target_pairs={{0,2},{1,3},{2,0},{3,1},{4,6},{5,7},{6,4},{7,5},{8,10},{9,11},{10,... | collective-permute-start | bytes 12296 | tf_op jit(solution)/shard_map/ppermute | solution.py:410
  34.1 0.0 collective-permute-start.10
  34.2 0.0 collective-permute-done.12
  34.2 2.1 %collective-permute-done.11 = f32[8,128]{1,0:T(8,128)S(1)} collective-permute-done((f32[8,128]{1,0:T(8,128)}, f32[8,128]{1,0:T(8,128)S(1)}, u32[]{:S(2)}, u32[]{:S(2)}) %collective-permute-start.11) | collective-permute-done | bytes 4128 | tf_op jit(solution)/shard_map/ppermute | solution.py:410
  36.3 1.1 %collective-permute-done.10 = f32[8,128]{1,0:T(8,128)S(1)} collective-permute-done((f32[8,128]{1,0:T(8,128)}, f32[8,128]{1,0:T(8,128)S(1)}, u32[]{:S(2)}, u32[]{:S(2)}) %collective-permute-start.10) | collective-permute-done | bytes 4128 | tf_op jit(solution)/shard_map/ppermute | solution.py:410
  37.4 0.7 %add_add_fusion = f32[8,128]{1,0:T(8,128)S(1)} fusion(f32[8,128]{1,0:T(8,128)} %get-tuple-element.31, f32[8,128]{1,0:T(8,128)S(1)} %collective-permute-done.12, f32[8,128]{1,0:T(8,128)S(1)} %collective-permute-done.10, f32[8,128]{1,0:T(8,128)S(1)} %collective-permute-done.11), kind=kLoop, calls=%fused_computation.1 | loop fusion | flops 3072 | bytes 20480 | tf_op jit(solution)/shard_map/add | solution.py:410
  38.1 0.1 broadcast_in_dim.7
  38.2 1.1 %pad_maximum_fusion = f32[8,32,256]{2,1,0:T(8,128)S(1)} fusion(f32[8,32,64]{2,1,0:T(8,128)S(1)} %broadcast_in_dim.8, f32[8,32,192]{2,1,0:T(8,128)} %bitcast.9), kind=kLoop, calls=%fused_computation | loop fusion | flops 65536 | bytes 524288 | tf_op jit(solution)/shard_map/concatenate | solution.py:416
  39.2 12.7 %all_to_all.5 = f32[8,32,256]{2,1,0:T(8,128)} all-to-all(f32[8,32,256]{2,1,0:T(8,128)S(1)} %pad_maximum_fusion), channel_id=1, replica_groups=mesh['gx'=2,'gy'=4,'gz'=4] {'gx','gy'}, dimensions={0} | all-to-all | bytes 524288 | tf_op jit(solution)/shard_map/all_to_all | solution.py:417
  52.0 2.2 %owner.1 = (f32[3,128,128]{2,1,0:T(8,128)}, f32[6,128]{1,0:T(8,128)}) custom-call(f32[256,256]{1,0:T(8,128)} %bitcast.7, s32[1,128]{1,0:T(1,128)} %bitcast.11, f32[32,128]{1,0:T(8,128)} %data_ref.1), custom_call_target="tpu_custom_call" | custom-call | tf_op jit(solution)/shard_map/owner/pallas_call | solution.py:420
  (3 shorter events, 0.0 us)
Async XLA Ops:
  2.9 10.3 %collective-permute-start = (f32[264,128]{1,0:T(8,128)}, f32[264,128]{1,0:T(8,128)S(1)}, u32[]{:S(2)}, u32[]{:S(2)}) collective-permute-start(f32[264,128]{1,0:T(8,128)} %get-tuple-element.18), channel_id=1, source_target_pairs={{0,16},{16,0},{1,17},{17,1},{2,18},{18,2},{3,19},{19,3},{4,20},{20... | collective-permute-start | bytes 405512 | tf_op jit(solution)/shard_map/ppermute | solution.py:24
  5.9 7.3 %collective-permute-start.1 = (f32[136,128]{1,0:T(8,128)}, f32[136,128]{1,0:T(8,128)S(1)}, u32[]{:S(2)}, u32[]{:S(2)}) collective-permute-start(f32[136,128]{1,0:T(8,128)} %get-tuple-element.19), channel_id=1, source_target_pairs={{0,4},{4,8},{8,12},{12,0},{1,5},{5,9},{9,13},{13,1},{2,6},{6,10},{... | collective-permute-start | bytes 208904 | tf_op jit(solution)/shard_map/ppermute | solution.py:27
  7.5 5.7 %collective-permute-start.2 = (f32[136,128]{1,0:T(8,128)}, f32[136,128]{1,0:T(8,128)S(1)}, u32[]{:S(2)}, u32[]{:S(2)}) collective-permute-start(f32[136,128]{1,0:T(8,128)} %get-tuple-element.20), channel_id=1, source_target_pairs={{0,12},{4,0},{8,4},{12,8},{1,13},{5,1},{9,5},{13,9},{2,14},{6,2},{... | collective-permute-start | bytes 208904 | tf_op jit(solution)/shard_map/ppermute | solution.py:27
  9.8 3.4 %collective-permute-start.3 = (f32[40,128]{1,0:T(8,128)}, f32[40,128]{1,0:T(8,128)S(1)}, u32[]{:S(2)}, u32[]{:S(2)}) collective-permute-start(f32[40,128]{1,0:T(8,128)} %get-tuple-element.21), channel_id=1, source_target_pairs={{0,1},{1,2},{2,3},{3,0},{4,5},{5,6},{6,7},{7,4},{8,9},{9,10},{10,1... | collective-permute-start | bytes 61448 | tf_op jit(solution)/shard_map/ppermute | solution.py:27
  9.8 3.4 %collective-permute-start.4 = (f32[40,128]{1,0:T(8,128)}, f32[40,128]{1,0:T(8,128)S(1)}, u32[]{:S(2)}, u32[]{:S(2)}) collective-permute-start(f32[40,128]{1,0:T(8,128)} %get-tuple-element.22), channel_id=1, source_target_pairs={{0,3},{1,0},{2,1},{3,2},{4,7},{5,4},{6,5},{7,6},{8,11},{9,8},{10,9... | collective-permute-start | bytes 61448 | tf_op jit(solution)/shard_map/ppermute | solution.py:27
  13.2 0.6 %copy-start.4 = (f32[40,128]{1,0:T(8,128)}, f32[40,128]{1,0:T(8,128)S(1)}, u32[]{:S(2)}) copy-start(f32[40,128]{1,0:T(8,128)S(1)} %collective-permute-done.3.refs_4_) | copy-start | bytes 61444
  13.2 0.6 %copy-start.5 = (f32[40,128]{1,0:T(8,128)}, f32[40,128]{1,0:T(8,128)S(1)}, u32[]{:S(2)}) copy-start(f32[40,128]{1,0:T(8,128)S(1)} %collective-permute-done.4.refs_5_) | copy-start | bytes 61444
  13.2 0.6 %copy-start.2 = (f32[136,128]{1,0:T(8,128)}, f32[136,128]{1,0:T(8,128)S(1)}, u32[]{:S(2)}) copy-start(f32[136,128]{1,0:T(8,128)S(1)} %collective-permute-done.1.refs_2_) | copy-start | bytes 208900
  13.2 0.7 %copy-start.3 = (f32[136,128]{1,0:T(8,128)}, f32[136,128]{1,0:T(8,128)S(1)}, u32[]{:S(2)}) copy-start(f32[136,128]{1,0:T(8,128)S(1)} %collective-permute-done.2.refs_3_) | copy-start | bytes 208900
  13.2 0.7 %copy-start = (f32[264,128]{1,0:T(8,128)}, f32[264,128]{1,0:T(8,128)S(1)}, u32[]{:S(2)}) copy-start(f32[264,128]{1,0:T(8,128)S(1)} %collective-permute-done.refs_0_.refs_1_) | copy-start | bytes 405508
  16.9 7.5 %collective-permute-start.5 = (f32[256,128]{1,0:T(8,128)}, f32[256,128]{1,0:T(8,128)S(1)}, u32[]{:S(2)}, u32[]{:S(2)}) collective-permute-start(f32[256,128]{1,0:T(8,128)} %get-tuple-element.25), channel_id=1, source_target_pairs={{0,16},{16,0},{1,17},{17,1},{2,18},{18,2},{3,19},{19,3},{4,20},{20... | collective-permute-start | bytes 393224 | tf_op jit(solution)/shard_map/ppermute | solution.py:24
  17.2 7.2 %collective-permute-start.6 = (f32[128,128]{1,0:T(8,128)}, f32[128,128]{1,0:T(8,128)S(1)}, u32[]{:S(2)}, u32[]{:S(2)}) collective-permute-start(f32[128,128]{1,0:T(8,128)} %get-tuple-element.26), channel_id=1, source_target_pairs={{0,4},{4,8},{8,12},{12,0},{1,5},{5,9},{9,13},{13,1},{2,6},{6,10},{... | collective-permute-start | bytes 196616 | tf_op jit(solution)/shard_map/ppermute | solution.py:27
  17.8 6.5 %collective-permute-start.7 = (f32[128,128]{1,0:T(8,128)}, f32[128,128]{1,0:T(8,128)S(1)}, u32[]{:S(2)}, u32[]{:S(2)}) collective-permute-start(f32[128,128]{1,0:T(8,128)} %get-tuple-element.27), channel_id=1, source_target_pairs={{0,12},{4,0},{8,4},{12,8},{1,13},{5,1},{9,5},{13,9},{2,14},{6,2},{... | collective-permute-start | bytes 196616 | tf_op jit(solution)/shard_map/ppermute | solution.py:27
  21.0 3.4 %collective-permute-start.8 = (f32[32,128]{1,0:T(8,128)}, f32[32,128]{1,0:T(8,128)S(1)}, u32[]{:S(2)}, u32[]{:S(2)}) collective-permute-start(f32[32,128]{1,0:T(8,128)} %get-tuple-element.28), channel_id=1, source_target_pairs={{0,1},{1,2},{2,3},{3,0},{4,5},{5,6},{6,7},{7,4},{8,9},{9,10},{10,1... | collective-permute-start | bytes 49160 | tf_op jit(solution)/shard_map/ppermute | solution.py:27
  21.9 0.8 %copy-start.10 = (s32[1,1,1,256]{3,2,1,0:T(1,128)S(1)}, s32[1,1,1,256]{3,2,1,0:T(1,128)}, u32[]{:S(2)}) copy-start(s32[1,1,1,256]{3,2,1,0:T(1,128)} %param.9) | copy-start | bytes 3076
  21.9 2.4 %collective-permute-start.9 = (f32[32,128]{1,0:T(8,128)}, f32[32,128]{1,0:T(8,128)S(1)}, u32[]{:S(2)}, u32[]{:S(2)}) collective-permute-start(f32[32,128]{1,0:T(8,128)} %get-tuple-element.29), channel_id=1, source_target_pairs={{0,3},{1,0},{2,1},{3,2},{4,7},{5,4},{6,5},{7,6},{8,11},{9,8},{10,9... | collective-permute-start | bytes 49160 | tf_op jit(solution)/shard_map/ppermute | solution.py:27
  24.4 0.6 %copy-start.8 = (f32[32,128]{1,0:T(8,128)}, f32[32,128]{1,0:T(8,128)S(1)}, u32[]{:S(2)}) copy-start(f32[32,128]{1,0:T(8,128)S(1)} %collective-permute-done.8.refs_10_) | copy-start | bytes 49156
  24.4 0.6 %copy-start.9 = (f32[32,128]{1,0:T(8,128)}, f32[32,128]{1,0:T(8,128)S(1)}, u32[]{:S(2)}) copy-start(f32[32,128]{1,0:T(8,128)S(1)} %collective-permute-done.9.refs_11_) | copy-start | bytes 49156
  24.4 0.6 %copy-start.6 = (f32[128,128]{1,0:T(8,128)}, f32[128,128]{1,0:T(8,128)S(1)}, u32[]{:S(2)}) copy-start(f32[128,128]{1,0:T(8,128)S(1)} %collective-permute-done.6.refs_8_) | copy-start | bytes 196612
  24.4 0.6 %copy-start.7 = (f32[128,128]{1,0:T(8,128)}, f32[128,128]{1,0:T(8,128)S(1)}, u32[]{:S(2)}) copy-start(f32[128,128]{1,0:T(8,128)S(1)} %collective-permute-done.7.refs_9_) | copy-start | bytes 196612
  24.4 0.7 %copy-start.1 = (f32[256,128]{1,0:T(8,128)}, f32[256,128]{1,0:T(8,128)S(1)}, u32[]{:S(2)}) copy-start(f32[256,128]{1,0:T(8,128)S(1)} %collective-permute-done.5.refs_6_.refs_7_) | copy-start | bytes 393220
  30.7 3.4 %collective-permute-start.12 = (f32[8,128]{1,0:T(8,128)}, f32[8,128]{1,0:T(8,128)S(1)}, u32[]{:S(2)}, u32[]{:S(2)}) collective-permute-start(f32[8,128]{1,0:T(8,128)} %get-tuple-element.31), channel_id=1, source_target_pairs={{0,3},{1,0},{2,1},{3,2},{4,7},{5,4},{6,5},{7,6},{8,11},{9,8},{10,9... | collective-permute-start | bytes 12296 | tf_op jit(solution)/shard_map/ppermute | solution.py:410
  32.4 3.8 %collective-permute-start.11 = (f32[8,128]{1,0:T(8,128)}, f32[8,128]{1,0:T(8,128)S(1)}, u32[]{:S(2)}, u32[]{:S(2)}) collective-permute-start(f32[8,128]{1,0:T(8,128)} %get-tuple-element.31), channel_id=1, source_target_pairs={{0,2},{1,3},{2,0},{3,1},{4,6},{5,7},{6,4},{7,5},{8,10},{9,11},{10,... | collective-permute-start | bytes 12296 | tf_op jit(solution)/shard_map/ppermute | solution.py:410
  34.1 3.2 %collective-permute-start.10 = (f32[8,128]{1,0:T(8,128)}, f32[8,128]{1,0:T(8,128)S(1)}, u32[]{:S(2)}, u32[]{:S(2)}) collective-permute-start(f32[8,128]{1,0:T(8,128)} %get-tuple-element.31), channel_id=1, source_target_pairs={{0,1},{1,2},{2,3},{3,0},{4,5},{5,6},{6,7},{7,4},{8,9},{9,10},{10,1... | collective-permute-start | bytes 12296 | tf_op jit(solution)/shard_map/ppermute | solution.py:410

commit v2 on v1

--- a/solution.py
+++ b/solution.py
@@ -9,6 +9,7 @@
 
 mass_term = 0.25
 lane_tile = 128
+vmem_grant = 16 << 20
 entry_pairs = ((0, 0), (1, 1), (2, 2), (0, 1), (0, 2), (1, 2))
 
 
@@ -330,6 +331,12 @@
         gram_ref[k : k + 1, :] = jnp.sum(lead[first] * lead[second], axis=0, keepdims=True)
 
 
+def call(body, **arguments):
+    return pl.pallas_call(
+        body, compiler_params=pltpu.CompilerParams(vmem_limit_bytes=vmem_grant), **arguments
+    )
+
+
 def in_vmem(count):
     return [pl.BlockSpec(memory_space=pltpu.VMEM)] * count
 
@@ -368,7 +375,7 @@
     positions = owner_slots.shape[0]
 
     field_shape = jax.ShapeDtypeStruct((rows_count * sensors, size_z), jnp.float32)
-    packed = pl.pallas_call(
+    packed = call(
         functools.partial(pack_kernel, dims, counts),
         out_shape=[field_shape] + face_shapes(dims, counts, 1),
         in_specs=in_vmem(2),
@@ -379,7 +386,7 @@
     source_halos = exchange_all(faces, counts)
 
     weight_shape = jax.ShapeDtypeStruct((8, size_x, size_y, size_z), jnp.float32)
-    result = pl.pallas_call(
+    result = call(
         functools.partial(apply_kernel, dims, counts),
         out_shape=[weight_shape, field_shape] + face_shapes(dims, counts, 0),
         in_specs=in_vmem(2) + [pl.BlockSpec(memory_space=pltpu.SMEM)] + in_vmem(6),
@@ -390,7 +397,7 @@
     applied_halos = exchange_all(faces, counts)
 
     base = 6 * sensors
-    columns, moment = pl.pallas_call(
+    columns, moment = call(
         functools.partial(select_kernel, dims),
         out_shape=[
             jax.ShapeDtypeStruct((slots, base), jnp.float32),
@@ -417,7 +424,7 @@
     received = lax.all_to_all(
         outgoing.reshape(owners, slots_each, base + extra), ("gx", "gy"), 0, 0, tiled=True
     ).reshape(slots, base + extra)
-    return pl.pallas_call(
+    return call(
         functools.partial(owner_kernel, sensors, slots_each),
         out_shape=[
             jax.ShapeDtypeStruct((3, times, positions), jnp.float32),

time: 54.5 us -> 47.5 us (0.87)
  Pallas kernels: 13.2 us -> 7.2 us
  other arithmetic: 1.75 us -> 0.11 us
    pallas_call x4, Pallas kernels: 13.2 us -> 7.2 us  [the longest x1 3.54 us: per_device(): call(functools.partial(select_kernel, dims), out_shape=[jax.ShapeDtypeStr...]
    unnamed x22 -> x12, local copies, waits for them, and re-layouts: 1.33 us -> 2.42 us
    concatenate x1, other arithmetic: 1.05 us -> 0.11 us  [per_device(): outgoing = jnp.concatenate([columns, spread], axis=1)]
    add x1, other arithmetic: 0.69 us -> 0.01 us  [per_device(): moment + sum((lax.ppermute(moment, 'gz', ring(depth, d)) for d in range(1...]
    reshape x1, local copies, waits for them, and re-layouts: 0.8 us -> 0.13 us  [per_device(): send_map.reshape(slots, 1)]
  transfers between devices with their start and end apart: 13 -> 13, of which waited for: 4 -> 4; matrix products, arithmetic and copies ran while one was open for 1% -> 0% of each run, Pallas kernels for 0% -> 0%
where the time goes in v2:
time: 47.5 us; the launch traced here: 47.2 us
  starting transfers between devices  18.1 us (38%)
  blocking collectives  12.6 us (27%)
  Pallas kernels  7.2 us (15%)
  waiting for transfers between devices  5.83 us (12%)
  local copies, waits for them, and re-layouts  2.65 us (6%)
  between operations  0.71 us (1%)
    all_to_all x1, blocking collectives, per_device(): lax.all_to_all(outgoing.reshape(owners, slots_each, base + extra), ('gx',...  12.6 us
    ppermute x4, starting transfers between devices, exchange(): lax.ppermute(low, axis, ring(count, -1))  7.9 us
    pallas_call x1, Pallas kernels, per_device(): call(functools.partial(select_kernel, dims), out_shape=[jax.ShapeDtypeStr...  3.54 us
    ppermute x3, starting transfers between devices, per_device(): lax.ppermute(moment, 'gz', ring(depth, d))  3.5 us
    ppermute x2, starting transfers between devices, exchange(): swapped = lax.ppermute(faces[0], axis, ring(2, 1))  3.41 us
    ppermute x4, starting transfers between devices, exchange(): lax.ppermute(high, axis, ring(count, 1))  3.24 us
    ppermute x3, waiting for transfers between devices, per_device(): lax.ppermute(moment, 'gz', ring(depth, d))  3.03 us
    ppermute x4, waiting for transfers between devices, exchange(): lax.ppermute(high, axis, ring(count, 1))  2.74 us
  transfers between devices with their start and end apart: 13, of which 4 were waited for; matrix products, arithmetic and copies ran while one was open for 0% of the time, Pallas kernels for 0%

profile of v2, /device:TPU:0, one launch (start us, length us, event | category | flops | bytes accessed | tf_op | source)
XLA Modules:
  0.0 47.2 jit_solution(7084896405899452218)
XLA Ops:
  0.6 0.0 copy-start
  0.6 1.0 %copy-done = f32[32,4,8,128]{3,2,1,0:T(8,128)S(1)} copy-done((f32[32,4,8,128]{3,2,1,0:T(8,128)S(1)}, f32[32,4,8,128]{3,2,1,0:T(8,128)}, u32[]{:S(2)}) %copy-start) | copy-done | bytes 524312
  1.7 0.0 copy-start.1
  1.7 0.7 %copy-done.1 = s32[4,8,128]{2,1,0:T(8,128)S(1)} copy-done((s32[4,8,128]{2,1,0:T(8,128)S(1)}, s32[4,8,128]{2,1,0:T(8,128)}, u32[]{:S(2)}) %copy-start.1) | copy-done | bytes 16408
  2.4 0.7 %pack.1 = (f32[1024,128]{1,0:T(8,128)S(1)}, f32[264,128]{1,0:T(8,128)S(1)}, f32[136,128]{1,0:T(8,128)S(1)}, f32[136,128]{1,0:T(8,128)S(1)}, f32[40,128]{1,0:T(8,128)S(1)}, /*index=5*/f32[40,128]{1,0:T(8,128)S(1)}) custom-call(f32[1024,128]{1,0:T(8,128)S(1)} %bitcast.8, s32[4,8,128]{2,1,0:T(8,128)S(1)} %copy-done.1), custom_call_target="tpu_custom_call" | custom-call | tf_op jit(solution)/shard_map/pack/pallas_call | solution.py:378
  3.1 3.1 %collective-permute-start = (f32[264,128]{1,0:T(8,128)S(1)}, f32[264,128]{1,0:T(8,128)S(1)}, u32[]{:S(2)}, u32[]{:S(2)}) collective-permute-start(f32[264,128]{1,0:T(8,128)S(1)} %get-tuple-element.18), channel_id=1, source_target_pairs={{0,16},{16,0},{1,17},{17,1},{2,18},{18,2},{3,19},{19,3},{4,20},{20... | collective-permute-start | bytes 405512 | tf_op jit(solution)/shard_map/ppermute | solution.py:25
  6.1 1.6 %collective-permute-start.1 = (f32[136,128]{1,0:T(8,128)S(1)}, f32[136,128]{1,0:T(8,128)S(1)}, u32[]{:S(2)}, u32[]{:S(2)}) collective-permute-start(f32[136,128]{1,0:T(8,128)S(1)} %get-tuple-element.19), channel_id=1, source_target_pairs={{0,4},{4,8},{8,12},{12,0},{1,5},{5,9},{9,13},{13,1},{2,6},{6,10},{... | collective-permute-start | bytes 208904 | tf_op jit(solution)/shard_map/ppermute | solution.py:28
  7.7 2.2 %collective-permute-start.2 = (f32[136,128]{1,0:T(8,128)S(1)}, f32[136,128]{1,0:T(8,128)S(1)}, u32[]{:S(2)}, u32[]{:S(2)}) collective-permute-start(f32[136,128]{1,0:T(8,128)S(1)} %get-tuple-element.20), channel_id=1, source_target_pairs={{0,12},{4,0},{8,4},{12,8},{1,13},{5,1},{9,5},{13,9},{2,14},{6,2},{... | collective-permute-start | bytes 208904 | tf_op jit(solution)/shard_map/ppermute | solution.py:28
  9.9 0.0 collective-permute-start.3
  9.9 0.0 copy-start.3
  9.9 1.7 %collective-permute-start.4 = (f32[40,128]{1,0:T(8,128)S(1)}, f32[40,128]{1,0:T(8,128)S(1)}, u32[]{:S(2)}, u32[]{:S(2)}) collective-permute-start(f32[40,128]{1,0:T(8,128)S(1)} %get-tuple-element.22), channel_id=1, source_target_pairs={{0,3},{1,0},{2,1},{3,2},{4,7},{5,4},{6,5},{7,6},{8,11},{9,8},{10,9... | collective-permute-start | bytes 61448 | tf_op jit(solution)/shard_map/ppermute | solution.py:28
  11.7 1.5 %collective-permute-done.3.refs_4_ = f32[40,128]{1,0:T(8,128)S(1)} collective-permute-done((f32[40,128]{1,0:T(8,128)S(1)}, f32[40,128]{1,0:T(8,128)S(1)}, u32[]{:S(2)}, u32[]{:S(2)}) %collective-permute-start.3) | collective-permute-done | bytes 20512 | tf_op jit(solution)/shard_map/ppermute | solution.py:28
  13.2 0.0 collective-permute-done.4.refs_5_
  13.2 0.0 collective-permute-done.1.refs_2_
  13.2 0.0 collective-permute-done.2.refs_3_
  13.2 0.0 collective-permute-done.refs_0_.refs_1_
  13.2 0.0 copy-done.3
  13.2 1.7 %apply.1 = (f32[8,4,8,128]{3,2,1,0:T(8,128)S(1)}, f32[1024,128]{1,0:T(8,128)S(1)}, f32[256,128]{1,0:T(8,128)S(1)}, f32[128,128]{1,0:T(8,128)S(1)}, f32[128,128]{...) custom-call(f32[1024,128]{1,0:T(8,128)S(1)} %get-tuple-element.17.rows_ref, s32[4,8,128]{2,1,0:T(8,128)S(1)} %copy-done.1, ...), custom_call_target="tpu_custom_call" | custom-call | tf_op jit(solution)/shard_map/apply/pallas_call | solution.py:389
  14.9 0.4 collective-permute-start.5
  15.3 0.7 %collective-permute-start.6 = (f32[128,128]{1,0:T(8,128)S(1)}, f32[128,128]{1,0:T(8,128)S(1)}, u32[]{:S(2)}, u32[]{:S(2)}) collective-permute-start(f32[128,128]{1,0:T(8,128)S(1)} %get-tuple-element.26), channel_id=1, source_target_pairs={{0,4},{4,8},{8,12},{12,0},{1,5},{5,9},{9,13},{13,1},{2,6},{6,10},{... | collective-permute-start | bytes 196616 | tf_op jit(solution)/shard_map/ppermute | solution.py:28
  16.0 3.1 %collective-permute-start.7 = (f32[128,128]{1,0:T(8,128)S(1)}, f32[128,128]{1,0:T(8,128)S(1)}, u32[]{:S(2)}, u32[]{:S(2)}) collective-permute-start(f32[128,128]{1,0:T(8,128)S(1)} %get-tuple-element.27), channel_id=1, source_target_pairs={{0,12},{4,0},{8,4},{12,8},{1,13},{5,1},{9,5},{13,9},{2,14},{6,2},{... | collective-permute-start | bytes 196616 | tf_op jit(solution)/shard_map/ppermute | solution.py:28
  19.1 1.0 %collective-permute-start.8 = (f32[32,128]{1,0:T(8,128)S(1)}, f32[32,128]{1,0:T(8,128)S(1)}, u32[]{:S(2)}, u32[]{:S(2)}) collective-permute-start(f32[32,128]{1,0:T(8,128)S(1)} %get-tuple-element.28), channel_id=1, source_target_pairs={{0,1},{1,2},{2,3},{3,0},{4,5},{5,6},{6,7},{7,4},{8,9},{9,10},{10,1... | collective-permute-start | bytes 49160 | tf_op jit(solution)/shard_map/ppermute | solution.py:28
  20.1 0.0 copy-start.5
  20.1 0.8 %collective-permute-start.9 = (f32[32,128]{1,0:T(8,128)S(1)}, f32[32,128]{1,0:T(8,128)S(1)}, u32[]{:S(2)}, u32[]{:S(2)}) collective-permute-start(f32[32,128]{1,0:T(8,128)S(1)} %get-tuple-element.29), channel_id=1, source_target_pairs={{0,3},{1,0},{2,1},{3,2},{4,7},{5,4},{6,5},{7,6},{8,11},{9,8},{10,9... | collective-permute-start | bytes 49160 | tf_op jit(solution)/shard_map/ppermute | solution.py:28
  20.8 0.0 copy-done.5
  20.8 0.1 copy.8.voxel_ref
  21.0 1.3 %collective-permute-done.8.refs_10_ = f32[32,128]{1,0:T(8,128)S(1)} collective-permute-done((f32[32,128]{1,0:T(8,128)S(1)}, f32[32,128]{1,0:T(8,128)S(1)}, u32[]{:S(2)}, u32[]{:S(2)}) %collective-permute-start.8) | collective-permute-done | bytes 16416 | tf_op jit(solution)/shard_map/ppermute | solution.py:28
  22.3 0.0 collective-permute-done.9.refs_11_
  22.3 0.0 collective-permute-done.6.refs_8_
  22.3 0.0 collective-permute-done.7.refs_9_
  22.3 0.0 collective-permute-done.5.refs_6_.refs_7_
  22.3 3.5 %choose.1 = (f32[256,192]{1,0:T(8,128)S(1)}, f32[8,128]{1,0:T(8,128)S(1)}) custom-call(f32[1024,128]{1,0:T(8,128)S(1)} %get-tuple-element.17.rows_ref, f32[1024,128]{1,0:T(8,128)S(1)} %get-tuple-element.23.applied_ref, f32[8,4,8,128]{3,2,1,0:T(8,128)S(1)} %get-tuple-element.24.weight_ref, s32[256,1]{1,0:T(8,128)S(1)} %copy.8.voxel_ref, ...), custom_call_target="tpu_custom_call" | custom-call | tf_op jit(solution)/shard_map/choose/pallas_call | solution.py:400
  25.8 1.8 %collective-permute-start.12 = (f32[8,128]{1,0:T(8,128)S(1)}, f32[8,128]{1,0:T(8,128)S(1)}, u32[]{:S(2)}, u32[]{:S(2)}) collective-permute-start(f32[8,128]{1,0:T(8,128)S(1)} %get-tuple-element.31), channel_id=1, source_target_pairs={{0,3},{1,0},{2,1},{3,2},{4,7},{5,4},{6,5},{7,6},{8,11},{9,8},{10,9... | collective-permute-start | bytes 12296 | tf_op jit(solution)/shard_map/ppermute | solution.py:417
  27.6 1.7 %collective-permute-start.11 = (f32[8,128]{1,0:T(8,128)S(1)}, f32[8,128]{1,0:T(8,128)S(1)}, u32[]{:S(2)}, u32[]{:S(2)}) collective-permute-start(f32[8,128]{1,0:T(8,128)S(1)} %get-tuple-element.31), channel_id=1, source_target_pairs={{0,2},{1,3},{2,0},{3,1},{4,6},{5,7},{6,4},{7,5},{8,10},{9,11},{10,... | collective-permute-start | bytes 12296 | tf_op jit(solution)/shard_map/ppermute | solution.py:417
  29.3 0.0 collective-permute-start.10
  29.4 0.0 collective-permute-done.12
  29.4 1.9 %collective-permute-done.11 = f32[8,128]{1,0:T(8,128)S(1)} collective-permute-done((f32[8,128]{1,0:T(8,128)S(1)}, f32[8,128]{1,0:T(8,128)S(1)}, u32[]{:S(2)}, u32[]{:S(2)}) %collective-permute-start.11) | collective-permute-done | bytes 4128 | tf_op jit(solution)/shard_map/ppermute | solution.py:417
  31.2 1.1 %collective-permute-done.10 = f32[8,128]{1,0:T(8,128)S(1)} collective-permute-done((f32[8,128]{1,0:T(8,128)S(1)}, f32[8,128]{1,0:T(8,128)S(1)}, u32[]{:S(2)}, u32[]{:S(2)}) %collective-permute-start.10) | collective-permute-done | bytes 4128 | tf_op jit(solution)/shard_map/ppermute | solution.py:417
  32.4 0.1 broadcast_in_dim.7
  32.5 0.1 pad_maximum_fusion
  32.6 0.0 copy-start.2
  32.6 12.6 %all_to_all.5 = f32[8,32,256]{2,1,0:T(8,128)S(1)} all-to-all(f32[8,32,256]{2,1,0:T(8,128)S(1)} %pad_maximum_fusion), channel_id=1, replica_groups=mesh['gx'=2,'gy'=4,'gz'=4] {'gx','gy'}, dimensions={0} | all-to-all | bytes 524288 | tf_op jit(solution)/shard_map/all_to_all | solution.py:424
  45.3 0.0 copy-start.4
  45.3 0.0 copy-done.2
  45.3 0.7 %copy-done.4 = s32[128]{0:T(128)S(1)} copy-done((s32[128]{0:T(128)S(1)}, s32[128]{0:T(128)}, u32[]{:S(2)}) %copy-start.4) | copy-done | bytes 536
  45.9 1.3 %owner.1 = (f32[3,128,128]{2,1,0:T(8,128)}, f32[6,128]{1,0:T(8,128)}) custom-call(f32[256,256]{1,0:T(8,128)S(1)} %bitcast.7, s32[1,128]{1,0:T(1,128)S(1)} %bitcast.10, f32[32,128]{1,0:T(8,128)S(1)} %copy-done.2), custom_call_target="tpu_custom_call" | custom-call | tf_op jit(solution)/shard_map/owner/pallas_call | solution.py:427
  (4 shorter events, 0.0 us)
Async XLA Ops:
  0.6 1.0 %copy-start = (f32[32,4,8,128]{3,2,1,0:T(8,128)S(1)}, f32[32,4,8,128]{3,2,1,0:T(8,128)}, u32[]{:S(2)}) copy-start(f32[32,4,8,128]{3,2,1,0:T(8,128)} %param.6) | copy-start | bytes 1572868
  1.7 0.7 %copy-start.1 = (s32[4,8,128]{2,1,0:T(8,128)S(1)}, s32[4,8,128]{2,1,0:T(8,128)}, u32[]{:S(2)}) copy-start(s32[4,8,128]{2,1,0:T(8,128)} %label_ref.3) | copy-start | bytes 49156
  3.1 10.1 %collective-permute-start = (f32[264,128]{1,0:T(8,128)S(1)}, f32[264,128]{1,0:T(8,128)S(1)}, u32[]{:S(2)}, u32[]{:S(2)}) collective-permute-start(f32[264,128]{1,0:T(8,128)S(1)} %get-tuple-element.18), channel_id=1, source_target_pairs={{0,16},{16,0},{1,17},{17,1},{2,18},{18,2},{3,19},{19,3},{4,20},{20... | collective-permute-start | bytes 405512 | tf_op jit(solution)/shard_map/ppermute | solution.py:25
  6.1 7.1 %collective-permute-start.1 = (f32[136,128]{1,0:T(8,128)S(1)}, f32[136,128]{1,0:T(8,128)S(1)}, u32[]{:S(2)}, u32[]{:S(2)}) collective-permute-start(f32[136,128]{1,0:T(8,128)S(1)} %get-tuple-element.19), channel_id=1, source_target_pairs={{0,4},{4,8},{8,12},{12,0},{1,5},{5,9},{9,13},{13,1},{2,6},{6,10},{... | collective-permute-start | bytes 208904 | tf_op jit(solution)/shard_map/ppermute | solution.py:28
  7.7 5.5 %collective-permute-start.2 = (f32[136,128]{1,0:T(8,128)S(1)}, f32[136,128]{1,0:T(8,128)S(1)}, u32[]{:S(2)}, u32[]{:S(2)}) collective-permute-start(f32[136,128]{1,0:T(8,128)S(1)} %get-tuple-element.20), channel_id=1, source_target_pairs={{0,12},{4,0},{8,4},{12,8},{1,13},{5,1},{9,5},{13,9},{2,14},{6,2},{... | collective-permute-start | bytes 208904 | tf_op jit(solution)/shard_map/ppermute | solution.py:28
  9.9 3.2 %collective-permute-start.3 = (f32[40,128]{1,0:T(8,128)S(1)}, f32[40,128]{1,0:T(8,128)S(1)}, u32[]{:S(2)}, u32[]{:S(2)}) collective-permute-start(f32[40,128]{1,0:T(8,128)S(1)} %get-tuple-element.21), channel_id=1, source_target_pairs={{0,1},{1,2},{2,3},{3,0},{4,5},{5,6},{6,7},{7,4},{8,9},{9,10},{10,1... | collective-permute-start | bytes 61448 | tf_op jit(solution)/shard_map/ppermute | solution.py:28
  9.9 3.2 %copy-start.3 = (f32[6]{0:T(128)S(1)}, f32[6]{0:T(128)}, u32[]{:S(2)}) copy-start(f32[6]{0:T(128)} %table_ref.1) | copy-start | bytes 76
  9.9 3.2 %collective-permute-start.4 = (f32[40,128]{1,0:T(8,128)S(1)}, f32[40,128]{1,0:T(8,128)S(1)}, u32[]{:S(2)}, u32[]{:S(2)}) collective-permute-start(f32[40,128]{1,0:T(8,128)S(1)} %get-tuple-element.22), channel_id=1, source_target_pairs={{0,3},{1,0},{2,1},{3,2},{4,7},{5,4},{6,5},{7,6},{8,11},{9,8},{10,9... | collective-permute-start | bytes 61448 | tf_op jit(solution)/shard_map/ppermute | solution.py:28
  14.9 7.4 %collective-permute-start.5 = (f32[256,128]{1,0:T(8,128)S(1)}, f32[256,128]{1,0:T(8,128)S(1)}, u32[]{:S(2)}, u32[]{:S(2)}) collective-permute-start(f32[256,128]{1,0:T(8,128)S(1)} %get-tuple-element.25), channel_id=1, source_target_pairs={{0,16},{16,0},{1,17},{17,1},{2,18},{18,2},{3,19},{19,3},{4,20},{20... | collective-permute-start | bytes 393224 | tf_op jit(solution)/shard_map/ppermute | solution.py:25
  15.3 7.0 %collective-permute-start.6 = (f32[128,128]{1,0:T(8,128)S(1)}, f32[128,128]{1,0:T(8,128)S(1)}, u32[]{:S(2)}, u32[]{:S(2)}) collective-permute-start(f32[128,128]{1,0:T(8,128)S(1)} %get-tuple-element.26), channel_id=1, source_target_pairs={{0,4},{4,8},{8,12},{12,0},{1,5},{5,9},{9,13},{13,1},{2,6},{6,10},{... | collective-permute-start | bytes 196616 | tf_op jit(solution)/shard_map/ppermute | solution.py:28
  16.0 6.3 %collective-permute-start.7 = (f32[128,128]{1,0:T(8,128)S(1)}, f32[128,128]{1,0:T(8,128)S(1)}, u32[]{:S(2)}, u32[]{:S(2)}) collective-permute-start(f32[128,128]{1,0:T(8,128)S(1)} %get-tuple-element.27), channel_id=1, source_target_pairs={{0,12},{4,0},{8,4},{12,8},{1,13},{5,1},{9,5},{13,9},{2,14},{6,2},{... | collective-permute-start | bytes 196616 | tf_op jit(solution)/shard_map/ppermute | solution.py:28
  19.1 3.2 %collective-permute-start.8 = (f32[32,128]{1,0:T(8,128)S(1)}, f32[32,128]{1,0:T(8,128)S(1)}, u32[]{:S(2)}, u32[]{:S(2)}) collective-permute-start(f32[32,128]{1,0:T(8,128)S(1)} %get-tuple-element.28), channel_id=1, source_target_pairs={{0,1},{1,2},{2,3},{3,0},{4,5},{5,6},{6,7},{7,4},{8,9},{9,10},{10,1... | collective-permute-start | bytes 49160 | tf_op jit(solution)/shard_map/ppermute | solution.py:28
  20.1 0.8 %copy-start.5 = (s32[1,1,1,256]{3,2,1,0:T(1,128)S(1)}, s32[1,1,1,256]{3,2,1,0:T(1,128)}, u32[]{:S(2)}) copy-start(s32[1,1,1,256]{3,2,1,0:T(1,128)} %param.9) | copy-start | bytes 3076
  20.1 2.2 %collective-permute-start.9 = (f32[32,128]{1,0:T(8,128)S(1)}, f32[32,128]{1,0:T(8,128)S(1)}, u32[]{:S(2)}, u32[]{:S(2)}) collective-permute-start(f32[32,128]{1,0:T(8,128)S(1)} %get-tuple-element.29), channel_id=1, source_target_pairs={{0,3},{1,0},{2,1},{3,2},{4,7},{5,4},{6,5},{7,6},{8,11},{9,8},{10,9... | collective-permute-start | bytes 49160 | tf_op jit(solution)/shard_map/ppermute | solution.py:28
  25.8 3.5 %collective-permute-start.12 = (f32[8,128]{1,0:T(8,128)S(1)}, f32[8,128]{1,0:T(8,128)S(1)}, u32[]{:S(2)}, u32[]{:S(2)}) collective-permute-start(f32[8,128]{1,0:T(8,128)S(1)} %get-tuple-element.31), channel_id=1, source_target_pairs={{0,3},{1,0},{2,1},{3,2},{4,7},{5,4},{6,5},{7,6},{8,11},{9,8},{10,9... | collective-permute-start | bytes 12296 | tf_op jit(solution)/shard_map/ppermute | solution.py:417
  27.6 3.6 %collective-permute-start.11 = (f32[8,128]{1,0:T(8,128)S(1)}, f32[8,128]{1,0:T(8,128)S(1)}, u32[]{:S(2)}, u32[]{:S(2)}) collective-permute-start(f32[8,128]{1,0:T(8,128)S(1)} %get-tuple-element.31), channel_id=1, source_target_pairs={{0,2},{1,3},{2,0},{3,1},{4,6},{5,7},{6,4},{7,5},{8,10},{9,11},{10,... | collective-permute-start | bytes 12296 | tf_op jit(solution)/shard_map/ppermute | solution.py:417
  29.3 3.0 %collective-permute-start.10 = (f32[8,128]{1,0:T(8,128)S(1)}, f32[8,128]{1,0:T(8,128)S(1)}, u32[]{:S(2)}, u32[]{:S(2)}) collective-permute-start(f32[8,128]{1,0:T(8,128)S(1)} %get-tuple-element.31), channel_id=1, source_target_pairs={{0,1},{1,2},{2,3},{3,0},{4,5},{5,6},{6,7},{7,4},{8,9},{9,10},{10,1... | collective-permute-start | bytes 12296 | tf_op jit(solution)/shard_map/ppermute | solution.py:417
  32.6 12.7 %copy-start.2 = (f32[32,128]{1,0:T(8,128)S(1)}, f32[32,128]{1,0:T(8,128)}, u32[]{:S(2)}) copy-start(f32[32,128]{1,0:T(8,128)} %data_ref.1) | copy-start | bytes 49156
  45.3 0.7 %copy-start.4 = (s32[128]{0:T(128)S(1)}, s32[128]{0:T(128)}, u32[]{:S(2)}) copy-start(s32[128]{0:T(128)} %param.10) | copy-start | bytes 1540

commit v3 on v2

--- a/solution.py
+++ b/solution.py
@@ -10,6 +10,7 @@
 mass_term = 0.25
 lane_tile = 128
 vmem_grant = 16 << 20
+last_with_last = (((1,), (1,)), ((), ()))
 entry_pairs = ((0, 0), (1, 1), (2, 2), (0, 1), (0, 2), (1, 2))
 
 
@@ -104,14 +105,73 @@
     return groups
 
 
-def pack_kernel(dims, counts, source_ref, label_ref, rows_ref, *face_refs):
-    sensors, size_x, size_y, size_z = dims
-    count = size_x * size_y
-    for r in range(count):
-        rows_ref[r * sensors : (r + 1) * sensors, :] = source_ref[pl.ds(r, sensors, stride=count), :]
-    shifted = [(label_ref[x] + 1).astype(jnp.float32) for x in range(size_x)]
+def pack_kernel(dims, counts, source_ref, label_ref, rows_ref, shifted_ref, *refs):
+    sensors, size_x, size_y, size_z = dims
+    face_refs, (staged_ref, label_vmem, semaphores) = refs[:-3], refs[-3:]
+    copies = [
+        pltpu.make_async_copy(source_ref.at[:, x], staged_ref.at[x], semaphores.at[x])
+        for x in range(size_x)
+    ]
+    copies.append(pltpu.make_async_copy(label_ref, label_vmem, semaphores.at[size_x]))
+    for copy in copies:
+        copy.start()
+    flat = staged_ref.reshape(size_x, sensors * size_y, size_z)
+    for x in range(size_x):
+        copies[x].wait()
+        for y in range(size_y):
+            r = x * size_y + y
+            rows_ref[r * sensors : (r + 1) * sensors, :] = flat[x, pl.ds(y, sensors, stride=size_y), :]
+    copies[size_x].wait()
+    shifted = [(label_vmem[x] + 1).astype(jnp.float32) for x in range(size_x)]
+    for x in range(size_x):
+        shifted_ref[x] = shifted[x]
     field = lambda r: rows_ref[r * sensors : (r + 1) * sensors, :]
     write_faces(dims, field, split_refs(face_refs, counts), shifted)
+
+
+def prepare_kernel(
+    size_z,
+    voxel_hbm,
+    owned_hbm,
+    data_hbm,
+    table_hbm,
+    chosen_ref,
+    owned_chosen_ref,
+    held_ref,
+    table_ref,
+    voxel_ref,
+    owned_ref,
+    level_ref,
+    semaphores,
+):
+    moves = (
+        (voxel_hbm, voxel_ref),
+        (owned_hbm, owned_ref),
+        (data_hbm, held_ref),
+        (table_hbm, level_ref),
+    )
+    copies = [pltpu.make_async_copy(*move, semaphores.at[k]) for k, move in enumerate(moves)]
+    for copy in copies:
+        copy.start()
+    for copy in copies:
+        copy.wait()
+    for level in range(level_ref.shape[0]):
+        table_ref[level] = jnp.full(table_ref.shape[1:], level_ref[level], jnp.float32)
+    slots, voxels = chosen_ref.shape
+    square = (slots, slots)
+    diagonal = lanes_equal(square, lax.broadcasted_iota(jnp.int32, square, 0))
+    voxel = jnp.where(diagonal, voxel_ref[...].astype(jnp.float32), 0.0)
+    voxel = jnp.sum(voxel, axis=1, keepdims=True).astype(jnp.int32)
+    voxel = jnp.broadcast_to(voxel, (slots, size_z))
+    lane_index = lax.broadcasted_iota(jnp.int32, (slots, size_z), 1)
+    for first in range(0, voxels, size_z):
+        chosen_ref[:, first : first + size_z] = one_hot(lane_index == voxel - first)
+    slot_index = lax.broadcasted_iota(jnp.int32, owned_chosen_ref.shape, 0)
+    owned_chosen_ref[...] = one_hot(slot_index == owned_ref[...])
+
+
+def one_hot(condition):
+    return condition.astype(jnp.float32).astype(jnp.bfloat16)
 
 
 def tissue(shifted, table_ref):
@@ -125,7 +185,7 @@
     return 0.5 * (first[0] + second[0]) * first[1] * second[1]
 
 
-def weights(dims, label_ref, table_ref, halo_refs, weight_ref):
+def weights(dims, shifted_ref, table_ref, halo_refs, weight_ref):
     sensors, size_x, size_y, size_z = dims
     flags = neighbour_flags()
     (x_low, x_high), (y_low, y_high), (z_low, z_high) = halo_refs
@@ -133,7 +193,7 @@
     def masked(value, flag):
         return jnp.where(flag, value, 0.0)
 
-    own = [(label_ref[x] + 1).astype(jnp.float32) for x in range(size_x)]
+    own = [shifted_ref[x] for x in range(size_x)]
     own_tissue = [tissue(plane, table_ref) for plane in own]
     x_rows = slice(size_y * sensors, size_y * (sensors + 1))
     below = tissue(masked(x_low[x_rows, :], flags[0][0]), table_ref)
@@ -217,12 +277,12 @@
     return [(refs[2 * i], refs[2 * i + 1]) for i in range(3)]
 
 
-def apply_kernel(dims, counts, rows_ref, label_ref, table_ref, *refs):
+def apply_kernel(dims, counts, rows_ref, shifted_ref, table_ref, *refs):
     sensors, size_x, size_y, size_z = dims
     halo_refs = pair_up(refs[:6])
     weight_ref, applied_ref = refs[6:8]
     face_refs = refs[8:]
-    weights(dims, label_ref, table_ref, halo_refs, weight_ref)
+    weights(dims, shifted_ref, table_ref, halo_refs, weight_ref)
     for r in range(size_x * size_y):
         x, y = divmod(r, size_y)
         centre, beside = around(dims, rows_ref, halo_refs, r)
@@ -236,64 +296,131 @@
     return high, (value - high.astype(jnp.float32)).astype(jnp.bfloat16)
 
 
-def select_kernel(dims, rows_ref, applied_ref, weight_ref, voxel_ref, *refs):
-    sensors, size_x, size_y, size_z = dims
-    source_halos = pair_up(refs[:6])
-    applied_halos = pair_up(refs[6:12])
-    column_ref, moment_ref, chosen_ref, high_ref, low_ref = refs[12:]
+def local_twice(dims, rows_ref, weight_ref, r):
+    sensors, size_x, size_y, size_z = dims
+    x, y = divmod(r, size_y)
+
+    def row(index):
+        return rows_ref[index * sensors : (index + 1) * sensors, :]
+
+    def weight(k):
+        return weight_ref[k, x, y : y + 1, :]
+
+    centre = row(r)
+    lane_index = lax.broadcasted_iota(jnp.int32, centre.shape, 1)
+    total = weight(6) * centre
+    if x > 0:
+        total = total - weight(0) * row(r - size_y)
+    if x < size_x - 1:
+        total = total - weight(1) * row(r + size_y)
+    if y > 0:
+        total = total - weight(2) * row(r - 1)
+    if y < size_y - 1:
+        total = total - weight(3) * row(r + 1)
+    before = jnp.where(lane_index == 0, 0.0, pltpu.roll(centre, 1, 1))
+    after = jnp.where(lane_index == size_z - 1, 0.0, pltpu.roll(centre, size_z - 1, 1))
+    return total - weight(4) * before - weight(5) * after
+
+
+def select_columns(dims, rows_ref, weight_ref, halo_refs, chosen_ref, high_ref, low_ref):
+    sensors, size_x, size_y, size_z = dims
     flags = neighbour_flags()
-    slots = voxel_ref.shape[0]
-    sums = [jnp.zeros((sensors, size_z), jnp.float32) for _ in range(4)]
-    lane_index = lax.broadcasted_iota(jnp.int32, (slots, size_z), 1)
-    voxel = voxel_ref[...]
     for r in range(size_x * size_y):
         x, y = divmod(r, size_y)
         span = slice(r * size_z, (r + 1) * size_z)
-        chosen_ref[:, span] = (lane_index == voxel - r * size_z).astype(jnp.float32).astype(jnp.bfloat16)
         scale = weight_ref[7, x, y : y + 1, :]
-        source, source_beside = around(dims, rows_ref, source_halos, r, flags)
-        applied, applied_beside = around(dims, applied_ref, applied_halos, r, flags)
-        twice = combine(weight_ref, x, y, applied, applied_beside)
+        _, beside = around(dims, rows_ref, halo_refs, r, flags)
+        for c in range(3):
+            high, low = halves(scale * (beside[2 * c + 1] - beside[2 * c]))
+            high_ref[c * sensors : (c + 1) * sensors, span] = high
+            low_ref[c * sensors : (c + 1) * sensors, span] = low
+    chosen = chosen_ref[...]
+    return lax.dot_general(
+        chosen, high_ref[...], last_with_last, preferred_element_type=jnp.float32
+    ) + lax.dot_general(chosen, low_ref[...], last_with_last, preferred_element_type=jnp.float32)
+
+
+def source_kernel(dims, rows_ref, applied_ref, weight_ref, chosen_ref, *refs):
+    sensors, size_x, size_y, size_z = dims
+    halo_refs = pair_up(refs[:6])
+    column_ref, sum_ref, high_ref, low_ref = refs[6:]
+    sums = [jnp.zeros((sensors, size_z), jnp.float32) for _ in range(4)]
+    for r in range(size_x * size_y):
+        source = rows_ref[r * sensors : (r + 1) * sensors, :]
+        applied = applied_ref[r * sensors : (r + 1) * sensors, :]
+        twice = local_twice(dims, applied_ref, weight_ref, r)
         for k, product in enumerate(
             (source * source, source * applied, applied * applied, applied * twice)
         ):
             sums[k] = sums[k] + product
-        for part, beside in enumerate((source_beside, applied_beside)):
-            for c in range(3):
-                high, low = halves(scale * (beside[2 * c + 1] - beside[2 * c]))
-                first = (part * 3 + c) * sensors
-                high_ref[first : first + sensors, span] = high
-                low_ref[first : first + sensors, span] = low
-    contract = (((1,), (1,)), ((), ()))
-    chosen = chosen_ref[...]
-    column_ref[...] = lax.dot_general(
-        chosen, high_ref[...], contract, preferred_element_type=jnp.float32
-    ) + lax.dot_general(chosen, low_ref[...], contract, preferred_element_type=jnp.float32)
-    stacked = jnp.concatenate(sums, axis=0)
+    for k in range(4):
+        sum_ref[k * sensors : (k + 1) * sensors, :] = sums[k]
+    column_ref[...] = select_columns(
+        dims, rows_ref, weight_ref, halo_refs, chosen_ref, high_ref, low_ref
+    )
+
+
+def moment_kernel(dims, applied_ref, weight_ref, sum_ref, *refs):
+    sensors, size_x, size_y, size_z = dims
+    (x_low, x_high), (y_low, y_high), (z_low, z_high) = pair_up(refs[:6])
+    moment_ref = refs[6]
+
+    def part(ref, index):
+        return ref[index * sensors : (index + 1) * sensors, :]
+
+    def crossing(k, r, beside):
+        x, y = divmod(r, size_y)
+        return weight_ref[k, x, y : y + 1, :] * part(applied_ref, r) * beside
+
+    zero = jnp.zeros((sensors, size_z), jnp.float32)
+    outward, below, above = zero, zero, zero
+    for y in range(size_y):
+        outward = outward + crossing(0, y, part(x_low, y))
+        outward = outward + crossing(1, (size_x - 1) * size_y + y, part(x_high, y))
+    for x in range(size_x):
+        outward = outward + crossing(2, x * size_y, part(y_low, x))
+        outward = outward + crossing(3, x * size_y + size_y - 1, part(y_high, x))
+    for r in range(size_x * size_y):
+        below = below + crossing(4, r, z_low[0:sensors, r : r + 1])
+        above = above + crossing(5, r, z_high[0:sensors, r : r + 1])
+    lane_index = lax.broadcasted_iota(jnp.int32, zero.shape, 1)
+    outward = outward + jnp.where(lane_index == 0, below, 0.0)
+    outward = outward + jnp.where(lane_index == size_z - 1, above, 0.0)
+    last = part(sum_ref, 3) - outward
     moment_ref[...] = lax.dot_general(
         jnp.ones((8, size_z), jnp.float32),
-        stacked,
-        contract,
+        jnp.concatenate([sum_ref[0 : 3 * sensors, :], last], axis=0),
+        last_with_last,
         precision=lax.Precision.HIGHEST,
         preferred_element_type=jnp.float32,
     )
 
 
-def owner_kernel(sensors, slots_each, received_ref, owned_ref, data_ref, projection_ref, gram_ref):
+def applied_kernel(dims, applied_ref, weight_ref, chosen_ref, source_column_ref, *refs):
+    sensors = dims[0]
+    column_ref, high_ref, low_ref = refs[6:]
+    half = column_ref.shape[1] // 2
+    column_ref[...] = jnp.zeros_like(column_ref)
+    column_ref[:, 0 : 3 * sensors] = source_column_ref[...]
+    column_ref[:, half : half + 3 * sensors] = select_columns(
+        dims, applied_ref, weight_ref, pair_up(refs[:6]), chosen_ref, high_ref, low_ref
+    )
+
+
+def owner_kernel(sensors, slots_each, received_ref, chosen_ref, data_ref, projection_ref, gram_ref):
     total, width = received_ref.shape
-    base = 6 * sensors
-    extra = width - base
-    moment_rows = -(-4 * sensors // extra)
-    gathered = jnp.zeros((moment_rows, extra), jnp.float32)
-    for source in range(total // slots_each):
-        first = source * slots_each
-        gathered = gathered + received_ref[first : first + moment_rows, base:width]
+    half = width // 2
+    gathered = [jnp.zeros((2, sensors), jnp.float32) for _ in range(2)]
+    for first in range(0, total, slots_each):
+        for k in range(2):
+            start = k * half + 3 * sensors
+            gathered[k] = gathered[k] + received_ref[first : first + 2, start : start + sensors]
     moments = []
-    sensor_index = lax.broadcasted_iota(jnp.int32, (sensors, extra), 0)
-    lane_index = lax.broadcasted_iota(jnp.int32, (sensors, extra), 1)
+    sensor_index = lax.broadcasted_iota(jnp.int32, (sensors, sensors), 0)
+    lane_index = lax.broadcasted_iota(jnp.int32, (sensors, sensors), 1)
     for k in range(4):
-        row, offset = divmod(k * sensors, extra)
-        picked = jnp.where(lane_index == sensor_index + offset, gathered[row : row + 1, :], 0.0)
+        row = gathered[k % 2][k // 2 : k // 2 + 1, :]
+        picked = jnp.where(lane_index == sensor_index, row, 0.0)
         moments.append(jnp.sum(picked, axis=1, keepdims=True))
     moment_zero, moment_one, moment_two, moment_three = moments
     first_step = moment_zero / moment_one
@@ -307,18 +434,18 @@
     second_step = residue / curvature
     source_coef = first_step + second_step * growth
     applied_coef = second_step * first_step
-    positions = owned_ref.shape[1]
-    slot_index = lax.broadcasted_iota(jnp.int32, (total, positions), 0)
-    chosen = (slot_index == owned_ref[...]).astype(jnp.float32).astype(jnp.bfloat16)
-    high, low = halves(received_ref[:, 0:base])
+    chosen = chosen_ref[...]
     contract = (((0,), (0,)), ((), ()))
-    owned = lax.dot_general(
-        high, chosen, contract, preferred_element_type=jnp.float32
-    ) + lax.dot_general(low, chosen, contract, preferred_element_type=jnp.float32)
+    owned = []
+    for start in (0, half):
+        high, low = halves(received_ref[:, start : start + half])
+        owned.append(
+            lax.dot_general(high, chosen, contract, preferred_element_type=jnp.float32)
+            + lax.dot_general(low, chosen, contract, preferred_element_type=jnp.float32)
+        )
     lead = []
     for c in range(3):
-        source_part = owned[c * sensors : (c + 1) * sensors, :]
-        applied_part = owned[(3 + c) * sensors : (4 + c) * sensors, :]
+        source_part, applied_part = (part[c * sensors : (c + 1) * sensors, :] for part in owned)
         lead.append(source_coef * source_part - applied_coef * applied_part)
         projection_ref[c] = lax.dot_general(
             data_ref[...],
@@ -337,6 +464,14 @@
     )
 
 
+def in_hbm(count):
+    return [pl.BlockSpec(memory_space=pltpu.HBM)] * count
+
+
+def held_in_hbm(*arrays):
+    return [pltpu.with_memory_space_constraint(a, pltpu.HBM) for a in arrays]
+
+
 def in_vmem(count):
     return [pl.BlockSpec(memory_space=pltpu.VMEM)] * count
 
@@ -374,66 +509,106 @@
     times = sensor_data.shape[1]
     positions = owner_slots.shape[0]
 
-    field_shape = jax.ShapeDtypeStruct((rows_count * sensors, size_z), jnp.float32)
+    voxels = rows_count * size_z
+
+    def array(shape, dtype=jnp.float32):
+        return jax.ShapeDtypeStruct(shape, dtype)
+
+    def halves_scratch(rows):
+        return [pltpu.VMEM((rows, voxels), jnp.bfloat16)] * 2
+
+    field_shape = array((rows_count * sensors, size_z))
     packed = call(
         functools.partial(pack_kernel, dims, counts),
-        out_shape=[field_shape] + face_shapes(dims, counts, 1),
-        in_specs=in_vmem(2),
-        out_specs=in_vmem(1 + sum(counts)),
+        out_shape=[field_shape, array(labels.shape)] + face_shapes(dims, counts, 1),
+        in_specs=in_hbm(2),
+        out_specs=in_vmem(2 + sum(counts)),
+        scratch_shapes=[
+            pltpu.VMEM((size_x, sensors, size_y, size_z), jnp.float32),
+            pltpu.VMEM((size_x, size_y, size_z), jnp.int32),
+            pltpu.SemaphoreType.DMA((size_x + 1,)),
+        ],
         name="pack",
-    )(source_term.reshape(sensors * rows_count, size_z), labels)
-    rows, faces = packed[0], packed[1:]
+    )(*held_in_hbm(source_term, labels))
+    rows, shifted, faces = packed[0], packed[1], packed[2:]
     source_halos = exchange_all(faces, counts)
-
-    weight_shape = jax.ShapeDtypeStruct((8, size_x, size_y, size_z), jnp.float32)
+    levels = conductivity_table.shape[0]
+    chosen, owned_chosen, data, table = call(
+        functools.partial(prepare_kernel, size_z),
+        out_shape=[
+            array((slots, voxels), jnp.bfloat16),
+            array((slots, positions), jnp.bfloat16),
+            array(sensor_data.shape),
+            array((levels, size_y, size_z)),
+        ],
+        in_specs=in_hbm(4),
+        out_specs=in_vmem(4),
+        scratch_shapes=[
+            pltpu.VMEM((1, slots), jnp.int32),
+            pltpu.VMEM((1, positions), jnp.int32),
+            pltpu.SMEM((levels,), jnp.float32),
+            pltpu.SemaphoreType.DMA((4,)),
+        ],
+        name="prepare",
+    )(
+        *held_in_hbm(
+            send_map.reshape(1, slots),
+            owner_slots.reshape(1, positions),
+            sensor_data,
+            conductivity_table,
+        )
+    )
+
     result = call(
         functools.partial(apply_kernel, dims, counts),
-        out_shape=[weight_shape, field_shape] + face_shapes(dims, counts, 0),
-        in_specs=in_vmem(2) + [pl.BlockSpec(memory_space=pltpu.SMEM)] + in_vmem(6),
+        out_shape=[array((8, size_x, size_y, size_z)), field_shape] + face_shapes(dims, counts, 0),
+        in_specs=in_vmem(9),
         out_specs=in_vmem(2 + sum(counts)),
         name="apply",
-    )(rows, labels, conductivity_table, *source_halos)
+    )(rows, shifted, table, *source_halos)
     weight, applied, faces = result[0], result[1], result[2:]
     applied_halos = exchange_all(faces, counts)
 
-    base = 6 * sensors
-    columns, moment = call(
-        functools.partial(select_kernel, dims),
-        out_shape=[
-            jax.ShapeDtypeStruct((slots, base), jnp.float32),
-            jax.ShapeDtypeStruct((8, 4 * sensors), jnp.float32),
-        ],
-        in_specs=in_vmem(16),
+    source_columns, sums = call(
+        functools.partial(source_kernel, dims),
+        out_shape=[array((slots, 3 * sensors)), array((4 * sensors, size_z))],
+        in_specs=in_vmem(10),
         out_specs=in_vmem(2),
-        scratch_shapes=[
-            pltpu.VMEM((slots, rows_count * size_z), jnp.bfloat16),
-            pltpu.VMEM((base, rows_count * size_z), jnp.bfloat16),
-            pltpu.VMEM((base, rows_count * size_z), jnp.bfloat16),
-        ],
-        name="choose",
-    )(rows, applied, weight, send_map.reshape(slots, 1), *source_halos, *applied_halos)
-
+        scratch_shapes=halves_scratch(3 * sensors),
+        name="source_columns",
+    )(rows, applied, weight, chosen, *source_halos)
+    moment = call(
+        functools.partial(moment_kernel, dims),
+        out_shape=array((8, 4 * sensors)),
+        in_specs=in_vmem(9),
+        out_specs=in_vmem(1)[0],
+        name="moments",
+    )(applied, weight, sums, *applied_halos)
     depth = lax.axis_size("gz")
     moment = moment + sum(lax.ppermute(moment, "gz", ring(depth, d)) for d in range(1, depth))
-    extra = -base % lane_tile
-    while slots_each * extra < 4 * sensors:
-        extra += lane_tile
-    spread = jnp.pad(moment[0], (0, slots_each * extra - 4 * sensors)).reshape(1, slots_each, extra)
-    spread = jnp.broadcast_to(spread, (owners, slots_each, extra)).reshape(slots, extra)
-    outgoing = jnp.concatenate([columns, spread], axis=1)
-    received = lax.all_to_all(
-        outgoing.reshape(owners, slots_each, base + extra), ("gx", "gy"), 0, 0, tiled=True
-    ).reshape(slots, base + extra)
+
+    half = -(-4 * sensors // lane_tile) * lane_tile
+    columns = call(
+        functools.partial(applied_kernel, dims),
+        out_shape=array((slots, 2 * half)),
+        in_specs=in_vmem(10),
+        out_specs=in_vmem(1)[0],
+        scratch_shapes=halves_scratch(3 * sensors),
+        name="applied_columns",
+    )(applied, weight, chosen, source_columns, *applied_halos)
+    stamp = jnp.pad(
+        moment[0].reshape(1, 2, 2, sensors),
+        ((0, 0), (0, slots_each - 2), (0, 0), (3 * sensors, half - 4 * sensors)),
+    ).reshape(1, slots_each, 2 * half)
+    outgoing = columns.reshape(owners, slots_each, 2 * half) + stamp
+    received = lax.all_to_all(outgoing, ("gx", "gy"), 0, 0, tiled=True).reshape(slots, 2 * half)
     return call(
         functools.partial(owner_kernel, sensors, slots_each),
-        out_shape=[
-            jax.ShapeDtypeStruct((3, times, positions), jnp.float32),
-            jax.ShapeDtypeStruct((6, positions), jnp.float32),
-        ],
+        out_shape=[array((3, times, positions)), array((6, positions))],
         in_specs=in_vmem(3),
         out_specs=in_vmem(2),
         name="owner",
-    )(received, owner_slots.reshape(1, positions), sensor_data)
+    )(received, owned_chosen, data)
 
 
 def solution(mesh):

time: 47.5 us -> 43 us (0.905)
  waiting for transfers between devices: 5.83 us -> 1.55 us
  Pallas kernels: 7.2 us -> 9.93 us
  local copies, waits for them, and re-layouts: 2.65 us -> 0.19 us
  starting transfers between devices: 18.1 us -> 17.6 us
    ppermute x4, waiting for transfers between devices: 2.74 us -> 0.01 us  [exchange(): lax.ppermute(high, axis, ring(count, 1))]
    unnamed x12 -> x1, local copies, waits for them, and re-layouts: 2.42 us -> 0.01 us
    pallas_call x3 -> x6, Pallas kernels: 6.54 us -> 8.39 us  [the longest x1 1.98 us: per_device(): call(functools.partial(prepare_kernel, size_z), out_shape=[array((slots,...]
    ppermute x3, waiting for transfers between devices: 3.03 us -> 1.52 us  [per_device(): lax.ppermute(moment, 'gz', ring(depth, d))]
    ppermute x4, starting transfers between devices: 3.24 us -> 2.15 us  [exchange(): lax.ppermute(high, axis, ring(count, 1))]
    ppermute x4, starting transfers between devices: 7.9 us -> 8.99 us  [exchange(): lax.ppermute(low, axis, ring(count, -1))]
    pallas_call x1, Pallas kernels: 0.66 us -> 1.54 us  [per_device(): call(functools.partial(pack_kernel, dims, counts), out_shape=[field_shape...]
  transfers between devices with their start and end apart: 13 -> 13, of which waited for: 4 -> 2; matrix products, arithmetic and copies ran while one was open for 0% -> 0% of each run, Pallas kernels for 0% -> 12%
where the time goes in v3:
time: 43 us; the launch traced here: 42.7 us
  starting transfers between devices  17.6 us (41%)
  blocking collectives  12.7 us (30%)
  Pallas kernels  9.93 us (23%)
  waiting for transfers between devices  1.55 us (4%)
  between operations  0.77 us (2%)
    all_to_all x1, blocking collectives, per_device(): lax.all_to_all(outgoing, ('gx', 'gy'), 0, 0, tiled=True)  12.7 us
    ppermute x4, starting transfers between devices, exchange(): lax.ppermute(low, axis, ring(count, -1))  8.99 us
    ppermute x2, starting transfers between devices, exchange(): swapped = lax.ppermute(faces[0], axis, ring(2, 1))  3.41 us
    ppermute x3, starting transfers between devices, per_device(): lax.ppermute(moment, 'gz', ring(depth, d))  3.03 us
    ppermute x4, starting transfers between devices, exchange(): lax.ppermute(high, axis, ring(count, 1))  2.15 us
    pallas_call x1, Pallas kernels, per_device(): call(functools.partial(prepare_kernel, size_z), out_shape=[array((slots,...  1.98 us
    pallas_call x1, Pallas kernels, per_device(): call(functools.partial(source_kernel, dims), out_shape=[array((slots, 3 *...  1.83 us
    pallas_call x1, Pallas kernels, per_device(): call(functools.partial(pack_kernel, dims, counts), out_shape=[field_shape...  1.54 us
  transfers between devices with their start and end apart: 13, of which 2 were waited for; matrix products, arithmetic and copies ran while one was open for 0% of the time, Pallas kernels for 12%

profile of v3, /device:TPU:0, one launch (start us, length us, event | category | flops | bytes accessed | tf_op | source)
XLA Modules:
  0.0 42.7 jit_solution(9971436258583744077)
XLA Ops:
  0.6 1.5 %pack.1 = (f32[1024,128]{1,0:T(8,128)S(1)}, f32[4,8,128]{2,1,0:T(8,128)S(1)}, f32[264,128]{1,0:T(8,128)S(1)}, f32[136,128]{1,0:T(8,128)S(1)}, f32[136,128]{1,0:T...) custom-call(f32[32,4,8,128]{3,2,1,0:T(8,128)} %source_ref.1, s32[4,8,128]{2,1,0:T(8,128)} %label_ref.1), custom_call_target="tpu_custom_call" | custom-call | tf_op jit(solution)/shard_map/pack/pallas_call | solution.py:521
  2.2 3.1 %collective-permute-start = (f32[264,128]{1,0:T(8,128)S(1)}, f32[264,128]{1,0:T(8,128)S(1)}, u32[]{:S(2)}, u32[]{:S(2)}) collective-permute-start(f32[264,128]{1,0:T(8,128)S(1)} %get-tuple-element.25), channel_id=1, source_target_pairs={{0,16},{16,0},{1,17},{17,1},{2,18},{18,2},{3,19},{19,3},{4,20},{20... | collective-permute-start | bytes 405512 | tf_op jit(solution)/shard_map/ppermute | solution.py:26
  5.2 1.6 %collective-permute-start.1 = (f32[136,128]{1,0:T(8,128)S(1)}, f32[136,128]{1,0:T(8,128)S(1)}, u32[]{:S(2)}, u32[]{:S(2)}) collective-permute-start(f32[136,128]{1,0:T(8,128)S(1)} %get-tuple-element.26), channel_id=1, source_target_pairs={{0,4},{4,8},{8,12},{12,0},{1,5},{5,9},{9,13},{13,1},{2,6},{6,10},{... | collective-permute-start | bytes 208904 | tf_op jit(solution)/shard_map/ppermute | solution.py:29
  6.8 2.2 %collective-permute-start.2 = (f32[136,128]{1,0:T(8,128)S(1)}, f32[136,128]{1,0:T(8,128)S(1)}, u32[]{:S(2)}, u32[]{:S(2)}) collective-permute-start(f32[136,128]{1,0:T(8,128)S(1)} %get-tuple-element.27), channel_id=1, source_target_pairs={{0,12},{4,0},{8,4},{12,8},{1,13},{5,1},{9,5},{13,9},{2,14},{6,2},{... | collective-permute-start | bytes 208904 | tf_op jit(solution)/shard_map/ppermute | solution.py:29
  9.1 0.0 collective-permute-start.3
  9.1 1.7 %collective-permute-start.4 = (f32[40,128]{1,0:T(8,128)S(1)}, f32[40,128]{1,0:T(8,128)S(1)}, u32[]{:S(2)}, u32[]{:S(2)}) collective-permute-start(f32[40,128]{1,0:T(8,128)S(1)} %get-tuple-element.29), channel_id=1, source_target_pairs={{0,3},{1,0},{2,1},{3,2},{4,7},{5,4},{6,5},{7,6},{8,11},{9,8},{10,9... | collective-permute-start | bytes 61448 | tf_op jit(solution)/shard_map/ppermute | solution.py:29
  10.8 2.0 %prepare.1 = (bf16[256,4096]{1,0:T(8,128)(2,1)S(1)}, bf16[256,128]{1,0:T(8,128)(2,1)S(1)}, f32[32,128]{1,0:T(8,128)S(1)}, f32[6,8,128]{2,1,0:T(8,128)S(1)}) custom-call(s32[1,256]{1,0:T(1,128)} %bitcast.13, s32[1,128]{1,0:T(1,128)} %bitcast.14, f32[32,128]{1,0:T(8,128)} %data_hbm.1, f32[6]{0:T(128)} %table_hbm.1), custom_call_target="tpu_custom_call" | custom-call | tf_op jit(solution)/shard_map/prepare/pallas_call | solution.py:536
  12.8 0.0 collective-permute-done.3.refs_4_
  12.8 0.0 collective-permute-done.4.refs_5_
  12.8 0.0 collective-permute-done.1.refs_2_
  12.8 0.0 collective-permute-done.2.refs_3_
  12.8 0.0 collective-permute-done.refs_0_.refs_1_
  12.9 1.2 %apply.1 = (f32[8,4,8,128]{3,2,1,0:T(8,128)S(1)}, f32[1024,128]{1,0:T(8,128)S(1)}, f32[256,128]{1,0:T(8,128)S(1)}, f32[128,128]{1,0:T(8,128)S(1)}, f32[128,128]{...) custom-call(f32[1024,128]{1,0:T(8,128)S(1)} %get-tuple-element.22.rows_ref, ...), custom_call_target="tpu_custom_call" | custom-call | tf_op jit(solution)/shard_map/apply/pallas_call | solution.py:562
  14.0 0.4 collective-permute-start.5
  14.4 0.2 collective-permute-start.6
  14.5 3.7 %collective-permute-start.7 = (f32[128,128]{1,0:T(8,128)S(1)}, f32[128,128]{1,0:T(8,128)S(1)}, u32[]{:S(2)}, u32[]{:S(2)}) collective-permute-start(f32[128,128]{1,0:T(8,128)S(1)} %get-tuple-element.36), channel_id=1, source_target_pairs={{0,12},{4,0},{8,4},{12,8},{1,13},{5,1},{9,5},{13,9},{2,14},{6,2},{... | collective-permute-start | bytes 196616 | tf_op jit(solution)/shard_map/ppermute | solution.py:29
  18.2 0.4 collective-permute-start.8
  18.6 1.3 %collective-permute-start.9 = (f32[32,128]{1,0:T(8,128)S(1)}, f32[32,128]{1,0:T(8,128)S(1)}, u32[]{:S(2)}, u32[]{:S(2)}) collective-permute-start(f32[32,128]{1,0:T(8,128)S(1)} %get-tuple-element.38), channel_id=1, source_target_pairs={{0,3},{1,0},{2,1},{3,2},{4,7},{5,4},{6,5},{7,6},{8,11},{9,8},{10,9... | collective-permute-start | bytes 49160 | tf_op jit(solution)/shard_map/ppermute | solution.py:29
  20.0 1.8 %source_columns.1 = (f32[256,96]{1,0:T(8,128)S(1)}, f32[128,128]{1,0:T(8,128)S(1)}) custom-call(f32[1024,128]{1,0:T(8,128)S(1)} %get-tuple-element.22.rows_ref, f32[1024,128]{1,0:T(8,128)S(1)} %get-tuple-element.30.applied_ref, f32[8,4,8,128]{3,2,1,0:T(8,128)S(1)} %get-tuple-element.31.weight_ref, bf16[256,4096]{1,0:T(8,128)(2,1)S(1)} %get-tuple-element.32.chosen_ref, ...), custom_call_target="tpu_custom_call" | custom-call | tf_op jit(solution)/shard_map/source_columns/pallas_call | solution.py:572
  21.8 0.0 collective-permute-done.8.refs_4_
  21.8 0.0 collective-permute-done.9.refs_5_
  21.8 0.0 collective-permute-done.6.refs_2_
  21.8 0.0 collective-permute-done.7.refs_3_
  21.8 0.0 collective-permute-done.5.refs_0_.refs_1_
  21.8 0.6 %moments.1 = f32[8,128]{1,0:T(8,128)S(1)} custom-call(f32[1024,128]{1,0:T(8,128)S(1)} %get-tuple-element.30.applied_ref, f32[8,4,8,128]{3,2,1,0:T(8,128)S(1)} %get-tuple-element.31.weight_ref, f32[128,128]{1,0:T(8,128)S(1)} %get-tuple-element.39.sum_ref, f32[256,128]{1,0:T(8,128)S(1)} %collective-permute-done.5.refs_0_.refs_1_, ...), custom_call_target="tpu_custom_call" | custom-call | tf_op jit(solution)/shard_map/moments/pallas_call | solution.py:580
  22.5 1.3 %collective-permute-start.12 = (f32[8,128]{1,0:T(8,128)S(1)}, f32[8,128]{1,0:T(8,128)S(1)}, u32[]{:S(2)}, u32[]{:S(2)}) collective-permute-start(f32[8,128]{1,0:T(8,128)S(1)} %moments.1), channel_id=1, source_target_pairs={{0,3},{1,0},{2,1},{3,2},{4,7},{5,4},{6,5},{7,6},{8,11},{9,8},{10,9... | collective-permute-start | bytes 12296 | tf_op jit(solution)/shard_map/ppermute | solution.py:588
  23.8 1.7 %collective-permute-start.11 = (f32[8,128]{1,0:T(8,128)S(1)}, f32[8,128]{1,0:T(8,128)S(1)}, u32[]{:S(2)}, u32[]{:S(2)}) collective-permute-start(f32[8,128]{1,0:T(8,128)S(1)} %moments.1), channel_id=1, source_target_pairs={{0,2},{1,3},{2,0},{3,1},{4,6},{5,7},{6,4},{7,5},{8,10},{9,11},{10,... | collective-permute-start | bytes 12296 | tf_op jit(solution)/shard_map/ppermute | solution.py:588
  25.5 0.0 collective-permute-start.10
  25.5 1.5 %applied_columns.1 = f32[256,256]{1,0:T(8,128)S(1)} custom-call(f32[1024,128]{1,0:T(8,128)S(1)} %get-tuple-element.30.applied_ref, f32[8,4,8,128]{3,2,1,0:T(8,128)S(1)} %get-tuple-element.31.weight_ref, bf16[256,4096]{1,0:T(8,128)(2,1)S(1)} %get-tuple-element.32.chosen_ref, f32[256,96]{1,0:T(8,128)S(1)} %get-tuple-element.33.source_column_ref, ...), custom_call_target="tpu_custom_call" | custom-call | tf_op jit(solution)/shard_map/applied_columns/pallas_call | solution.py:591
  27.0 0.0 collective-permute-done.12
  27.0 0.4 collective-permute-done.11
  27.4 1.1 %collective-permute-done.10 = f32[8,128]{1,0:T(8,128)S(1)} collective-permute-done((f32[8,128]{1,0:T(8,128)S(1)}, f32[8,128]{1,0:T(8,128)S(1)}, u32[]{:S(2)}, u32[]{:S(2)}) %collective-permute-start.10) | collective-permute-done | bytes 4128 | tf_op jit(solution)/shard_map/ppermute | solution.py:588
  28.6 0.1 reshape_squeeze.3
  28.6 0.1 pad.4
  28.8 12.7 %all_to_all.5 = f32[8,32,256]{2,1,0:T(8,128)S(1)} all-to-all(f32[8,32,256]{2,1,0:T(8,128)S(1)} %broadcast_add_fusion), channel_id=1, replica_groups=mesh['gx'=2,'gy'=4,'gz'=4] {'gx','gy'}, dimensions={0} | all-to-all | bytes 524288 | tf_op jit(solution)/shard_map/all_to_all | solution.py:604
  41.4 1.3 %owner.1 = (f32[3,128,128]{2,1,0:T(8,128)}, f32[6,128]{1,0:T(8,128)}) custom-call(f32[256,256]{1,0:T(8,128)S(1)} %bitcast.10, bf16[256,128]{1,0:T(8,128)(2,1)S(1)} %get-tuple-element.40.chosen_ref, f32[32,128]{1,0:T(8,128)S(1)} %get-tuple-element.41.data_ref), custom_call_target="tpu_custom_call" | custom-call | tf_op jit(solution)/shard_map/owner/pallas_call | solution.py:605
  (4 shorter events, 0.1 us)
Async XLA Ops:
  2.2 10.7 %collective-permute-start = (f32[264,128]{1,0:T(8,128)S(1)}, f32[264,128]{1,0:T(8,128)S(1)}, u32[]{:S(2)}, u32[]{:S(2)}) collective-permute-start(f32[264,128]{1,0:T(8,128)S(1)} %get-tuple-element.25), channel_id=1, source_target_pairs={{0,16},{16,0},{1,17},{17,1},{2,18},{18,2},{3,19},{19,3},{4,20},{20... | collective-permute-start | bytes 405512 | tf_op jit(solution)/shard_map/ppermute | solution.py:26
  5.2 7.6 %collective-permute-start.1 = (f32[136,128]{1,0:T(8,128)S(1)}, f32[136,128]{1,0:T(8,128)S(1)}, u32[]{:S(2)}, u32[]{:S(2)}) collective-permute-start(f32[136,128]{1,0:T(8,128)S(1)} %get-tuple-element.26), channel_id=1, source_target_pairs={{0,4},{4,8},{8,12},{12,0},{1,5},{5,9},{9,13},{13,1},{2,6},{6,10},{... | collective-permute-start | bytes 208904 | tf_op jit(solution)/shard_map/ppermute | solution.py:29
  6.8 6.0 %collective-permute-start.2 = (f32[136,128]{1,0:T(8,128)S(1)}, f32[136,128]{1,0:T(8,128)S(1)}, u32[]{:S(2)}, u32[]{:S(2)}) collective-permute-start(f32[136,128]{1,0:T(8,128)S(1)} %get-tuple-element.27), channel_id=1, source_target_pairs={{0,12},{4,0},{8,4},{12,8},{1,13},{5,1},{9,5},{13,9},{2,14},{6,2},{... | collective-permute-start | bytes 208904 | tf_op jit(solution)/shard_map/ppermute | solution.py:29
  9.1 3.7 %collective-permute-start.3 = (f32[40,128]{1,0:T(8,128)S(1)}, f32[40,128]{1,0:T(8,128)S(1)}, u32[]{:S(2)}, u32[]{:S(2)}) collective-permute-start(f32[40,128]{1,0:T(8,128)S(1)} %get-tuple-element.28), channel_id=1, source_target_pairs={{0,1},{1,2},{2,3},{3,0},{4,5},{5,6},{6,7},{7,4},{8,9},{9,10},{10,1... | collective-permute-start | bytes 61448 | tf_op jit(solution)/shard_map/ppermute | solution.py:29
  9.1 3.7 %collective-permute-start.4 = (f32[40,128]{1,0:T(8,128)S(1)}, f32[40,128]{1,0:T(8,128)S(1)}, u32[]{:S(2)}, u32[]{:S(2)}) collective-permute-start(f32[40,128]{1,0:T(8,128)S(1)} %get-tuple-element.29), channel_id=1, source_target_pairs={{0,3},{1,0},{2,1},{3,2},{4,7},{5,4},{6,5},{7,6},{8,11},{9,8},{10,9... | collective-permute-start | bytes 61448 | tf_op jit(solution)/shard_map/ppermute | solution.py:29
  14.0 7.8 %collective-permute-start.5 = (f32[256,128]{1,0:T(8,128)S(1)}, f32[256,128]{1,0:T(8,128)S(1)}, u32[]{:S(2)}, u32[]{:S(2)}) collective-permute-start(f32[256,128]{1,0:T(8,128)S(1)} %get-tuple-element.34), channel_id=1, source_target_pairs={{0,16},{16,0},{1,17},{17,1},{2,18},{18,2},{3,19},{19,3},{4,20},{20... | collective-permute-start | bytes 393224 | tf_op jit(solution)/shard_map/ppermute | solution.py:26
  14.4 7.4 %collective-permute-start.6 = (f32[128,128]{1,0:T(8,128)S(1)}, f32[128,128]{1,0:T(8,128)S(1)}, u32[]{:S(2)}, u32[]{:S(2)}) collective-permute-start(f32[128,128]{1,0:T(8,128)S(1)} %get-tuple-element.35), channel_id=1, source_target_pairs={{0,4},{4,8},{8,12},{12,0},{1,5},{5,9},{9,13},{13,1},{2,6},{6,10},{... | collective-permute-start | bytes 196616 | tf_op jit(solution)/shard_map/ppermute | solution.py:29
  14.5 7.3 %collective-permute-start.7 = (f32[128,128]{1,0:T(8,128)S(1)}, f32[128,128]{1,0:T(8,128)S(1)}, u32[]{:S(2)}, u32[]{:S(2)}) collective-permute-start(f32[128,128]{1,0:T(8,128)S(1)} %get-tuple-element.36), channel_id=1, source_target_pairs={{0,12},{4,0},{8,4},{12,8},{1,13},{5,1},{9,5},{13,9},{2,14},{6,2},{... | collective-permute-start | bytes 196616 | tf_op jit(solution)/shard_map/ppermute | solution.py:29
  18.2 3.6 %collective-permute-start.8 = (f32[32,128]{1,0:T(8,128)S(1)}, f32[32,128]{1,0:T(8,128)S(1)}, u32[]{:S(2)}, u32[]{:S(2)}) collective-permute-start(f32[32,128]{1,0:T(8,128)S(1)} %get-tuple-element.37), channel_id=1, source_target_pairs={{0,1},{1,2},{2,3},{3,0},{4,5},{5,6},{6,7},{7,4},{8,9},{9,10},{10,1... | collective-permute-start | bytes 49160 | tf_op jit(solution)/shard_map/ppermute | solution.py:29
  18.6 3.2 %collective-permute-start.9 = (f32[32,128]{1,0:T(8,128)S(1)}, f32[32,128]{1,0:T(8,128)S(1)}, u32[]{:S(2)}, u32[]{:S(2)}) collective-permute-start(f32[32,128]{1,0:T(8,128)S(1)} %get-tuple-element.38), channel_id=1, source_target_pairs={{0,3},{1,0},{2,1},{3,2},{4,7},{5,4},{6,5},{7,6},{8,11},{9,8},{10,9... | collective-permute-start | bytes 49160 | tf_op jit(solution)/shard_map/ppermute | solution.py:29
  22.5 4.5 %collective-permute-start.12 = (f32[8,128]{1,0:T(8,128)S(1)}, f32[8,128]{1,0:T(8,128)S(1)}, u32[]{:S(2)}, u32[]{:S(2)}) collective-permute-start(f32[8,128]{1,0:T(8,128)S(1)} %moments.1), channel_id=1, source_target_pairs={{0,3},{1,0},{2,1},{3,2},{4,7},{5,4},{6,5},{7,6},{8,11},{9,8},{10,9... | collective-permute-start | bytes 12296 | tf_op jit(solution)/shard_map/ppermute | solution.py:588
  23.8 3.6 %collective-permute-start.11 = (f32[8,128]{1,0:T(8,128)S(1)}, f32[8,128]{1,0:T(8,128)S(1)}, u32[]{:S(2)}, u32[]{:S(2)}) collective-permute-start(f32[8,128]{1,0:T(8,128)S(1)} %moments.1), channel_id=1, source_target_pairs={{0,2},{1,3},{2,0},{3,1},{4,6},{5,7},{6,4},{7,5},{8,10},{9,11},{10,... | collective-permute-start | bytes 12296 | tf_op jit(solution)/shard_map/ppermute | solution.py:588
  25.5 3.0 %collective-permute-start.10 = (f32[8,128]{1,0:T(8,128)S(1)}, f32[8,128]{1,0:T(8,128)S(1)}, u32[]{:S(2)}, u32[]{:S(2)}) collective-permute-start(f32[8,128]{1,0:T(8,128)S(1)} %moments.1), channel_id=1, source_target_pairs={{0,1},{1,2},{2,3},{3,0},{4,5},{5,6},{6,7},{7,4},{8,9},{9,10},{10,1... | collective-permute-start | bytes 12296 | tf_op jit(solution)/shard_map/ppermute | solution.py:588

commit v4 on v3

--- a/solution.py
+++ b/solution.py
@@ -131,6 +131,7 @@
 
 def prepare_kernel(
     size_z,
+    folding,
     voxel_hbm,
     owned_hbm,
     data_hbm,
@@ -166,8 +167,18 @@
     lane_index = lax.broadcasted_iota(jnp.int32, (slots, size_z), 1)
     for first in range(0, voxels, size_z):
         chosen_ref[:, first : first + size_z] = one_hot(lane_index == voxel - first)
-    slot_index = lax.broadcasted_iota(jnp.int32, owned_chosen_ref.shape, 0)
-    owned_chosen_ref[...] = one_hot(slot_index == owned_ref[...])
+    row_index = lax.broadcasted_iota(jnp.int32, (slots, owned_ref.shape[1]), 0)
+    owned_chosen_ref[0:slots, :] = one_hot(row_index == owned_ref[...])
+    slots_each, fold = folding
+    if fold:
+        part = slots_each // fold
+        row_index = lax.broadcasted_iota(jnp.int32, (slots // fold, owned_ref.shape[1]), 0)
+        slot_index = row_index // part * slots_each + row_index % part
+        for k in range(fold):
+            first = slots + k * (slots // fold)
+            owned_chosen_ref[first : first + slots // fold, :] = one_hot(
+                slot_index + k * part == owned_ref[...]
+            )
 
 
 def one_hot(condition):
@@ -396,32 +407,63 @@
     )
 
 
-def applied_kernel(dims, applied_ref, weight_ref, chosen_ref, source_column_ref, *refs):
+def payload_rows(sensors, slots_each):
+    whole, rest = divmod(6 * sensors, lane_tile)
+    fold = lane_tile // rest if rest else 0
+    assert not fold or (fold * rest == lane_tile and slots_each % fold == 0)
+    rows = whole * slots_each + (slots_each // fold if fold else 0)
+    return whole, rest, fold, rows, -(-4 * sensors // lane_tile)
+
+
+def applied_kernel(dims, slots_each, applied_ref, weight_ref, chosen_ref, source_column_ref, *refs):
     sensors = dims[0]
     column_ref, high_ref, low_ref = refs[6:]
-    half = column_ref.shape[1] // 2
-    column_ref[...] = jnp.zeros_like(column_ref)
-    column_ref[:, 0 : 3 * sensors] = source_column_ref[...]
-    column_ref[:, half : half + 3 * sensors] = select_columns(
+    applied_columns = select_columns(
         dims, applied_ref, weight_ref, pair_up(refs[:6]), chosen_ref, high_ref, low_ref
     )
+    columns = jnp.concatenate([source_column_ref[...], applied_columns], axis=1)
+    whole, rest, fold, rows, moment_rows = payload_rows(sensors, slots_each)
+    for owner in range(columns.shape[0] // slots_each):
+        mine = slice(owner * slots_each, (owner + 1) * slots_each)
+        at = owner * (rows + moment_rows)
+        for tile in range(whole):
+            column_ref[at : at + slots_each, :] = columns[mine, tile * lane_tile : (tile + 1) * lane_tile]
+            at += slots_each
+        if fold:
+            part = slots_each // fold
+            others = columns[mine, whole * lane_tile :]
+            column_ref[at : at + part, :] = jnp.concatenate(
+                [others[k * part : (k + 1) * part, :] for k in range(fold)], axis=1
+            )
+            at += part
+        column_ref[at : at + moment_rows, :] = jnp.zeros((moment_rows, lane_tile), jnp.float32)
 
 
 def owner_kernel(sensors, slots_each, received_ref, chosen_ref, data_ref, projection_ref, gram_ref):
-    total, width = received_ref.shape
-    half = width // 2
-    gathered = [jnp.zeros((2, sensors), jnp.float32) for _ in range(2)]
-    for first in range(0, total, slots_each):
-        for k in range(2):
-            start = k * half + 3 * sensors
-            gathered[k] = gathered[k] + received_ref[first : first + 2, start : start + sensors]
+    whole, rest, fold, rows, moment_rows = payload_rows(sensors, slots_each)
+    each = rows + moment_rows
+    sources = received_ref.shape[0] // each
+    slots = sources * slots_each
+
+    def collected(start, count):
+        return jnp.concatenate(
+            [received_ref[k * each + start : k * each + start + count, :] for k in range(sources)],
+            axis=0,
+        )
+
+    gathered = jnp.zeros((moment_rows, lane_tile), jnp.float32)
+    for k in range(sources):
+        gathered = gathered + received_ref[k * each + rows : (k + 1) * each, :]
     moments = []
-    sensor_index = lax.broadcasted_iota(jnp.int32, (sensors, sensors), 0)
-    lane_index = lax.broadcasted_iota(jnp.int32, (sensors, sensors), 1)
+    sensor_index = lax.broadcasted_iota(jnp.int32, (sensors, lane_tile), 0)
+    lane_index = lax.broadcasted_iota(jnp.int32, (sensors, lane_tile), 1)
     for k in range(4):
-        row = gathered[k % 2][k // 2 : k // 2 + 1, :]
-        picked = jnp.where(lane_index == sensor_index, row, 0.0)
-        moments.append(jnp.sum(picked, axis=1, keepdims=True))
+        total = jnp.zeros((sensors, 1), jnp.float32)
+        for row in range(moment_rows):
+            here = lane_index + row * lane_tile == sensor_index + k * sensors
+            picked = jnp.where(here, gathered[row : row + 1, :], 0.0)
+            total = total + jnp.sum(picked, axis=1, keepdims=True)
+        moments.append(total)
     moment_zero, moment_one, moment_two, moment_three = moments
     first_step = moment_zero / moment_one
     residue = first_step * first_step * moment_two - moment_zero
@@ -434,18 +476,30 @@
     second_step = residue / curvature
     source_coef = first_step + second_step * growth
     applied_coef = second_step * first_step
-    chosen = chosen_ref[...]
     contract = (((0,), (0,)), ((), ()))
-    owned = []
-    for start in (0, half):
-        high, low = halves(received_ref[:, start : start + half])
-        owned.append(
-            lax.dot_general(high, chosen, contract, preferred_element_type=jnp.float32)
-            + lax.dot_general(low, chosen, contract, preferred_element_type=jnp.float32)
-        )
+
+    def selected(values, first):
+        chosen = chosen_ref[first : first + values.shape[0], :]
+        high, low = halves(values)
+        return lax.dot_general(
+            high, chosen, contract, preferred_element_type=jnp.float32
+        ) + lax.dot_general(low, chosen, contract, preferred_element_type=jnp.float32)
+
+    owned = [
+        selected(collected(tile * slots_each, slots_each), 0) for tile in range(whole)
+    ]
+    if fold:
+        folded = collected(whole * slots_each, slots_each // fold)
+        others = jnp.zeros((rest, chosen_ref.shape[1]), jnp.float32)
+        for k in range(fold):
+            found = selected(folded, slots + k * (slots // fold))
+            others = others + found[k * rest : (k + 1) * rest, :]
+        owned.append(others)
+    owned = jnp.concatenate(owned, axis=0)
     lead = []
     for c in range(3):
-        source_part, applied_part = (part[c * sensors : (c + 1) * sensors, :] for part in owned)
+        source_part = owned[c * sensors : (c + 1) * sensors, :]
+        applied_part = owned[(3 + c) * sensors : (4 + c) * sensors, :]
         lead.append(source_coef * source_part - applied_coef * applied_part)
         projection_ref[c] = lax.dot_general(
             data_ref[...],
@@ -506,6 +560,7 @@
     owners = lax.axis_size("gx") * lax.axis_size("gy")
     slots = send_map.size
     slots_each = slots // owners
+    _, _, fold, payload, moment_rows = payload_rows(sensors, slots_each)
     times = sensor_data.shape[1]
     positions = owner_slots.shape[0]
 
@@ -534,10 +589,10 @@
     source_halos = exchange_all(faces, counts)
     levels = conductivity_table.shape[0]
     chosen, owned_chosen, data, table = call(
-        functools.partial(prepare_kernel, size_z),
+        functools.partial(prepare_kernel, size_z, (slots_each, fold)),
         out_shape=[
             array((slots, voxels), jnp.bfloat16),
-            array((slots, positions), jnp.bfloat16),
+            array((slots * (2 if fold else 1), positions), jnp.bfloat16),
             array(sensor_data.shape),
             array((levels, size_y, size_z)),
         ],
@@ -585,23 +640,24 @@
         name="moments",
     )(applied, weight, sums, *applied_halos)
     depth = lax.axis_size("gz")
-    moment = moment + sum(lax.ppermute(moment, "gz", ring(depth, d)) for d in range(1, depth))
-
-    half = -(-4 * sensors // lane_tile) * lane_tile
+    moment = moment + sum(lax.ppermute(moment, "gz", ring(depth, d)) for d in range(depth - 1, 0, -1))
+
+    each = payload + moment_rows
     columns = call(
-        functools.partial(applied_kernel, dims),
-        out_shape=array((slots, 2 * half)),
+        functools.partial(applied_kernel, dims, slots_each),
+        out_shape=array((owners * each, lane_tile)),
         in_specs=in_vmem(10),
         out_specs=in_vmem(1)[0],
         scratch_shapes=halves_scratch(3 * sensors),
         name="applied_columns",
     )(applied, weight, chosen, source_columns, *applied_halos)
-    stamp = jnp.pad(
-        moment[0].reshape(1, 2, 2, sensors),
-        ((0, 0), (0, slots_each - 2), (0, 0), (3 * sensors, half - 4 * sensors)),
-    ).reshape(1, slots_each, 2 * half)
-    outgoing = columns.reshape(owners, slots_each, 2 * half) + stamp
-    received = lax.all_to_all(outgoing, ("gx", "gy"), 0, 0, tiled=True).reshape(slots, 2 * half)
+    place = lax.broadcasted_iota(jnp.int32, columns.shape, 0) % each
+    stamp = jnp.pad(moment[0], (0, moment_rows * lane_tile - 4 * sensors)).reshape(-1, lane_tile)
+    for row in range(moment_rows):
+        columns = jnp.where(place == payload + row, stamp[row : row + 1], columns)
+    received = lax.all_to_all(
+        columns.reshape(owners, 1, each * lane_tile), ("gx", "gy"), 0, 0, tiled=True
+    ).reshape(columns.shape)
     return call(
         functools.partial(owner_kernel, sensors, slots_each),
         out_shape=[array((3, times, positions)), array((6, positions))],

time: 43 us -> 41.9 us (0.974)
  blocking collectives: 12.7 us -> 11.6 us
    all_to_all x1, blocking collectives: 12.7 us -> 11.6 us  [per_device(): lax.all_to_all(columns.reshape(owners, 1, each * lane_tile), ('gx', 'gy')...]
  transfers between devices with their start and end apart: 13 -> 13, of which waited for: 2 -> 2; matrix products, arithmetic and copies ran while one was open for 0% -> 0% of each run, Pallas kernels for 12% -> 13%
where the time goes in v4:
time: 41.9 us; the launch traced here: 41.7 us
  starting transfers between devices  17.6 us (42%)
  blocking collectives  11.6 us (28%)
  Pallas kernels  10 us (24%)
  waiting for transfers between devices  1.41 us (3%)
  between operations  0.76 us (2%)
    all_to_all x1, blocking collectives, per_device(): lax.all_to_all(columns.reshape(owners, 1, each * lane_tile), ('gx', 'gy')...  11.6 us
    ppermute x4, starting transfers between devices, exchange(): lax.ppermute(low, axis, ring(count, -1))  9.04 us
    ppermute x2, starting transfers between devices, exchange(): swapped = lax.ppermute(faces[0], axis, ring(2, 1))  3.41 us
    ppermute x3, starting transfers between devices, per_device(): lax.ppermute(moment, 'gz', ring(depth, d))  3.02 us
    ppermute x4, starting transfers between devices, exchange(): lax.ppermute(high, axis, ring(count, 1))  2.1 us
    pallas_call x1, Pallas kernels, per_device(): call(functools.partial(prepare_kernel, size_z, (slots_each, fold)), out_s...  2.01 us
    pallas_call x1, Pallas kernels, per_device(): call(functools.partial(source_kernel, dims), out_shape=[array((slots, 3 *...  1.83 us
    pallas_call x1, Pallas kernels, per_device(): call(functools.partial(applied_kernel, dims, slots_each), out_shape=array...  1.63 us
  transfers between devices with their start and end apart: 13, of which 2 were waited for; matrix products, arithmetic and copies ran while one was open for 0% of the time, Pallas kernels for 13%

profile of v4, /device:TPU:0, one launch (start us, length us, event | category | flops | bytes accessed | tf_op | source)
XLA Modules:
  0.0 41.7 jit_solution(12389985447953986199)
XLA Ops:
  0.6 1.5 %pack.1 = (f32[1024,128]{1,0:T(8,128)S(1)}, f32[4,8,128]{2,1,0:T(8,128)S(1)}, f32[264,128]{1,0:T(8,128)S(1)}, f32[136,128]{1,0:T(8,128)S(1)}, f32[136,128]{1,0:T...) custom-call(f32[32,4,8,128]{3,2,1,0:T(8,128)} %source_ref.1, s32[4,8,128]{2,1,0:T(8,128)} %label_ref.1), custom_call_target="tpu_custom_call" | custom-call | tf_op jit(solution)/shard_map/pack/pallas_call | solution.py:576
  2.2 3.1 %collective-permute-start = (f32[264,128]{1,0:T(8,128)S(1)}, f32[264,128]{1,0:T(8,128)S(1)}, u32[]{:S(2)}, u32[]{:S(2)}) collective-permute-start(f32[264,128]{1,0:T(8,128)S(1)} %get-tuple-element.25), channel_id=1, source_target_pairs={{0,16},{16,0},{1,17},{17,1},{2,18},{18,2},{3,19},{19,3},{4,20},{20... | collective-permute-start | bytes 405512 | tf_op jit(solution)/shard_map/ppermute | solution.py:26
  5.2 1.6 %collective-permute-start.1 = (f32[136,128]{1,0:T(8,128)S(1)}, f32[136,128]{1,0:T(8,128)S(1)}, u32[]{:S(2)}, u32[]{:S(2)}) collective-permute-start(f32[136,128]{1,0:T(8,128)S(1)} %get-tuple-element.26), channel_id=1, source_target_pairs={{0,4},{4,8},{8,12},{12,0},{1,5},{5,9},{9,13},{13,1},{2,6},{6,10},{... | collective-permute-start | bytes 208904 | tf_op jit(solution)/shard_map/ppermute | solution.py:29
  6.8 2.2 %collective-permute-start.2 = (f32[136,128]{1,0:T(8,128)S(1)}, f32[136,128]{1,0:T(8,128)S(1)}, u32[]{:S(2)}, u32[]{:S(2)}) collective-permute-start(f32[136,128]{1,0:T(8,128)S(1)} %get-tuple-element.27), channel_id=1, source_target_pairs={{0,12},{4,0},{8,4},{12,8},{1,13},{5,1},{9,5},{13,9},{2,14},{6,2},{... | collective-permute-start | bytes 208904 | tf_op jit(solution)/shard_map/ppermute | solution.py:29
  9.1 0.0 collective-permute-start.3
  9.1 1.7 %collective-permute-start.4 = (f32[40,128]{1,0:T(8,128)S(1)}, f32[40,128]{1,0:T(8,128)S(1)}, u32[]{:S(2)}, u32[]{:S(2)}) collective-permute-start(f32[40,128]{1,0:T(8,128)S(1)} %get-tuple-element.29), channel_id=1, source_target_pairs={{0,3},{1,0},{2,1},{3,2},{4,7},{5,4},{6,5},{7,6},{8,11},{9,8},{10,9... | collective-permute-start | bytes 61448 | tf_op jit(solution)/shard_map/ppermute | solution.py:29
  10.8 2.0 %prepare.1 = (bf16[256,4096]{1,0:T(8,128)(2,1)S(1)}, bf16[512,128]{1,0:T(8,128)(2,1)S(1)}, f32[32,128]{1,0:T(8,128)S(1)}, f32[6,8,128]{2,1,0:T(8,128)S(1)}) custom-call(s32[1,256]{1,0:T(1,128)} %bitcast.8, s32[1,128]{1,0:T(1,128)} %bitcast.9, f32[32,128]{1,0:T(8,128)} %data_hbm.1, f32[6]{0:T(128)} %table_hbm.1), custom_call_target="tpu_custom_call" | custom-call | tf_op jit(solution)/shard_map/prepare/pallas_call | solution.py:591
  12.8 0.0 collective-permute-done.3.refs_4_
  12.8 0.0 collective-permute-done.4.refs_5_
  12.8 0.0 collective-permute-done.1.refs_2_
  12.9 0.0 collective-permute-done.2.refs_3_
  12.9 0.0 collective-permute-done.refs_0_.refs_1_
  12.9 1.2 %apply.1 = (f32[8,4,8,128]{3,2,1,0:T(8,128)S(1)}, f32[1024,128]{1,0:T(8,128)S(1)}, f32[256,128]{1,0:T(8,128)S(1)}, f32[128,128]{1,0:T(8,128)S(1)}, f32[128,128]{...) custom-call(f32[1024,128]{1,0:T(8,128)S(1)} %get-tuple-element.22.rows_ref, ...), custom_call_target="tpu_custom_call" | custom-call | tf_op jit(solution)/shard_map/apply/pallas_call | solution.py:617
  14.1 0.4 collective-permute-start.5
  14.4 0.1 collective-permute-start.6
  14.5 3.7 %collective-permute-start.7 = (f32[128,128]{1,0:T(8,128)S(1)}, f32[128,128]{1,0:T(8,128)S(1)}, u32[]{:S(2)}, u32[]{:S(2)}) collective-permute-start(f32[128,128]{1,0:T(8,128)S(1)} %get-tuple-element.36), channel_id=1, source_target_pairs={{0,12},{4,0},{8,4},{12,8},{1,13},{5,1},{9,5},{13,9},{2,14},{6,2},{... | collective-permute-start | bytes 196616 | tf_op jit(solution)/shard_map/ppermute | solution.py:29
  18.2 0.4 collective-permute-start.8
  18.6 1.4 %collective-permute-start.9 = (f32[32,128]{1,0:T(8,128)S(1)}, f32[32,128]{1,0:T(8,128)S(1)}, u32[]{:S(2)}, u32[]{:S(2)}) collective-permute-start(f32[32,128]{1,0:T(8,128)S(1)} %get-tuple-element.38), channel_id=1, source_target_pairs={{0,3},{1,0},{2,1},{3,2},{4,7},{5,4},{6,5},{7,6},{8,11},{9,8},{10,9... | collective-permute-start | bytes 49160 | tf_op jit(solution)/shard_map/ppermute | solution.py:29
  20.0 1.8 %source_columns.1 = (f32[256,96]{1,0:T(8,128)S(1)}, f32[128,128]{1,0:T(8,128)S(1)}) custom-call(f32[1024,128]{1,0:T(8,128)S(1)} %get-tuple-element.22.rows_ref, f32[1024,128]{1,0:T(8,128)S(1)} %get-tuple-element.30.applied_ref, f32[8,4,8,128]{3,2,1,0:T(8,128)S(1)} %get-tuple-element.31.weight_ref, bf16[256,4096]{1,0:T(8,128)(2,1)S(1)} %get-tuple-element.32.chosen_ref, ...), custom_call_target="tpu_custom_call" | custom-call | tf_op jit(solution)/shard_map/source_columns/pallas_call | solution.py:627
  21.8 0.0 collective-permute-done.8.refs_4_
  21.8 0.0 collective-permute-done.9.refs_5_
  21.9 0.0 collective-permute-done.6.refs_2_
  21.9 0.0 collective-permute-done.7.refs_3_
  21.9 0.0 collective-permute-done.5.refs_0_.refs_1_
  21.9 0.6 %moments.1 = f32[8,128]{1,0:T(8,128)S(1)} custom-call(f32[1024,128]{1,0:T(8,128)S(1)} %get-tuple-element.30.applied_ref, f32[8,4,8,128]{3,2,1,0:T(8,128)S(1)} %get-tuple-element.31.weight_ref, f32[128,128]{1,0:T(8,128)S(1)} %get-tuple-element.33.sum_ref, f32[256,128]{1,0:T(8,128)S(1)} %collective-permute-done.5.refs_0_.refs_1_, ...), custom_call_target="tpu_custom_call" | custom-call | tf_op jit(solution)/shard_map/moments/pallas_call | solution.py:635
  22.5 1.3 %collective-permute-start.10 = (f32[8,128]{1,0:T(8,128)S(1)}, f32[8,128]{1,0:T(8,128)S(1)}, u32[]{:S(2)}, u32[]{:S(2)}) collective-permute-start(f32[8,128]{1,0:T(8,128)S(1)} %moments.1), channel_id=1, source_target_pairs={{0,3},{1,0},{2,1},{3,2},{4,7},{5,4},{6,5},{7,6},{8,11},{9,8},{10,9... | collective-permute-start | bytes 12296 | tf_op jit(solution)/shard_map/ppermute | solution.py:643
  23.8 1.7 %collective-permute-start.11 = (f32[8,128]{1,0:T(8,128)S(1)}, f32[8,128]{1,0:T(8,128)S(1)}, u32[]{:S(2)}, u32[]{:S(2)}) collective-permute-start(f32[8,128]{1,0:T(8,128)S(1)} %moments.1), channel_id=1, source_target_pairs={{0,2},{1,3},{2,0},{3,1},{4,6},{5,7},{6,4},{7,5},{8,10},{9,11},{10,... | collective-permute-start | bytes 12296 | tf_op jit(solution)/shard_map/ppermute | solution.py:643
  25.5 0.0 collective-permute-start.12
  25.5 1.6 %applied_columns.1 = f32[392,128]{1,0:T(8,128)S(1)} custom-call(f32[1024,128]{1,0:T(8,128)S(1)} %get-tuple-element.30.applied_ref, f32[8,4,8,128]{3,2,1,0:T(8,128)S(1)} %get-tuple-element.31.weight_ref, bf16[256,4096]{1,0:T(8,128)(2,1)S(1)} %get-tuple-element.32.chosen_ref, f32[256,96]{1,0:T(8,128)S(1)} %get-tuple-element.39.source_column_ref, ...), custom_call_target="tpu_custom_call" | custom-call | tf_op jit(solution)/shard_map/applied_columns/pallas_call | solution.py:646
  27.2 0.0 collective-permute-done.10
  27.2 0.2 collective-permute-done.11
  27.4 1.1 %collective-permute-done.12 = f32[8,128]{1,0:T(8,128)S(1)} collective-permute-done((f32[8,128]{1,0:T(8,128)S(1)}, f32[8,128]{1,0:T(8,128)S(1)}, u32[]{:S(2)}, u32[]{:S(2)}) %collective-permute-start.12) | collective-permute-done | bytes 4128 | tf_op jit(solution)/shard_map/ppermute | solution.py:643
  28.6 0.2 fusion
  28.8 11.6 %all_to_all.5 = f32[8,1,6272]{2,1,0:T(1,128)S(1)} all-to-all(f32[8,1,6272]{2,1,0:T(1,128)S(1)} %bitcast.7), channel_id=1, replica_groups=mesh['gx'=2,'gy'=4,'gz'=4] {'gx','gy'}, dimensions={0} | all-to-all | bytes 401408 | tf_op jit(solution)/shard_map/all_to_all | solution.py:658
  40.4 1.2 %owner.1 = (f32[3,128,128]{2,1,0:T(8,128)}, f32[6,128]{1,0:T(8,128)}) custom-call(f32[392,128]{1,0:T(8,128)S(1)} %bitcast.6, bf16[512,128]{1,0:T(8,128)(2,1)S(1)} %get-tuple-element.40.chosen_ref, f32[32,128]{1,0:T(8,128)S(1)} %get-tuple-element.41.data_ref), custom_call_target="tpu_custom_call" | custom-call | tf_op jit(solution)/shard_map/owner/pallas_call | solution.py:661
  (4 shorter events, 0.0 us)
Async XLA Ops:
  2.2 10.7 %collective-permute-start = (f32[264,128]{1,0:T(8,128)S(1)}, f32[264,128]{1,0:T(8,128)S(1)}, u32[]{:S(2)}, u32[]{:S(2)}) collective-permute-start(f32[264,128]{1,0:T(8,128)S(1)} %get-tuple-element.25), channel_id=1, source_target_pairs={{0,16},{16,0},{1,17},{17,1},{2,18},{18,2},{3,19},{19,3},{4,20},{20... | collective-permute-start | bytes 405512 | tf_op jit(solution)/shard_map/ppermute | solution.py:26
  5.2 7.6 %collective-permute-start.1 = (f32[136,128]{1,0:T(8,128)S(1)}, f32[136,128]{1,0:T(8,128)S(1)}, u32[]{:S(2)}, u32[]{:S(2)}) collective-permute-start(f32[136,128]{1,0:T(8,128)S(1)} %get-tuple-element.26), channel_id=1, source_target_pairs={{0,4},{4,8},{8,12},{12,0},{1,5},{5,9},{9,13},{13,1},{2,6},{6,10},{... | collective-permute-start | bytes 208904 | tf_op jit(solution)/shard_map/ppermute | solution.py:29
  6.8 6.0 %collective-permute-start.2 = (f32[136,128]{1,0:T(8,128)S(1)}, f32[136,128]{1,0:T(8,128)S(1)}, u32[]{:S(2)}, u32[]{:S(2)}) collective-permute-start(f32[136,128]{1,0:T(8,128)S(1)} %get-tuple-element.27), channel_id=1, source_target_pairs={{0,12},{4,0},{8,4},{12,8},{1,13},{5,1},{9,5},{13,9},{2,14},{6,2},{... | collective-permute-start | bytes 208904 | tf_op jit(solution)/shard_map/ppermute | solution.py:29
  9.1 3.8 %collective-permute-start.3 = (f32[40,128]{1,0:T(8,128)S(1)}, f32[40,128]{1,0:T(8,128)S(1)}, u32[]{:S(2)}, u32[]{:S(2)}) collective-permute-start(f32[40,128]{1,0:T(8,128)S(1)} %get-tuple-element.28), channel_id=1, source_target_pairs={{0,1},{1,2},{2,3},{3,0},{4,5},{5,6},{6,7},{7,4},{8,9},{9,10},{10,1... | collective-permute-start | bytes 61448 | tf_op jit(solution)/shard_map/ppermute | solution.py:29
  9.1 3.8 %collective-permute-start.4 = (f32[40,128]{1,0:T(8,128)S(1)}, f32[40,128]{1,0:T(8,128)S(1)}, u32[]{:S(2)}, u32[]{:S(2)}) collective-permute-start(f32[40,128]{1,0:T(8,128)S(1)} %get-tuple-element.29), channel_id=1, source_target_pairs={{0,3},{1,0},{2,1},{3,2},{4,7},{5,4},{6,5},{7,6},{8,11},{9,8},{10,9... | collective-permute-start | bytes 61448 | tf_op jit(solution)/shard_map/ppermute | solution.py:29
  14.1 7.8 %collective-permute-start.5 = (f32[256,128]{1,0:T(8,128)S(1)}, f32[256,128]{1,0:T(8,128)S(1)}, u32[]{:S(2)}, u32[]{:S(2)}) collective-permute-start(f32[256,128]{1,0:T(8,128)S(1)} %get-tuple-element.34), channel_id=1, source_target_pairs={{0,16},{16,0},{1,17},{17,1},{2,18},{18,2},{3,19},{19,3},{4,20},{20... | collective-permute-start | bytes 393224 | tf_op jit(solution)/shard_map/ppermute | solution.py:26
  14.4 7.4 %collective-permute-start.6 = (f32[128,128]{1,0:T(8,128)S(1)}, f32[128,128]{1,0:T(8,128)S(1)}, u32[]{:S(2)}, u32[]{:S(2)}) collective-permute-start(f32[128,128]{1,0:T(8,128)S(1)} %get-tuple-element.35), channel_id=1, source_target_pairs={{0,4},{4,8},{8,12},{12,0},{1,5},{5,9},{9,13},{13,1},{2,6},{6,10},{... | collective-permute-start | bytes 196616 | tf_op jit(solution)/shard_map/ppermute | solution.py:29
  14.5 7.3 %collective-permute-start.7 = (f32[128,128]{1,0:T(8,128)S(1)}, f32[128,128]{1,0:T(8,128)S(1)}, u32[]{:S(2)}, u32[]{:S(2)}) collective-permute-start(f32[128,128]{1,0:T(8,128)S(1)} %get-tuple-element.36), channel_id=1, source_target_pairs={{0,12},{4,0},{8,4},{12,8},{1,13},{5,1},{9,5},{13,9},{2,14},{6,2},{... | collective-permute-start | bytes 196616 | tf_op jit(solution)/shard_map/ppermute | solution.py:29
  18.2 3.6 %collective-permute-start.8 = (f32[32,128]{1,0:T(8,128)S(1)}, f32[32,128]{1,0:T(8,128)S(1)}, u32[]{:S(2)}, u32[]{:S(2)}) collective-permute-start(f32[32,128]{1,0:T(8,128)S(1)} %get-tuple-element.37), channel_id=1, source_target_pairs={{0,1},{1,2},{2,3},{3,0},{4,5},{5,6},{6,7},{7,4},{8,9},{9,10},{10,1... | collective-permute-start | bytes 49160 | tf_op jit(solution)/shard_map/ppermute | solution.py:29
  18.6 3.2 %collective-permute-start.9 = (f32[32,128]{1,0:T(8,128)S(1)}, f32[32,128]{1,0:T(8,128)S(1)}, u32[]{:S(2)}, u32[]{:S(2)}) collective-permute-start(f32[32,128]{1,0:T(8,128)S(1)} %get-tuple-element.38), channel_id=1, source_target_pairs={{0,3},{1,0},{2,1},{3,2},{4,7},{5,4},{6,5},{7,6},{8,11},{9,8},{10,9... | collective-permute-start | bytes 49160 | tf_op jit(solution)/shard_map/ppermute | solution.py:29
  22.5 4.7 %collective-permute-start.10 = (f32[8,128]{1,0:T(8,128)S(1)}, f32[8,128]{1,0:T(8,128)S(1)}, u32[]{:S(2)}, u32[]{:S(2)}) collective-permute-start(f32[8,128]{1,0:T(8,128)S(1)} %moments.1), channel_id=1, source_target_pairs={{0,3},{1,0},{2,1},{3,2},{4,7},{5,4},{6,5},{7,6},{8,11},{9,8},{10,9... | collective-permute-start | bytes 12296 | tf_op jit(solution)/shard_map/ppermute | solution.py:643
  23.8 3.6 %collective-permute-start.11 = (f32[8,128]{1,0:T(8,128)S(1)}, f32[8,128]{1,0:T(8,128)S(1)}, u32[]{:S(2)}, u32[]{:S(2)}) collective-permute-start(f32[8,128]{1,0:T(8,128)S(1)} %moments.1), channel_id=1, source_target_pairs={{0,2},{1,3},{2,0},{3,1},{4,6},{5,7},{6,4},{7,5},{8,10},{9,11},{10,... | collective-permute-start | bytes 12296 | tf_op jit(solution)/shard_map/ppermute | solution.py:643
  25.5 3.0 %collective-permute-start.12 = (f32[8,128]{1,0:T(8,128)S(1)}, f32[8,128]{1,0:T(8,128)S(1)}, u32[]{:S(2)}, u32[]{:S(2)}) collective-permute-start(f32[8,128]{1,0:T(8,128)S(1)} %moments.1), channel_id=1, source_target_pairs={{0,1},{1,2},{2,3},{3,0},{4,5},{5,6},{6,7},{7,4},{8,9},{9,10},{10,1... | collective-permute-start | bytes 12296 | tf_op jit(solution)/shard_map/ppermute | solution.py:643

commit v5 on v4

--- a/solution.py
+++ b/solution.py
@@ -9,28 +9,73 @@
 
 mass_term = 0.25
 lane_tile = 128
+axes = ("gx", "gy", "gz")
 vmem_grant = 16 << 20
 last_with_last = (((1,), (1,)), ((), ()))
 entry_pairs = ((0, 0), (1, 1), (2, 2), (0, 1), (0, 2), (1, 2))
 
 
-def ring(count, step):
-    return [(i, (i + step) % count) for i in range(count)]
-
-
-def exchange(faces, axis):
+def swap(value, axis, odd):
+    count, beside = lax.axis_size(axis), lax.axis_size("gz")
+    partner = {}
+    for first in range(odd, count - 1, 2):
+        partner[first], partner[first + 1] = first + 1, first
+    alone = [i for i in range(count) if i not in partner]
+    if alone and axis != "gz" and beside % 2 == 0:
+        table = [
+            (i * beside + k, partner[i] * beside + k if i in partner else i * beside + (k ^ 1))
+            for i in range(count)
+            for k in range(beside)
+        ]
+        return lax.ppermute(value, (axis, "gz"), table)
+    for source, target in zip(alone, alone[::-1]):
+        partner[source] = target
+    return lax.ppermute(value, axis, sorted(partner.items()))
+
+
+def sum_over(value, axis):
     count = lax.axis_size(axis)
-    if count == 1:
-        return faces[0], faces[1]
-    if count == 2:
-        swapped = lax.ppermute(faces[0], axis, ring(2, 1))
-        return swapped, swapped
-    low, high = faces
-    return lax.ppermute(high, axis, ring(count, 1)), lax.ppermute(low, axis, ring(count, -1))
-
-
-def faces_per_axis(count):
-    return 1 if count == 2 else 2
+    if count & (count - 1) == 0:
+        tables = [[(i, i ^ d) for i in range(count)] for d in range(count - 1, 0, -1)]
+    else:
+        tables = [[(i, (i + d) % count) for i in range(count)] for d in range(count - 1, 0, -1)]
+    return value + sum(lax.ppermute(value, axis, table) for table in tables)
+
+
+def face_counts():
+    return [1 if lax.axis_size(axis) <= 2 else 2 for axis in axes]
+
+
+def exchange_all(faces, counts):
+    halos = []
+    for axis, group in zip(axes, split_refs(faces, counts)):
+        if lax.axis_size(axis) > 1:
+            group = [swap(face, axis, odd) for odd, face in enumerate(group)]
+        halos.extend(group)
+    return halos
+
+
+def sort_halos(halo_refs, held_refs, counts):
+    sorted_refs, held_refs = [], list(held_refs)
+    for axis, group in zip(axes, split_refs(halo_refs, counts)):
+        if len(group) == 1:
+            sorted_refs.append((group[0], group[0]))
+            continue
+        even = lax.axis_index(axis) % 2 == 0
+        below, above = held_refs.pop(0), held_refs.pop(0)
+        first, second = group[0][...], group[1][...]
+        below[...] = jnp.where(even, second, first)
+        above[...] = jnp.where(even, first, second)
+        sorted_refs.append((below, above))
+    return sorted_refs
+
+
+def held_halos(faces, counts):
+    return [
+        pltpu.VMEM(face.shape, face.dtype)
+        for group in split_refs(faces, counts)
+        for face in (group if len(group) == 2 else [])
+    ]
 
 
 def lanes_equal(shape, value):
@@ -39,62 +84,54 @@
 
 def neighbour_flags():
     flags = []
-    for axis in ("gx", "gy", "gz"):
+    for axis in axes:
         index = lax.axis_index(axis)
         flags.append((index > 0, index < lax.axis_size(axis) - 1))
     return flags
 
 
-def write_faces(dims, field, face_refs, extra=None):
+def write_faces(dims, rows_ref, face_refs, extra=None):
     sensors, size_x, size_y, size_z = dims
     x_refs, y_refs, z_refs = face_refs
 
-    def put(refs, axis, write):
-        if len(refs) == 2:
-            write(refs[0], 0)
-            write(refs[1], 1)
-            return
-        index = lax.axis_index(axis)
-
-        @pl.when(index == 0)
-        def _():
-            write(refs[0], 1)
-
-        @pl.when(index != 0)
-        def _():
-            write(refs[0], 0)
-
-    def write_x(ref, end):
-        x = (size_x - 1) * end
+    def field(r):
+        return rows_ref[pl.ds(pl.multiple_of(r * sensors, sensors), sensors), :]
+
+    def high_end(axis, number):
+        return lax.axis_index(axis) % 2 == number
+
+    for number, ref in enumerate(x_refs):
+        high = high_end("gx", number)
+        x = jnp.where(high, size_x - 1, 0)
         for y in range(size_y):
             ref[y * sensors : (y + 1) * sensors, :] = field(x * size_y + y)
         if extra is not None:
-            ref[size_y * sensors : size_y * (sensors + 1), :] = extra[x]
-
-    def write_y(ref, end):
-        y = (size_y - 1) * end
+            ref[size_y * sensors : size_y * (sensors + 1), :] = jnp.where(high, extra[-1], extra[0])
+
+    for number, ref in enumerate(y_refs):
+        high = high_end("gy", number)
+        y = jnp.where(high, size_y - 1, 0)
         for x in range(size_x):
             ref[x * sensors : (x + 1) * sensors, :] = field(x * size_y + y)
-        if extra is not None:
-            for x in range(size_x):
-                ref[size_x * sensors + x : size_x * sensors + x + 1, :] = extra[x][y : y + 1, :]
-
-    def write_z(ref, end):
-        z = (size_z - 1) * end
-        lanes = ref.shape[1]
+            if extra is not None:
+                row = size_x * sensors + x
+                ref[row : row + 1, :] = jnp.where(high, extra[x][size_y - 1 :, :], extra[x][0:1, :])
+
+    lanes = z_refs[0].shape[1]
+    ends = []
+    for z in (0, size_z - 1):
         packed = jnp.zeros((sensors, lanes), jnp.float32)
         for r in range(size_x * size_y):
-            packed = jnp.where(lanes_equal(packed.shape, r), field(r)[:, z : z + 1], packed)
-        ref[0:sensors, :] = packed
+            row = rows_ref[r * sensors : (r + 1) * sensors, :]
+            packed = jnp.where(lanes_equal(packed.shape, r), row[:, z : z + 1], packed)
         if extra is not None:
-            packed = jnp.zeros((size_y, lanes), jnp.float32)
+            labels = jnp.zeros((size_y, lanes), jnp.float32)
             for x in range(size_x):
-                packed = jnp.where(lanes_equal(packed.shape, x), extra[x][:, z : z + 1], packed)
-            ref[sensors : sensors + size_y, :] = packed
-
-    put(x_refs, "gx", write_x)
-    put(y_refs, "gy", write_y)
-    put(z_refs, "gz", write_z)
+                labels = jnp.where(lanes_equal(labels.shape, x), extra[x][:, z : z + 1], labels)
+            packed = jnp.concatenate([packed, labels], axis=0)
+        ends.append(packed)
+    for number, ref in enumerate(z_refs):
+        ref[...] = jnp.where(high_end("gz", number), ends[1], ends[0])
 
 
 def split_refs(refs, counts):
@@ -125,8 +162,7 @@
     shifted = [(label_vmem[x] + 1).astype(jnp.float32) for x in range(size_x)]
     for x in range(size_x):
         shifted_ref[x] = shifted[x]
-    field = lambda r: rows_ref[r * sensors : (r + 1) * sensors, :]
-    write_faces(dims, field, split_refs(face_refs, counts), shifted)
+    write_faces(dims, rows_ref, split_refs(face_refs, counts), shifted)
 
 
 def prepare_kernel(
@@ -284,22 +320,18 @@
     return total
 
 
-def pair_up(refs):
-    return [(refs[2 * i], refs[2 * i + 1]) for i in range(3)]
-
-
 def apply_kernel(dims, counts, rows_ref, shifted_ref, table_ref, *refs):
     sensors, size_x, size_y, size_z = dims
-    halo_refs = pair_up(refs[:6])
-    weight_ref, applied_ref = refs[6:8]
-    face_refs = refs[8:]
+    messages = sum(counts)
+    halo_refs = sort_halos(refs[:messages], refs[2 * messages + 2 :], counts)
+    weight_ref, applied_ref = refs[messages : messages + 2]
+    face_refs = refs[messages + 2 : 2 * messages + 2]
     weights(dims, shifted_ref, table_ref, halo_refs, weight_ref)
     for r in range(size_x * size_y):
         x, y = divmod(r, size_y)
         centre, beside = around(dims, rows_ref, halo_refs, r)
         applied_ref[r * sensors : (r + 1) * sensors, :] = combine(weight_ref, x, y, centre, beside)
-    field = lambda r: applied_ref[r * sensors : (r + 1) * sensors, :]
-    write_faces(dims, field, split_refs(face_refs, counts))
+    write_faces(dims, applied_ref, split_refs(face_refs, counts))
 
 
 def halves(value):
@@ -351,10 +383,11 @@
     ) + lax.dot_general(chosen, low_ref[...], last_with_last, preferred_element_type=jnp.float32)
 
 
-def source_kernel(dims, rows_ref, applied_ref, weight_ref, chosen_ref, *refs):
-    sensors, size_x, size_y, size_z = dims
-    halo_refs = pair_up(refs[:6])
-    column_ref, sum_ref, high_ref, low_ref = refs[6:]
+def source_kernel(dims, counts, rows_ref, applied_ref, weight_ref, chosen_ref, *refs):
+    sensors, size_x, size_y, size_z = dims
+    messages = sum(counts)
+    column_ref, sum_ref, high_ref, low_ref = refs[messages : messages + 4]
+    halo_refs = sort_halos(refs[:messages], refs[messages + 4 :], counts)
     sums = [jnp.zeros((sensors, size_z), jnp.float32) for _ in range(4)]
     for r in range(size_x * size_y):
         source = rows_ref[r * sensors : (r + 1) * sensors, :]
@@ -371,10 +404,12 @@
     )
 
 
-def moment_kernel(dims, applied_ref, weight_ref, sum_ref, *refs):
-    sensors, size_x, size_y, size_z = dims
-    (x_low, x_high), (y_low, y_high), (z_low, z_high) = pair_up(refs[:6])
-    moment_ref = refs[6]
+def moment_kernel(dims, counts, applied_ref, weight_ref, sum_ref, *refs):
+    sensors, size_x, size_y, size_z = dims
+    messages = sum(counts)
+    moment_ref = refs[messages]
+    halo_refs = sort_halos(refs[:messages], refs[messages + 1 :], counts)
+    (x_low, x_high), (y_low, y_high), (z_low, z_high) = halo_refs
 
     def part(ref, index):
         return ref[index * sensors : (index + 1) * sensors, :]
@@ -415,11 +450,14 @@
     return whole, rest, fold, rows, -(-4 * sensors // lane_tile)
 
 
-def applied_kernel(dims, slots_each, applied_ref, weight_ref, chosen_ref, source_column_ref, *refs):
-    sensors = dims[0]
-    column_ref, high_ref, low_ref = refs[6:]
+def applied_kernel(
+    dims, counts, slots_each, applied_ref, weight_ref, chosen_ref, source_column_ref, *refs
+):
+    sensors, messages = dims[0], sum(counts)
+    column_ref, high_ref, low_ref = refs[messages : messages + 3]
+    halo_refs = sort_halos(refs[:messages], refs[messages + 3 :], counts)
     applied_columns = select_columns(
-        dims, applied_ref, weight_ref, pair_up(refs[:6]), chosen_ref, high_ref, low_ref
+        dims, applied_ref, weight_ref, halo_refs, chosen_ref, high_ref, low_ref
     )
     columns = jnp.concatenate([source_column_ref[...], applied_columns], axis=1)
     whole, rest, fold, rows, moment_rows = payload_rows(sensors, slots_each)
@@ -545,18 +583,12 @@
     ]
 
 
-def exchange_all(faces, counts):
-    halos = []
-    for axis, group in zip(("gx", "gy", "gz"), split_refs(faces, counts)):
-        halos.extend(exchange(group, axis))
-    return halos
-
-
 def per_device(source_term, labels, conductivity_table, send_map, owner_slots, sensor_data):
     dims = source_term.shape
     sensors, size_x, size_y, size_z = dims
     rows_count = size_x * size_y
-    counts = [faces_per_axis(lax.axis_size(axis)) for axis in ("gx", "gy", "gz")]
+    counts = face_counts()
+    messages = sum(counts)
     owners = lax.axis_size("gx") * lax.axis_size("gy")
     slots = send_map.size
     slots_each = slots // owners
@@ -577,7 +609,7 @@
         functools.partial(pack_kernel, dims, counts),
         out_shape=[field_shape, array(labels.shape)] + face_shapes(dims, counts, 1),
         in_specs=in_hbm(2),
-        out_specs=in_vmem(2 + sum(counts)),
+        out_specs=in_vmem(2 + messages),
         scratch_shapes=[
             pltpu.VMEM((size_x, sensors, size_y, size_z), jnp.float32),
             pltpu.VMEM((size_x, size_y, size_z), jnp.int32),
@@ -617,38 +649,39 @@
     result = call(
         functools.partial(apply_kernel, dims, counts),
         out_shape=[array((8, size_x, size_y, size_z)), field_shape] + face_shapes(dims, counts, 0),
-        in_specs=in_vmem(9),
-        out_specs=in_vmem(2 + sum(counts)),
+        in_specs=in_vmem(3 + messages),
+        out_specs=in_vmem(2 + messages),
+        scratch_shapes=held_halos(source_halos, counts),
         name="apply",
     )(rows, shifted, table, *source_halos)
     weight, applied, faces = result[0], result[1], result[2:]
     applied_halos = exchange_all(faces, counts)
 
     source_columns, sums = call(
-        functools.partial(source_kernel, dims),
+        functools.partial(source_kernel, dims, counts),
         out_shape=[array((slots, 3 * sensors)), array((4 * sensors, size_z))],
-        in_specs=in_vmem(10),
+        in_specs=in_vmem(4 + messages),
         out_specs=in_vmem(2),
-        scratch_shapes=halves_scratch(3 * sensors),
+        scratch_shapes=halves_scratch(3 * sensors) + held_halos(source_halos, counts),
         name="source_columns",
     )(rows, applied, weight, chosen, *source_halos)
     moment = call(
-        functools.partial(moment_kernel, dims),
+        functools.partial(moment_kernel, dims, counts),
         out_shape=array((8, 4 * sensors)),
-        in_specs=in_vmem(9),
+        in_specs=in_vmem(3 + messages),
         out_specs=in_vmem(1)[0],
+        scratch_shapes=held_halos(applied_halos, counts),
         name="moments",
     )(applied, weight, sums, *applied_halos)
-    depth = lax.axis_size("gz")
-    moment = moment + sum(lax.ppermute(moment, "gz", ring(depth, d)) for d in range(depth - 1, 0, -1))
+    moment = sum_over(moment, "gz")
 
     each = payload + moment_rows
     columns = call(
-        functools.partial(applied_kernel, dims, slots_each),
+        functools.partial(applied_kernel, dims, counts, slots_each),
         out_shape=array((owners * each, lane_tile)),
-        in_specs=in_vmem(10),
+        in_specs=in_vmem(4 + messages),
         out_specs=in_vmem(1)[0],
-        scratch_shapes=halves_scratch(3 * sensors),
+        scratch_shapes=halves_scratch(3 * sensors) + held_halos(applied_halos, counts),
         name="applied_columns",
     )(applied, weight, chosen, source_columns, *applied_halos)
     place = lax.broadcasted_iota(jnp.int32, columns.shape, 0) % each

time: 41.9 us -> 38.2 us (0.912)
  starting transfers between devices: 17.6 us -> 12.9 us
  blocking collectives: 11.6 us -> 12.3 us
    ppermute x13, starting transfers between devices: 17.6 us -> 12.9 us  [the longest x8 11 us: swap(): return lax.ppermute(value, axis, sorted(partner.items()))]
    all_to_all x1, blocking collectives: 11.6 us -> 12.3 us  [per_device(): lax.all_to_all(columns.reshape(owners, 1, each * lane_tile), ('gx', 'gy')...]
  transfers between devices with their start and end apart: 13 -> 13, of which waited for: 2 -> 3; matrix products, arithmetic and copies ran while one was open for 0% -> 0% of each run, Pallas kernels for 13% -> 15%
where the time goes in v5:
time: 38.2 us; the launch traced here: 37.9 us
  starting transfers between devices  12.9 us (34%)
  blocking collectives  12.3 us (32%)
  Pallas kernels  10.1 us (26%)
  waiting for transfers between devices  1.63 us (4%)
  between operations  0.71 us (2%)
    all_to_all x1, blocking collectives, per_device(): lax.all_to_all(columns.reshape(owners, 1, each * lane_tile), ('gx', 'gy')...  12.3 us
    ppermute x8, starting transfers between devices, swap(): return lax.ppermute(value, axis, sorted(partner.items()))  11 us
    pallas_call x1, Pallas kernels, per_device(): call(functools.partial(prepare_kernel, size_z, (slots_each, fold)), out_s...  2.01 us
    ppermute x3, starting transfers between devices, sum_over(): return value + sum((lax.ppermute(value, axis, table) for table in tables))  1.89 us
    pallas_call x1, Pallas kernels, per_device(): call(functools.partial(source_kernel, dims, counts), out_shape=[array((sl...  1.85 us
    pallas_call x1, Pallas kernels, per_device(): call(functools.partial(applied_kernel, dims, counts, slots_each), out_sha...  1.64 us
    pallas_call x1, Pallas kernels, per_device(): call(functools.partial(pack_kernel, dims, counts), out_shape=[field_shape...  1.52 us
    pallas_call x1, Pallas kernels, per_device(): call(functools.partial(owner_kernel, sensors, slots_each), out_shape=[arr...  1.23 us
  transfers between devices with their start and end apart: 13, of which 3 were waited for; matrix products, arithmetic and copies ran while one was open for 0% of the time, Pallas kernels for 15%

profile of v5, /device:TPU:0, one launch (start us, length us, event | category | flops | bytes accessed | tf_op | source)
XLA Modules:
  0.0 37.9 jit_solution(14873816726821192510)
XLA Ops:
  0.6 1.5 %pack.1 = (f32[1024,128]{1,0:T(8,128)S(1)}, f32[4,8,128]{2,1,0:T(8,128)S(1)}, f32[264,128]{1,0:T(8,128)S(1)}, f32[136,128]{1,0:T(8,128)S(1)}, f32[136,128]{1,0:T...) custom-call(f32[32,4,8,128]{3,2,1,0:T(8,128)} %source_ref.1, s32[4,8,128]{2,1,0:T(8,128)} %label_ref.1), custom_call_target="tpu_custom_call" | custom-call | tf_op jit(solution)/shard_map/pack/pallas_call | solution.py:608
  2.2 3.1 %collective-permute-start = (f32[264,128]{1,0:T(8,128)S(1)}, f32[264,128]{1,0:T(8,128)S(1)}, u32[]{:S(2)}, u32[]{:S(2)}) collective-permute-start(f32[264,128]{1,0:T(8,128)S(1)} %get-tuple-element.25), channel_id=1, source_target_pairs={{0,16},{16,0},{1,17},{17,1},{2,18},{18,2},{3,19},{19,3},{4,20},{20... | collective-permute-start | bytes 405512 | tf_op jit(solution)/shard_map/ppermute | solution.py:33
  5.2 1.6 %collective-permute-start.1 = (f32[136,128]{1,0:T(8,128)S(1)}, f32[136,128]{1,0:T(8,128)S(1)}, u32[]{:S(2)}, u32[]{:S(2)}) collective-permute-start(f32[136,128]{1,0:T(8,128)S(1)} %get-tuple-element.26), channel_id=1, source_target_pairs={{0,4},{4,0},{8,12},{12,8},{1,5},{5,1},{9,13},{13,9},{2,6},{6,2},{1... | collective-permute-start | bytes 208904 | tf_op jit(solution)/shard_map/ppermute | solution.py:33
  6.8 0.0 collective-permute-start.2
  6.8 0.5 %collective-permute-start.3 = (f32[40,128]{1,0:T(8,128)S(1)}, f32[40,128]{1,0:T(8,128)S(1)}, u32[]{:S(2)}, u32[]{:S(2)}) collective-permute-start(f32[40,128]{1,0:T(8,128)S(1)} %get-tuple-element.28), channel_id=1, source_target_pairs={{0,1},{1,0},{2,3},{3,2},{4,5},{5,4},{6,7},{7,6},{8,9},{9,8},{10,11... | collective-permute-start | bytes 61448 | tf_op jit(solution)/shard_map/ppermute | solution.py:33
  7.3 1.1 %collective-permute-start.4 = (f32[40,128]{1,0:T(8,128)S(1)}, f32[40,128]{1,0:T(8,128)S(1)}, u32[]{:S(2)}, u32[]{:S(2)}) collective-permute-start(f32[40,128]{1,0:T(8,128)S(1)} %get-tuple-element.29), channel_id=1, source_target_pairs={{0,3},{1,2},{2,1},{3,0},{4,7},{5,6},{6,5},{7,4},{8,11},{9,10},{10,... | collective-permute-start | bytes 61448 | tf_op jit(solution)/shard_map/ppermute | solution.py:33
  8.4 2.0 %prepare.1 = (bf16[256,4096]{1,0:T(8,128)(2,1)S(1)}, bf16[512,128]{1,0:T(8,128)(2,1)S(1)}, f32[32,128]{1,0:T(8,128)S(1)}, f32[6,8,128]{2,1,0:T(8,128)S(1)}) custom-call(s32[1,256]{1,0:T(1,128)} %bitcast.8, s32[1,128]{1,0:T(1,128)} %bitcast.9, f32[32,128]{1,0:T(8,128)} %data_hbm.1, f32[6]{0:T(128)} %table_hbm.1), custom_call_target="tpu_custom_call" | custom-call | tf_op jit(solution)/shard_map/prepare/pallas_call | solution.py:623
  10.4 0.0 collective-permute-done.3.refs_3_
  10.4 0.1 collective-permute-done.4.refs_4_
  10.5 0.0 collective-permute-done.1.refs_1_
  10.6 0.0 collective-permute-done.2.refs_2_
  10.6 0.0 collective-permute-done.refs_0_
  10.6 1.2 %apply.1 = (f32[8,4,8,128]{3,2,1,0:T(8,128)S(1)}, f32[1024,128]{1,0:T(8,128)S(1)}, f32[256,128]{1,0:T(8,128)S(1)}, f32[128,128]{1,0:T(8,128)S(1)}, f32[128,128]{...) custom-call(f32[1024,128]{1,0:T(8,128)S(1)} %get-tuple-element.22.rows_ref, ...), custom_call_target="tpu_custom_call" | custom-call | tf_op jit(solution)/shard_map/apply/pallas_call | solution.py:649
  11.8 0.6 %collective-permute-start.5 = (f32[256,128]{1,0:T(8,128)S(1)}, f32[256,128]{1,0:T(8,128)S(1)}, u32[]{:S(2)}, u32[]{:S(2)}) collective-permute-start(f32[256,128]{1,0:T(8,128)S(1)} %get-tuple-element.34), channel_id=1, source_target_pairs={{0,16},{16,0},{1,17},{17,1},{2,18},{18,2},{3,19},{19,3},{4,20},{20... | collective-permute-start | bytes 393224 | tf_op jit(solution)/shard_map/ppermute | solution.py:33
  12.3 3.1 %collective-permute-start.6 = (f32[128,128]{1,0:T(8,128)S(1)}, f32[128,128]{1,0:T(8,128)S(1)}, u32[]{:S(2)}, u32[]{:S(2)}) collective-permute-start(f32[128,128]{1,0:T(8,128)S(1)} %get-tuple-element.35), channel_id=1, source_target_pairs={{0,4},{4,0},{8,12},{12,8},{1,5},{5,1},{9,13},{13,9},{2,6},{6,2},{1... | collective-permute-start | bytes 196616 | tf_op jit(solution)/shard_map/ppermute | solution.py:33
  15.4 0.0 collective-permute-start.7
  15.4 0.5 %collective-permute-start.8 = (f32[32,128]{1,0:T(8,128)S(1)}, f32[32,128]{1,0:T(8,128)S(1)}, u32[]{:S(2)}, u32[]{:S(2)}) collective-permute-start(f32[32,128]{1,0:T(8,128)S(1)} %get-tuple-element.37), channel_id=1, source_target_pairs={{0,1},{1,0},{2,3},{3,2},{4,5},{5,4},{6,7},{7,6},{8,9},{9,8},{10,11... | collective-permute-start | bytes 49160 | tf_op jit(solution)/shard_map/ppermute | solution.py:33
  15.9 0.6 %collective-permute-start.9 = (f32[32,128]{1,0:T(8,128)S(1)}, f32[32,128]{1,0:T(8,128)S(1)}, u32[]{:S(2)}, u32[]{:S(2)}) collective-permute-start(f32[32,128]{1,0:T(8,128)S(1)} %get-tuple-element.38), channel_id=1, source_target_pairs={{0,3},{1,2},{2,1},{3,0},{4,7},{5,6},{6,5},{7,4},{8,11},{9,10},{10,... | collective-permute-start | bytes 49160 | tf_op jit(solution)/shard_map/ppermute | solution.py:33
  16.6 1.9 %source_columns.1 = (f32[256,96]{1,0:T(8,128)S(1)}, f32[128,128]{1,0:T(8,128)S(1)}) custom-call(f32[1024,128]{1,0:T(8,128)S(1)} %get-tuple-element.22.rows_ref, f32[1024,128]{1,0:T(8,128)S(1)} %get-tuple-element.30.applied_ref, f32[8,4,8,128]{3,2,1,0:T(8,128)S(1)} %get-tuple-element.31.weight_ref, bf16[256,4096]{1,0:T(8,128)(2,1)S(1)} %get-tuple-element.32.chosen_ref, ...), custom_call_target="tpu_custom_call" | custom-call | tf_op jit(solution)/shard_map/source_columns/pallas_call | solution.py:660
  18.4 0.0 collective-permute-done.8.refs_3_
  18.4 0.6 %collective-permute-done.9.refs_4_ = f32[32,128]{1,0:T(8,128)S(1)} collective-permute-done((f32[32,128]{1,0:T(8,128)S(1)}, f32[32,128]{1,0:T(8,128)S(1)}, u32[]{:S(2)}, u32[]{:S(2)}) %collective-permute-start.9) | collective-permute-done | bytes 16416 | tf_op jit(solution)/shard_map/ppermute | solution.py:33
  19.1 0.0 collective-permute-done.6.refs_1_
  19.1 0.0 collective-permute-done.7.refs_2_
  19.1 0.0 collective-permute-done.5.refs_0_
  19.1 0.6 %moments.1 = f32[8,128]{1,0:T(8,128)S(1)} custom-call(f32[1024,128]{1,0:T(8,128)S(1)} %get-tuple-element.30.applied_ref, f32[8,4,8,128]{3,2,1,0:T(8,128)S(1)} %get-tuple-element.31.weight_ref, f32[128,128]{1,0:T(8,128)S(1)} %get-tuple-element.33.sum_ref, f32[256,128]{1,0:T(8,128)S(1)} %collective-permute-done.5.refs_0_, ...), custom_call_target="tpu_custom_call" | custom-call | tf_op jit(solution)/shard_map/moments/pallas_call | solution.py:668
  19.7 0.8 %collective-permute-start.10 = (f32[8,128]{1,0:T(8,128)S(1)}, f32[8,128]{1,0:T(8,128)S(1)}, u32[]{:S(2)}, u32[]{:S(2)}) collective-permute-start(f32[8,128]{1,0:T(8,128)S(1)} %moments.1), channel_id=1, source_target_pairs={{0,3},{1,2},{2,1},{3,0},{4,7},{5,6},{6,5},{7,4},{8,11},{9,10},{10,... | collective-permute-start | bytes 12296 | tf_op jit(solution)/shard_map/ppermute | solution.py:42
  20.5 1.0 %collective-permute-start.11 = (f32[8,128]{1,0:T(8,128)S(1)}, f32[8,128]{1,0:T(8,128)S(1)}, u32[]{:S(2)}, u32[]{:S(2)}) collective-permute-start(f32[8,128]{1,0:T(8,128)S(1)} %moments.1), channel_id=1, source_target_pairs={{0,2},{1,3},{2,0},{3,1},{4,6},{5,7},{6,4},{7,5},{8,10},{9,11},{10,... | collective-permute-start | bytes 12296 | tf_op jit(solution)/shard_map/ppermute | solution.py:42
  21.5 0.1 collective-permute-start.12
  21.6 1.6 %applied_columns.1 = f32[392,128]{1,0:T(8,128)S(1)} custom-call(f32[1024,128]{1,0:T(8,128)S(1)} %get-tuple-element.30.applied_ref, f32[8,4,8,128]{3,2,1,0:T(8,128)S(1)} %get-tuple-element.31.weight_ref, bf16[256,4096]{1,0:T(8,128)(2,1)S(1)} %get-tuple-element.32.chosen_ref, f32[256,96]{1,0:T(8,128)S(1)} %get-tuple-element.39.source_column_ref, ...), custom_call_target="tpu_custom_call" | custom-call | tf_op jit(solution)/shard_map/applied_columns/pallas_call | solution.py:679
  23.3 0.0 collective-permute-done.10
  23.3 0.8 %collective-permute-done.11 = f32[8,128]{1,0:T(8,128)S(1)} collective-permute-done((f32[8,128]{1,0:T(8,128)S(1)}, f32[8,128]{1,0:T(8,128)S(1)}, u32[]{:S(2)}, u32[]{:S(2)}) %collective-permute-start.11) | collective-permute-done | bytes 4128 | tf_op jit(solution)/shard_map/ppermute | solution.py:42
  24.1 0.0 collective-permute-done.12
  24.1 0.2 fusion
  24.4 12.3 %all_to_all.5 = f32[8,1,6272]{2,1,0:T(1,128)S(1)} all-to-all(f32[8,1,6272]{2,1,0:T(1,128)S(1)} %bitcast.7), channel_id=1, replica_groups=mesh['gx'=2,'gy'=4,'gz'=4] {'gx','gy'}, dimensions={0} | all-to-all | bytes 401408 | tf_op jit(solution)/shard_map/all_to_all | solution.py:691
  36.7 1.2 %owner.1 = (f32[3,128,128]{2,1,0:T(8,128)}, f32[6,128]{1,0:T(8,128)}) custom-call(f32[392,128]{1,0:T(8,128)S(1)} %bitcast.6, bf16[512,128]{1,0:T(8,128)(2,1)S(1)} %get-tuple-element.40.chosen_ref, f32[32,128]{1,0:T(8,128)S(1)} %get-tuple-element.41.data_ref), custom_call_target="tpu_custom_call" | custom-call | tf_op jit(solution)/shard_map/owner/pallas_call | solution.py:694
  (4 shorter events, 0.0 us)
Async XLA Ops:
  2.2 8.4 %collective-permute-start = (f32[264,128]{1,0:T(8,128)S(1)}, f32[264,128]{1,0:T(8,128)S(1)}, u32[]{:S(2)}, u32[]{:S(2)}) collective-permute-start(f32[264,128]{1,0:T(8,128)S(1)} %get-tuple-element.25), channel_id=1, source_target_pairs={{0,16},{16,0},{1,17},{17,1},{2,18},{18,2},{3,19},{19,3},{4,20},{20... | collective-permute-start | bytes 405512 | tf_op jit(solution)/shard_map/ppermute | solution.py:33
  5.2 5.3 %collective-permute-start.1 = (f32[136,128]{1,0:T(8,128)S(1)}, f32[136,128]{1,0:T(8,128)S(1)}, u32[]{:S(2)}, u32[]{:S(2)}) collective-permute-start(f32[136,128]{1,0:T(8,128)S(1)} %get-tuple-element.26), channel_id=1, source_target_pairs={{0,4},{4,0},{8,12},{12,8},{1,5},{5,1},{9,13},{13,9},{2,6},{6,2},{1... | collective-permute-start | bytes 208904 | tf_op jit(solution)/shard_map/ppermute | solution.py:33
  6.8 3.8 %collective-permute-start.2 = (f32[136,128]{1,0:T(8,128)S(1)}, f32[136,128]{1,0:T(8,128)S(1)}, u32[]{:S(2)}, u32[]{:S(2)}) collective-permute-start(f32[136,128]{1,0:T(8,128)S(1)} %get-tuple-element.27), channel_id=1, source_target_pairs={{0,1},{1,0},{2,3},{3,2},{4,8},{5,9},{6,10},{7,11},{8,4},{9,5},{10,... | collective-permute-start | bytes 208904 | tf_op jit(solution)/shard_map/ppermute | solution.py:30
  6.8 3.6 %collective-permute-start.3 = (f32[40,128]{1,0:T(8,128)S(1)}, f32[40,128]{1,0:T(8,128)S(1)}, u32[]{:S(2)}, u32[]{:S(2)}) collective-permute-start(f32[40,128]{1,0:T(8,128)S(1)} %get-tuple-element.28), channel_id=1, source_target_pairs={{0,1},{1,0},{2,3},{3,2},{4,5},{5,4},{6,7},{7,6},{8,9},{9,8},{10,11... | collective-permute-start | bytes 61448 | tf_op jit(solution)/shard_map/ppermute | solution.py:33
  7.3 3.2 %collective-permute-start.4 = (f32[40,128]{1,0:T(8,128)S(1)}, f32[40,128]{1,0:T(8,128)S(1)}, u32[]{:S(2)}, u32[]{:S(2)}) collective-permute-start(f32[40,128]{1,0:T(8,128)S(1)} %get-tuple-element.29), channel_id=1, source_target_pairs={{0,3},{1,2},{2,1},{3,0},{4,7},{5,6},{6,5},{7,4},{8,11},{9,10},{10,... | collective-permute-start | bytes 61448 | tf_op jit(solution)/shard_map/ppermute | solution.py:33
  11.8 7.3 %collective-permute-start.5 = (f32[256,128]{1,0:T(8,128)S(1)}, f32[256,128]{1,0:T(8,128)S(1)}, u32[]{:S(2)}, u32[]{:S(2)}) collective-permute-start(f32[256,128]{1,0:T(8,128)S(1)} %get-tuple-element.34), channel_id=1, source_target_pairs={{0,16},{16,0},{1,17},{17,1},{2,18},{18,2},{3,19},{19,3},{4,20},{20... | collective-permute-start | bytes 393224 | tf_op jit(solution)/shard_map/ppermute | solution.py:33
  12.3 6.7 %collective-permute-start.6 = (f32[128,128]{1,0:T(8,128)S(1)}, f32[128,128]{1,0:T(8,128)S(1)}, u32[]{:S(2)}, u32[]{:S(2)}) collective-permute-start(f32[128,128]{1,0:T(8,128)S(1)} %get-tuple-element.35), channel_id=1, source_target_pairs={{0,4},{4,0},{8,12},{12,8},{1,5},{5,1},{9,13},{13,9},{2,6},{6,2},{1... | collective-permute-start | bytes 196616 | tf_op jit(solution)/shard_map/ppermute | solution.py:33
  15.4 3.7 %collective-permute-start.7 = (f32[128,128]{1,0:T(8,128)S(1)}, f32[128,128]{1,0:T(8,128)S(1)}, u32[]{:S(2)}, u32[]{:S(2)}) collective-permute-start(f32[128,128]{1,0:T(8,128)S(1)} %get-tuple-element.36), channel_id=1, source_target_pairs={{0,1},{1,0},{2,3},{3,2},{4,8},{5,9},{6,10},{7,11},{8,4},{9,5},{10,... | collective-permute-start | bytes 196616 | tf_op jit(solution)/shard_map/ppermute | solution.py:30
  15.4 3.0 %collective-permute-start.8 = (f32[32,128]{1,0:T(8,128)S(1)}, f32[32,128]{1,0:T(8,128)S(1)}, u32[]{:S(2)}, u32[]{:S(2)}) collective-permute-start(f32[32,128]{1,0:T(8,128)S(1)} %get-tuple-element.37), channel_id=1, source_target_pairs={{0,1},{1,0},{2,3},{3,2},{4,5},{5,4},{6,7},{7,6},{8,9},{9,8},{10,11... | collective-permute-start | bytes 49160 | tf_op jit(solution)/shard_map/ppermute | solution.py:33
  15.9 3.2 %collective-permute-start.9 = (f32[32,128]{1,0:T(8,128)S(1)}, f32[32,128]{1,0:T(8,128)S(1)}, u32[]{:S(2)}, u32[]{:S(2)}) collective-permute-start(f32[32,128]{1,0:T(8,128)S(1)} %get-tuple-element.38), channel_id=1, source_target_pairs={{0,3},{1,2},{2,1},{3,0},{4,7},{5,6},{6,5},{7,4},{8,11},{9,10},{10,... | collective-permute-start | bytes 49160 | tf_op jit(solution)/shard_map/ppermute | solution.py:33
  19.7 3.5 %collective-permute-start.10 = (f32[8,128]{1,0:T(8,128)S(1)}, f32[8,128]{1,0:T(8,128)S(1)}, u32[]{:S(2)}, u32[]{:S(2)}) collective-permute-start(f32[8,128]{1,0:T(8,128)S(1)} %moments.1), channel_id=1, source_target_pairs={{0,3},{1,2},{2,1},{3,0},{4,7},{5,6},{6,5},{7,4},{8,11},{9,10},{10,... | collective-permute-start | bytes 12296 | tf_op jit(solution)/shard_map/ppermute | solution.py:42
  20.5 3.6 %collective-permute-start.11 = (f32[8,128]{1,0:T(8,128)S(1)}, f32[8,128]{1,0:T(8,128)S(1)}, u32[]{:S(2)}, u32[]{:S(2)}) collective-permute-start(f32[8,128]{1,0:T(8,128)S(1)} %moments.1), channel_id=1, source_target_pairs={{0,2},{1,3},{2,0},{3,1},{4,6},{5,7},{6,4},{7,5},{8,10},{9,11},{10,... | collective-permute-start | bytes 12296 | tf_op jit(solution)/shard_map/ppermute | solution.py:42
  21.5 2.6 %collective-permute-start.12 = (f32[8,128]{1,0:T(8,128)S(1)}, f32[8,128]{1,0:T(8,128)S(1)}, u32[]{:S(2)}, u32[]{:S(2)}) collective-permute-start(f32[8,128]{1,0:T(8,128)S(1)} %moments.1), channel_id=1, source_target_pairs={{0,1},{1,0},{2,3},{3,2},{4,5},{5,4},{6,7},{7,6},{8,9},{9,8},{10,11... | collective-permute-start | bytes 12296 | tf_op jit(solution)/shard_map/ppermute | solution.py:42

commit v6 on v5

--- a/solution.py
+++ b/solution.py
@@ -90,7 +90,7 @@
     return flags
 
 
-def write_faces(dims, rows_ref, face_refs, extra=None):
+def write_faces(dims, rows_ref, face_refs, z_ends, extra=None):
     sensors, size_x, size_y, size_z = dims
     x_refs, y_refs, z_refs = face_refs
 
@@ -117,21 +117,28 @@
                 row = size_x * sensors + x
                 ref[row : row + 1, :] = jnp.where(high, extra[x][size_y - 1 :, :], extra[x][0:1, :])
 
-    lanes = z_refs[0].shape[1]
+    ends = z_ends
+    if extra is not None:
+        ends = []
+        for z, packed in zip((0, size_z - 1), z_ends):
+            labels = jnp.zeros((size_y, packed.shape[1]), jnp.float32)
+            for x in range(size_x):
+                labels = jnp.where(lanes_equal(labels.shape, x), extra[x][:, z : z + 1], labels)
+            ends.append(jnp.concatenate([packed, labels], axis=0))
+    for number, ref in enumerate(z_refs):
+        ref[...] = jnp.where(high_end("gz", number), ends[1], ends[0])
+
+
+def pack_ends(dims, rows_ref, lanes):
+    sensors, size_x, size_y, size_z = dims
     ends = []
     for z in (0, size_z - 1):
         packed = jnp.zeros((sensors, lanes), jnp.float32)
         for r in range(size_x * size_y):
             row = rows_ref[r * sensors : (r + 1) * sensors, :]
             packed = jnp.where(lanes_equal(packed.shape, r), row[:, z : z + 1], packed)
-        if extra is not None:
-            labels = jnp.zeros((size_y, lanes), jnp.float32)
-            for x in range(size_x):
-                labels = jnp.where(lanes_equal(labels.shape, x), extra[x][:, z : z + 1], labels)
-            packed = jnp.concatenate([packed, labels], axis=0)
         ends.append(packed)
-    for number, ref in enumerate(z_refs):
-        ref[...] = jnp.where(high_end("gz", number), ends[1], ends[0])
+    return ends
 
 
 def split_refs(refs, counts):
@@ -142,67 +149,56 @@
     return groups
 
 
-def pack_kernel(dims, counts, source_ref, label_ref, rows_ref, shifted_ref, *refs):
-    sensors, size_x, size_y, size_z = dims
-    face_refs, (staged_ref, label_vmem, semaphores) = refs[:-3], refs[-3:]
+def pack_kernel(dims, counts, source_ref, label_ref, *refs):
+    sensors, size_x, size_y, size_z = dims
+    small_hbm, refs = refs[:4], refs[4:]
+    (rows_ref, shifted_ref, table_ref), small_refs = refs[:3], refs[3:6]
+    face_refs = refs[6 : 6 + sum(counts)]
+    staged_ref, label_vmem, level_ref, semaphores = refs[6 + sum(counts) :]
     copies = [
         pltpu.make_async_copy(source_ref.at[:, x], staged_ref.at[x], semaphores.at[x])
         for x in range(size_x)
     ]
-    copies.append(pltpu.make_async_copy(label_ref, label_vmem, semaphores.at[size_x]))
-    for copy in copies:
+    moves = [(label_ref, label_vmem), *zip(small_hbm, (*small_refs, level_ref))]
+    for k, move in enumerate(moves):
+        copies.append(pltpu.make_async_copy(*move, semaphores.at[size_x + k]))
+    for copy in copies[size_x:] + copies[:size_x]:
         copy.start()
+    for copy in copies[size_x:]:
+        copy.wait()
+    for level in range(level_ref.shape[0]):
+        table_ref[level] = jnp.full(table_ref.shape[1:], level_ref[level], jnp.float32)
+    shifted = [(label_vmem[x] + 1).astype(jnp.float32) for x in range(size_x)]
+    for x in range(size_x):
+        shifted_ref[x] = shifted[x]
     flat = staged_ref.reshape(size_x, sensors * size_y, size_z)
     for x in range(size_x):
         copies[x].wait()
         for y in range(size_y):
             r = x * size_y + y
             rows_ref[r * sensors : (r + 1) * sensors, :] = flat[x, pl.ds(y, sensors, stride=size_y), :]
-    copies[size_x].wait()
-    shifted = [(label_vmem[x] + 1).astype(jnp.float32) for x in range(size_x)]
-    for x in range(size_x):
-        shifted_ref[x] = shifted[x]
-    write_faces(dims, rows_ref, split_refs(face_refs, counts), shifted)
+    face_refs = split_refs(face_refs, counts)
+    z_ends = pack_ends(dims, rows_ref, face_refs[2][0].shape[1])
+    write_faces(dims, rows_ref, face_refs, z_ends, shifted)
 
 
 def prepare_kernel(
-    size_z,
-    folding,
-    voxel_hbm,
-    owned_hbm,
-    data_hbm,
-    table_hbm,
-    chosen_ref,
-    owned_chosen_ref,
-    held_ref,
-    table_ref,
-    voxel_ref,
-    owned_ref,
-    level_ref,
-    semaphores,
+    size_z, folding, voxel_ref, owned_ref, level_ref, chosen_ref, owned_chosen_ref, table_ref
 ):
-    moves = (
-        (voxel_hbm, voxel_ref),
-        (owned_hbm, owned_ref),
-        (data_hbm, held_ref),
-        (table_hbm, level_ref),
-    )
-    copies = [pltpu.make_async_copy(*move, semaphores.at[k]) for k, move in enumerate(moves)]
-    for copy in copies:
-        copy.start()
-    for copy in copies:
-        copy.wait()
-    for level in range(level_ref.shape[0]):
-        table_ref[level] = jnp.full(table_ref.shape[1:], level_ref[level], jnp.float32)
+    table_ref[...] = level_ref[...]
     slots, voxels = chosen_ref.shape
     square = (slots, slots)
     diagonal = lanes_equal(square, lax.broadcasted_iota(jnp.int32, square, 0))
     voxel = jnp.where(diagonal, voxel_ref[...].astype(jnp.float32), 0.0)
     voxel = jnp.sum(voxel, axis=1, keepdims=True).astype(jnp.int32)
     voxel = jnp.broadcast_to(voxel, (slots, size_z))
+    row = voxel // size_z
     lane_index = lax.broadcasted_iota(jnp.int32, (slots, size_z), 1)
-    for first in range(0, voxels, size_z):
-        chosen_ref[:, first : first + size_z] = one_hot(lane_index == voxel - first)
+    lane = one_hot(lane_index == voxel - row * size_z)
+    row = row.astype(jnp.float32).astype(jnp.bfloat16)
+    none = jnp.zeros_like(lane)
+    for r in range(voxels // size_z):
+        chosen_ref[:, r * size_z : (r + 1) * size_z] = jnp.where(row == r, lane, none)
     row_index = lax.broadcasted_iota(jnp.int32, (slots, owned_ref.shape[1]), 0)
     owned_chosen_ref[0:slots, :] = one_hot(row_index == owned_ref[...])
     slots_each, fold = folding
@@ -323,15 +319,23 @@
 def apply_kernel(dims, counts, rows_ref, shifted_ref, table_ref, *refs):
     sensors, size_x, size_y, size_z = dims
     messages = sum(counts)
-    halo_refs = sort_halos(refs[:messages], refs[2 * messages + 2 :], counts)
-    weight_ref, applied_ref = refs[messages : messages + 2]
-    face_refs = refs[messages + 2 : 2 * messages + 2]
+    halo_refs = sort_halos(refs[:messages], refs[2 * messages + 3 :], counts)
+    weight_ref, end_ref, applied_ref = refs[messages : messages + 3]
+    face_refs = split_refs(refs[messages + 3 : 2 * messages + 3], counts)
     weights(dims, shifted_ref, table_ref, halo_refs, weight_ref)
     for r in range(size_x * size_y):
         x, y = divmod(r, size_y)
         centre, beside = around(dims, rows_ref, halo_refs, r)
         applied_ref[r * sensors : (r + 1) * sensors, :] = combine(weight_ref, x, y, centre, beside)
-    write_faces(dims, applied_ref, split_refs(face_refs, counts))
+    z_ends = pack_ends(dims, applied_ref, end_ref.shape[2])
+    write_faces(dims, applied_ref, face_refs, z_ends)
+    for end, (k, z) in enumerate(((4, 0), (5, size_z - 1))):
+        packed = jnp.zeros((size_y, end_ref.shape[2]), jnp.float32)
+        row_index = lax.broadcasted_iota(jnp.int32, packed.shape, 0)
+        for x in range(size_x):
+            here = lanes_equal(packed.shape, row_index + x * size_y)
+            packed = jnp.where(here, weight_ref[k, x][:, z : z + 1], packed)
+        end_ref[end] = jnp.sum(packed, axis=0, keepdims=True) * z_ends[end]
 
 
 def halves(value):
@@ -365,9 +369,10 @@
     return total - weight(4) * before - weight(5) * after
 
 
-def select_columns(dims, rows_ref, weight_ref, halo_refs, chosen_ref, high_ref, low_ref):
+def select_columns(dims, rows_ref, weight_ref, halo_refs, chosen_ref, parts_ref):
     sensors, size_x, size_y, size_z = dims
     flags = neighbour_flags()
+    width = 3 * sensors
     for r in range(size_x * size_y):
         x, y = divmod(r, size_y)
         span = slice(r * size_z, (r + 1) * size_z)
@@ -375,19 +380,19 @@
         _, beside = around(dims, rows_ref, halo_refs, r, flags)
         for c in range(3):
             high, low = halves(scale * (beside[2 * c + 1] - beside[2 * c]))
-            high_ref[c * sensors : (c + 1) * sensors, span] = high
-            low_ref[c * sensors : (c + 1) * sensors, span] = low
-    chosen = chosen_ref[...]
-    return lax.dot_general(
-        chosen, high_ref[...], last_with_last, preferred_element_type=jnp.float32
-    ) + lax.dot_general(chosen, low_ref[...], last_with_last, preferred_element_type=jnp.float32)
+            parts_ref[c * sensors : (c + 1) * sensors, span] = high
+            parts_ref[width + c * sensors : width + (c + 1) * sensors, span] = low
+    found = lax.dot_general(
+        chosen_ref[...], parts_ref[...], last_with_last, preferred_element_type=jnp.float32
+    )
+    return found[:, :width] + found[:, width:]
 
 
 def source_kernel(dims, counts, rows_ref, applied_ref, weight_ref, chosen_ref, *refs):
     sensors, size_x, size_y, size_z = dims
     messages = sum(counts)
-    column_ref, sum_ref, high_ref, low_ref = refs[messages : messages + 4]
-    halo_refs = sort_halos(refs[:messages], refs[messages + 4 :], counts)
+    column_ref, sum_ref, parts_ref = refs[messages : messages + 3]
+    halo_refs = sort_halos(refs[:messages], refs[messages + 3 :], counts)
     sums = [jnp.zeros((sensors, size_z), jnp.float32) for _ in range(4)]
     for r in range(size_x * size_y):
         source = rows_ref[r * sensors : (r + 1) * sensors, :]
@@ -400,11 +405,11 @@
     for k in range(4):
         sum_ref[k * sensors : (k + 1) * sensors, :] = sums[k]
     column_ref[...] = select_columns(
-        dims, rows_ref, weight_ref, halo_refs, chosen_ref, high_ref, low_ref
-    )
-
-
-def moment_kernel(dims, counts, applied_ref, weight_ref, sum_ref, *refs):
+        dims, rows_ref, weight_ref, halo_refs, chosen_ref, parts_ref
+    )
+
+
+def moment_kernel(dims, counts, applied_ref, weight_ref, sum_ref, end_ref, *refs):
     sensors, size_x, size_y, size_z = dims
     messages = sum(counts)
     moment_ref = refs[messages]
@@ -418,20 +423,20 @@
         x, y = divmod(r, size_y)
         return weight_ref[k, x, y : y + 1, :] * part(applied_ref, r) * beside
 
-    zero = jnp.zeros((sensors, size_z), jnp.float32)
-    outward, below, above = zero, zero, zero
+    outward = jnp.zeros((sensors, size_z), jnp.float32)
     for y in range(size_y):
         outward = outward + crossing(0, y, part(x_low, y))
         outward = outward + crossing(1, (size_x - 1) * size_y + y, part(x_high, y))
     for x in range(size_x):
         outward = outward + crossing(2, x * size_y, part(y_low, x))
         outward = outward + crossing(3, x * size_y + size_y - 1, part(y_high, x))
-    for r in range(size_x * size_y):
-        below = below + crossing(4, r, z_low[0:sensors, r : r + 1])
-        above = above + crossing(5, r, z_high[0:sensors, r : r + 1])
-    lane_index = lax.broadcasted_iota(jnp.int32, zero.shape, 1)
-    outward = outward + jnp.where(lane_index == 0, below, 0.0)
-    outward = outward + jnp.where(lane_index == size_z - 1, above, 0.0)
+    crossed = end_ref[0] * z_low[0:sensors, :] + end_ref[1] * z_high[0:sensors, :]
+    for first in range(0, crossed.shape[1], size_z):
+        piece = crossed[:, first : first + size_z]
+        spare = size_z - piece.shape[1]
+        if spare:
+            piece = jnp.concatenate([piece, jnp.zeros((sensors, spare), jnp.float32)], axis=1)
+        outward = outward + piece
     last = part(sum_ref, 3) - outward
     moment_ref[...] = lax.dot_general(
         jnp.ones((8, size_z), jnp.float32),
@@ -454,10 +459,10 @@
     dims, counts, slots_each, applied_ref, weight_ref, chosen_ref, source_column_ref, *refs
 ):
     sensors, messages = dims[0], sum(counts)
-    column_ref, high_ref, low_ref = refs[messages : messages + 3]
-    halo_refs = sort_halos(refs[:messages], refs[messages + 3 :], counts)
+    column_ref, parts_ref = refs[messages : messages + 2]
+    halo_refs = sort_halos(refs[:messages], refs[messages + 2 :], counts)
     applied_columns = select_columns(
-        dims, applied_ref, weight_ref, halo_refs, chosen_ref, high_ref, low_ref
+        dims, applied_ref, weight_ref, halo_refs, chosen_ref, parts_ref
     )
     columns = jnp.concatenate([source_column_ref[...], applied_columns], axis=1)
     whole, rest, fold, rows, moment_rows = payload_rows(sensors, slots_each)
@@ -601,60 +606,55 @@
     def array(shape, dtype=jnp.float32):
         return jax.ShapeDtypeStruct(shape, dtype)
 
-    def halves_scratch(rows):
-        return [pltpu.VMEM((rows, voxels), jnp.bfloat16)] * 2
-
+    parts = [pltpu.VMEM((6 * sensors, voxels), jnp.bfloat16)]
     field_shape = array((rows_count * sensors, size_z))
+    levels = conductivity_table.shape[0]
+    small = (
+        send_map.reshape(1, slots),
+        owner_slots.reshape(1, positions),
+        sensor_data,
+        conductivity_table,
+    )
     packed = call(
         functools.partial(pack_kernel, dims, counts),
-        out_shape=[field_shape, array(labels.shape)] + face_shapes(dims, counts, 1),
-        in_specs=in_hbm(2),
-        out_specs=in_vmem(2 + messages),
+        out_shape=[field_shape, array(labels.shape), array((levels, size_y, size_z))]
+        + [array(value.shape, value.dtype) for value in small[:3]]
+        + face_shapes(dims, counts, 1),
+        in_specs=in_hbm(6),
+        out_specs=in_vmem(6 + messages),
         scratch_shapes=[
             pltpu.VMEM((size_x, sensors, size_y, size_z), jnp.float32),
             pltpu.VMEM((size_x, size_y, size_z), jnp.int32),
-            pltpu.SemaphoreType.DMA((size_x + 1,)),
+            pltpu.SMEM((levels,), jnp.float32),
+            pltpu.SemaphoreType.DMA((size_x + 5,)),
         ],
         name="pack",
-    )(*held_in_hbm(source_term, labels))
-    rows, shifted, faces = packed[0], packed[1], packed[2:]
+    )(*held_in_hbm(source_term, labels, *small))
+    rows, shifted, table, voxel, owned, data, *faces = packed
     source_halos = exchange_all(faces, counts)
-    levels = conductivity_table.shape[0]
-    chosen, owned_chosen, data, table = call(
+    chosen, owned_chosen, table = call(
         functools.partial(prepare_kernel, size_z, (slots_each, fold)),
         out_shape=[
             array((slots, voxels), jnp.bfloat16),
             array((slots * (2 if fold else 1), positions), jnp.bfloat16),
-            array(sensor_data.shape),
-            array((levels, size_y, size_z)),
+            array(table.shape),
         ],
-        in_specs=in_hbm(4),
-        out_specs=in_vmem(4),
-        scratch_shapes=[
-            pltpu.VMEM((1, slots), jnp.int32),
-            pltpu.VMEM((1, positions), jnp.int32),
-            pltpu.SMEM((levels,), jnp.float32),
-            pltpu.SemaphoreType.DMA((4,)),
-        ],
+        in_specs=in_vmem(3),
+        out_specs=in_vmem(3),
         name="prepare",
-    )(
-        *held_in_hbm(
-            send_map.reshape(1, slots),
-            owner_slots.reshape(1, positions),
-            sensor_data,
-            conductivity_table,
-        )
-    )
-
+    )(voxel, owned, table)
+
+    faces_out = face_shapes(dims, counts, 0)
+    end_shape = (2, *faces_out[-1].shape)
     result = call(
         functools.partial(apply_kernel, dims, counts),
-        out_shape=[array((8, size_x, size_y, size_z)), field_shape] + face_shapes(dims, counts, 0),
+        out_shape=[array((8, size_x, size_y, size_z)), array(end_shape), field_shape] + faces_out,
         in_specs=in_vmem(3 + messages),
-        out_specs=in_vmem(2 + messages),
+        out_specs=in_vmem(3 + messages),
         scratch_shapes=held_halos(source_halos, counts),
         name="apply",
     )(rows, shifted, table, *source_halos)
-    weight, applied, faces = result[0], result[1], result[2:]
+    weight, ends, applied, faces = *result[:3], result[3:]
     applied_halos = exchange_all(faces, counts)
 
     source_columns, sums = call(
@@ -662,17 +662,17 @@
         out_shape=[array((slots, 3 * sensors)), array((4 * sensors, size_z))],
         in_specs=in_vmem(4 + messages),
         out_specs=in_vmem(2),
-        scratch_shapes=halves_scratch(3 * sensors) + held_halos(source_halos, counts),
+        scratch_shapes=parts + held_halos(source_halos, counts),
         name="source_columns",
     )(rows, applied, weight, chosen, *source_halos)
     moment = call(
         functools.partial(moment_kernel, dims, counts),
         out_shape=array((8, 4 * sensors)),
-        in_specs=in_vmem(3 + messages),
+        in_specs=in_vmem(4 + messages),
         out_specs=in_vmem(1)[0],
         scratch_shapes=held_halos(applied_halos, counts),
         name="moments",
-    )(applied, weight, sums, *applied_halos)
+    )(applied, weight, sums, ends, *applied_halos)
     moment = sum_over(moment, "gz")
 
     each = payload + moment_rows
@@ -681,7 +681,7 @@
         out_shape=array((owners * each, lane_tile)),
         in_specs=in_vmem(4 + messages),
         out_specs=in_vmem(1)[0],
-        scratch_shapes=halves_scratch(3 * sensors) + held_halos(applied_halos, counts),
+        scratch_shapes=parts + held_halos(applied_halos, counts),
         name="applied_columns",
     )(applied, weight, chosen, source_columns, *applied_halos)
     place = lax.broadcasted_iota(jnp.int32, columns.shape, 0) % each

time: 38.2 us -> 37.8 us (0.990)
  Pallas kernels: 10.1 us -> 8.02 us
  waiting for transfers between devices: 1.63 us -> 3.39 us
    pallas_call x1, Pallas kernels: 2.01 us -> 0.83 us  [per_device(): call(functools.partial(prepare_kernel, size_z, (slots_each, fold)), out_s...]
    ppermute x8, waiting for transfers between devices: 0.77 us -> 1.78 us  [swap(): return lax.ppermute(value, axis, sorted(partner.items()))]
    ppermute x3, waiting for transfers between devices: 0.86 us -> 1.6 us  [sum_over(): return value + sum((lax.ppermute(value, axis, table) for table in tables))]
    pallas_call x1, Pallas kernels: 0.63 us -> 0.24 us  [per_device(): call(functools.partial(moment_kernel, dims, counts), out_shape=array((8,...]
  transfers between devices with their start and end apart: 13 -> 13, of which waited for: 3 -> 3; matrix products, arithmetic and copies ran while one was open for 0% -> 0% of each run, Pallas kernels for 15% -> 10%
where the time goes in v6:
time: 37.8 us; the launch traced here: 37.5 us
  starting transfers between devices  12.9 us (34%)
  blocking collectives  12.2 us (32%)
  Pallas kernels  8.02 us (21%)
  waiting for transfers between devices  3.39 us (9%)
  between operations  0.71 us (2%)
    all_to_all x1, blocking collectives, per_device(): lax.all_to_all(columns.reshape(owners, 1, each * lane_tile), ('gx', 'gy')...  12.2 us
    ppermute x8, starting transfers between devices, swap(): return lax.ppermute(value, axis, sorted(partner.items()))  11 us
    ppermute x3, starting transfers between devices, sum_over(): return value + sum((lax.ppermute(value, axis, table) for table in tables))  1.89 us
    ppermute x8, waiting for transfers between devices, swap(): return lax.ppermute(value, axis, sorted(partner.items()))  1.78 us
    ppermute x3, waiting for transfers between devices, sum_over(): return value + sum((lax.ppermute(value, axis, table) for table in tables))  1.6 us
    pallas_call x1, Pallas kernels, per_device(): call(functools.partial(pack_kernel, dims, counts), out_shape=[field_shape...  1.6 us
    pallas_call x1, Pallas kernels, per_device(): call(functools.partial(source_kernel, dims, counts), out_shape=[array((sl...  1.56 us
    pallas_call x1, Pallas kernels, per_device(): call(functools.partial(applied_kernel, dims, counts, slots_each), out_sha...  1.35 us
  transfers between devices with their start and end apart: 13, of which 3 were waited for; matrix products, arithmetic and copies ran while one was open for 0% of the time, Pallas kernels for 10%

profile of v6, /device:TPU:0, one launch (start us, length us, event | category | flops | bytes accessed | tf_op | source)
XLA Modules:
  0.0 37.5 jit_solution(7868157204945579077)
XLA Ops:
  0.6 1.6 %pack.1 = (f32[1024,128]{1,0:T(8,128)S(1)}, f32[4,8,128]{2,1,0:T(8,128)S(1)}, f32[6,8,128]{2,1,0:T(8,128)S(1)}, s32[1,256]{1,0:T(1,128)S(1)}, s32[1,128]{1,0:T(1...) custom-call(f32[32,4,8,128]{3,2,1,0:T(8,128)} %source_ref.1, ...), custom_call_target="tpu_custom_call" | custom-call | tf_op jit(solution)/shard_map/pack/pallas_call | solution.py:618
  2.2 3.1 %collective-permute-start = (f32[264,128]{1,0:T(8,128)S(1)}, f32[264,128]{1,0:T(8,128)S(1)}, u32[]{:S(2)}, u32[]{:S(2)}) collective-permute-start(f32[264,128]{1,0:T(8,128)S(1)} %get-tuple-element.32), channel_id=1, source_target_pairs={{0,16},{16,0},{1,17},{17,1},{2,18},{18,2},{3,19},{19,3},{4,20},{20... | collective-permute-start | bytes 405512 | tf_op jit(solution)/shard_map/ppermute | solution.py:33
  5.3 1.6 %collective-permute-start.1 = (f32[136,128]{1,0:T(8,128)S(1)}, f32[136,128]{1,0:T(8,128)S(1)}, u32[]{:S(2)}, u32[]{:S(2)}) collective-permute-start(f32[136,128]{1,0:T(8,128)S(1)} %get-tuple-element.33), channel_id=1, source_target_pairs={{0,4},{4,0},{8,12},{12,8},{1,5},{5,1},{9,13},{13,9},{2,6},{6,2},{1... | collective-permute-start | bytes 208904 | tf_op jit(solution)/shard_map/ppermute | solution.py:33
  6.9 0.0 collective-permute-start.2
  6.9 0.5 %collective-permute-start.3 = (f32[40,128]{1,0:T(8,128)S(1)}, f32[40,128]{1,0:T(8,128)S(1)}, u32[]{:S(2)}, u32[]{:S(2)}) collective-permute-start(f32[40,128]{1,0:T(8,128)S(1)} %get-tuple-element.35), channel_id=1, source_target_pairs={{0,1},{1,0},{2,3},{3,2},{4,5},{5,4},{6,7},{7,6},{8,9},{9,8},{10,11... | collective-permute-start | bytes 61448 | tf_op jit(solution)/shard_map/ppermute | solution.py:33
  7.4 1.1 %collective-permute-start.4 = (f32[40,128]{1,0:T(8,128)S(1)}, f32[40,128]{1,0:T(8,128)S(1)}, u32[]{:S(2)}, u32[]{:S(2)}) collective-permute-start(f32[40,128]{1,0:T(8,128)S(1)} %get-tuple-element.36), channel_id=1, source_target_pairs={{0,3},{1,2},{2,1},{3,0},{4,7},{5,6},{6,5},{7,4},{8,11},{9,10},{10,... | collective-permute-start | bytes 61448 | tf_op jit(solution)/shard_map/ppermute | solution.py:33
  8.5 0.8 %prepare.1 = (bf16[256,4096]{1,0:T(8,128)(2,1)S(1)}, bf16[512,128]{1,0:T(8,128)(2,1)S(1)}, f32[6,8,128]{2,1,0:T(8,128)S(1)}) custom-call(s32[1,256]{1,0:T(1,128)S(1)} %get-tuple-element.28.voxel_ref, s32[1,128]{1,0:T(1,128)S(1)} %get-tuple-element.29.owned_ref, f32[6,8,128]{2,1,0:T(8,128)S(1)} %get-tuple-element.30.level_ref), custom_call_target="tpu_custom_call" | custom-call | tf_op jit(solution)/shard_map/prepare/pallas_call | solution.py:635
  9.3 0.0 collective-permute-done.3.refs_3_
  9.3 1.3 %collective-permute-done.4.refs_4_ = f32[40,128]{1,0:T(8,128)S(1)} collective-permute-done((f32[40,128]{1,0:T(8,128)S(1)}, f32[40,128]{1,0:T(8,128)S(1)}, u32[]{:S(2)}, u32[]{:S(2)}) %collective-permute-start.4) | collective-permute-done | bytes 20512 | tf_op jit(solution)/shard_map/ppermute | solution.py:33
  10.6 0.0 collective-permute-done.1.refs_1_
  10.6 0.0 collective-permute-done.2.refs_2_
  10.6 0.0 collective-permute-done.refs_0_
  10.6 1.2 %apply.1 = (f32[8,4,8,128]{3,2,1,0:T(8,128)S(1)}, f32[2,32,128]{2,1,0:T(8,128)S(1)}, f32[1024,128]{1,0:T(8,128)S(1)}, f32[256,128]{1,0:T(8,128)S(1)}, f32[128,12...) custom-call(f32[1024,128]{1,0:T(8,128)S(1)} %get-tuple-element.26.rows_ref, ...), custom_call_target="tpu_custom_call" | custom-call | tf_op jit(solution)/shard_map/apply/pallas_call | solution.py:649
  11.9 0.6 %collective-permute-start.5 = (f32[256,128]{1,0:T(8,128)S(1)}, f32[256,128]{1,0:T(8,128)S(1)}, u32[]{:S(2)}, u32[]{:S(2)}) collective-permute-start(f32[256,128]{1,0:T(8,128)S(1)} %get-tuple-element.42), channel_id=1, source_target_pairs={{0,16},{16,0},{1,17},{17,1},{2,18},{18,2},{3,19},{19,3},{4,20},{20... | collective-permute-start | bytes 393224 | tf_op jit(solution)/shard_map/ppermute | solution.py:33
  12.4 2.6 %collective-permute-start.6 = (f32[128,128]{1,0:T(8,128)S(1)}, f32[128,128]{1,0:T(8,128)S(1)}, u32[]{:S(2)}, u32[]{:S(2)}) collective-permute-start(f32[128,128]{1,0:T(8,128)S(1)} %get-tuple-element.43), channel_id=1, source_target_pairs={{0,4},{4,0},{8,12},{12,8},{1,5},{5,1},{9,13},{13,9},{2,6},{6,2},{1... | collective-permute-start | bytes 196616 | tf_op jit(solution)/shard_map/ppermute | solution.py:33
  15.0 0.0 collective-permute-start.7
  15.0 0.5 %collective-permute-start.8 = (f32[32,128]{1,0:T(8,128)S(1)}, f32[32,128]{1,0:T(8,128)S(1)}, u32[]{:S(2)}, u32[]{:S(2)}) collective-permute-start(f32[32,128]{1,0:T(8,128)S(1)} %get-tuple-element.45), channel_id=1, source_target_pairs={{0,1},{1,0},{2,3},{3,2},{4,5},{5,4},{6,7},{7,6},{8,9},{9,8},{10,11... | collective-permute-start | bytes 49160 | tf_op jit(solution)/shard_map/ppermute | solution.py:33
  15.6 1.1 %collective-permute-start.9 = (f32[32,128]{1,0:T(8,128)S(1)}, f32[32,128]{1,0:T(8,128)S(1)}, u32[]{:S(2)}, u32[]{:S(2)}) collective-permute-start(f32[32,128]{1,0:T(8,128)S(1)} %get-tuple-element.46), channel_id=1, source_target_pairs={{0,3},{1,2},{2,1},{3,0},{4,7},{5,6},{6,5},{7,4},{8,11},{9,10},{10,... | collective-permute-start | bytes 49160 | tf_op jit(solution)/shard_map/ppermute | solution.py:33
  16.7 1.6 %source_columns.1 = (f32[256,96]{1,0:T(8,128)S(1)}, f32[128,128]{1,0:T(8,128)S(1)}) custom-call(f32[1024,128]{1,0:T(8,128)S(1)} %get-tuple-element.26.rows_ref, f32[1024,128]{1,0:T(8,128)S(1)} %get-tuple-element.37.applied_ref, f32[8,4,8,128]{3,2,1,0:T(8,128)S(1)} %get-tuple-element.38.weight_ref, bf16[256,4096]{1,0:T(8,128)(2,1)S(1)} %get-tuple-element.39.chosen_ref, ...), custom_call_target="tpu_custom_call" | custom-call | tf_op jit(solution)/shard_map/source_columns/pallas_call | solution.py:660
  18.2 0.0 collective-permute-done.8.refs_3_
  18.2 0.5 %collective-permute-done.9.refs_4_ = f32[32,128]{1,0:T(8,128)S(1)} collective-permute-done((f32[32,128]{1,0:T(8,128)S(1)}, f32[32,128]{1,0:T(8,128)S(1)}, u32[]{:S(2)}, u32[]{:S(2)}) %collective-permute-start.9) | collective-permute-done | bytes 16416 | tf_op jit(solution)/shard_map/ppermute | solution.py:33
  18.7 0.0 collective-permute-done.6.refs_1_
  18.7 0.0 collective-permute-done.7.refs_2_
  18.7 0.0 collective-permute-done.5.refs_0_
  18.7 0.2 moments.1
  19.0 1.2 %collective-permute-start.10 = (f32[8,128]{1,0:T(8,128)S(1)}, f32[8,128]{1,0:T(8,128)S(1)}, u32[]{:S(2)}, u32[]{:S(2)}) collective-permute-start(f32[8,128]{1,0:T(8,128)S(1)} %moments.1), channel_id=1, source_target_pairs={{0,3},{1,2},{2,1},{3,0},{4,7},{5,6},{6,5},{7,4},{8,11},{9,10},{10,... | collective-permute-start | bytes 12296 | tf_op jit(solution)/shard_map/ppermute | solution.py:42
  20.2 0.5 %collective-permute-start.11 = (f32[8,128]{1,0:T(8,128)S(1)}, f32[8,128]{1,0:T(8,128)S(1)}, u32[]{:S(2)}, u32[]{:S(2)}) collective-permute-start(f32[8,128]{1,0:T(8,128)S(1)} %moments.1), channel_id=1, source_target_pairs={{0,2},{1,3},{2,0},{3,1},{4,6},{5,7},{6,4},{7,5},{8,10},{9,11},{10,... | collective-permute-start | bytes 12296 | tf_op jit(solution)/shard_map/ppermute | solution.py:42
  20.7 0.1 collective-permute-start.12
  20.9 1.3 %applied_columns.1 = f32[392,128]{1,0:T(8,128)S(1)} custom-call(f32[1024,128]{1,0:T(8,128)S(1)} %get-tuple-element.37.applied_ref, f32[8,4,8,128]{3,2,1,0:T(8,128)S(1)} %get-tuple-element.38.weight_ref, bf16[256,4096]{1,0:T(8,128)(2,1)S(1)} %get-tuple-element.39.chosen_ref, f32[256,96]{1,0:T(8,128)S(1)} %get-tuple-element.47.source_column_ref, ...), custom_call_target="tpu_custom_call" | custom-call | tf_op jit(solution)/shard_map/applied_columns/pallas_call | solution.py:679
  22.2 0.0 collective-permute-done.10
  22.2 1.6 %collective-permute-done.11 = f32[8,128]{1,0:T(8,128)S(1)} collective-permute-done((f32[8,128]{1,0:T(8,128)S(1)}, f32[8,128]{1,0:T(8,128)S(1)}, u32[]{:S(2)}, u32[]{:S(2)}) %collective-permute-start.11) | collective-permute-done | bytes 4128 | tf_op jit(solution)/shard_map/ppermute | solution.py:42
  23.8 0.0 collective-permute-done.12
  23.8 0.2 fusion
  24.1 12.2 %all_to_all.5 = f32[8,1,6272]{2,1,0:T(1,128)S(1)} all-to-all(f32[8,1,6272]{2,1,0:T(1,128)S(1)} %bitcast.7), channel_id=1, replica_groups=mesh['gx'=2,'gy'=4,'gz'=4] {'gx','gy'}, dimensions={0} | all-to-all | bytes 401408 | tf_op jit(solution)/shard_map/all_to_all | solution.py:691
  36.3 1.2 %owner.1 = (f32[3,128,128]{2,1,0:T(8,128)}, f32[6,128]{1,0:T(8,128)}) custom-call(f32[392,128]{1,0:T(8,128)S(1)} %bitcast.6, bf16[512,128]{1,0:T(8,128)(2,1)S(1)} %get-tuple-element.48.chosen_ref, f32[32,128]{1,0:T(8,128)S(1)} %get-tuple-element.49.data_ref), custom_call_target="tpu_custom_call" | custom-call | tf_op jit(solution)/shard_map/owner/pallas_call | solution.py:694
  (4 shorter events, 0.0 us)
Async XLA Ops:
  2.2 8.4 %collective-permute-start = (f32[264,128]{1,0:T(8,128)S(1)}, f32[264,128]{1,0:T(8,128)S(1)}, u32[]{:S(2)}, u32[]{:S(2)}) collective-permute-start(f32[264,128]{1,0:T(8,128)S(1)} %get-tuple-element.32), channel_id=1, source_target_pairs={{0,16},{16,0},{1,17},{17,1},{2,18},{18,2},{3,19},{19,3},{4,20},{20... | collective-permute-start | bytes 405512 | tf_op jit(solution)/shard_map/ppermute | solution.py:33
  5.3 5.3 %collective-permute-start.1 = (f32[136,128]{1,0:T(8,128)S(1)}, f32[136,128]{1,0:T(8,128)S(1)}, u32[]{:S(2)}, u32[]{:S(2)}) collective-permute-start(f32[136,128]{1,0:T(8,128)S(1)} %get-tuple-element.33), channel_id=1, source_target_pairs={{0,4},{4,0},{8,12},{12,8},{1,5},{5,1},{9,13},{13,9},{2,6},{6,2},{1... | collective-permute-start | bytes 208904 | tf_op jit(solution)/shard_map/ppermute | solution.py:33
  6.9 3.8 %collective-permute-start.2 = (f32[136,128]{1,0:T(8,128)S(1)}, f32[136,128]{1,0:T(8,128)S(1)}, u32[]{:S(2)}, u32[]{:S(2)}) collective-permute-start(f32[136,128]{1,0:T(8,128)S(1)} %get-tuple-element.34), channel_id=1, source_target_pairs={{0,1},{1,0},{2,3},{3,2},{4,8},{5,9},{6,10},{7,11},{8,4},{9,5},{10,... | collective-permute-start | bytes 208904 | tf_op jit(solution)/shard_map/ppermute | solution.py:30
  6.9 2.4 %collective-permute-start.3 = (f32[40,128]{1,0:T(8,128)S(1)}, f32[40,128]{1,0:T(8,128)S(1)}, u32[]{:S(2)}, u32[]{:S(2)}) collective-permute-start(f32[40,128]{1,0:T(8,128)S(1)} %get-tuple-element.35), channel_id=1, source_target_pairs={{0,1},{1,0},{2,3},{3,2},{4,5},{5,4},{6,7},{7,6},{8,9},{9,8},{10,11... | collective-permute-start | bytes 61448 | tf_op jit(solution)/shard_map/ppermute | solution.py:33
  7.4 3.2 %collective-permute-start.4 = (f32[40,128]{1,0:T(8,128)S(1)}, f32[40,128]{1,0:T(8,128)S(1)}, u32[]{:S(2)}, u32[]{:S(2)}) collective-permute-start(f32[40,128]{1,0:T(8,128)S(1)} %get-tuple-element.36), channel_id=1, source_target_pairs={{0,3},{1,2},{2,1},{3,0},{4,7},{5,6},{6,5},{7,4},{8,11},{9,10},{10,... | collective-permute-start | bytes 61448 | tf_op jit(solution)/shard_map/ppermute | solution.py:33
  11.9 6.9 %collective-permute-start.5 = (f32[256,128]{1,0:T(8,128)S(1)}, f32[256,128]{1,0:T(8,128)S(1)}, u32[]{:S(2)}, u32[]{:S(2)}) collective-permute-start(f32[256,128]{1,0:T(8,128)S(1)} %get-tuple-element.42), channel_id=1, source_target_pairs={{0,16},{16,0},{1,17},{17,1},{2,18},{18,2},{3,19},{19,3},{4,20},{20... | collective-permute-start | bytes 393224 | tf_op jit(solution)/shard_map/ppermute | solution.py:33
  12.4 6.3 %collective-permute-start.6 = (f32[128,128]{1,0:T(8,128)S(1)}, f32[128,128]{1,0:T(8,128)S(1)}, u32[]{:S(2)}, u32[]{:S(2)}) collective-permute-start(f32[128,128]{1,0:T(8,128)S(1)} %get-tuple-element.43), channel_id=1, source_target_pairs={{0,4},{4,0},{8,12},{12,8},{1,5},{5,1},{9,13},{13,9},{2,6},{6,2},{1... | collective-permute-start | bytes 196616 | tf_op jit(solution)/shard_map/ppermute | solution.py:33
  15.0 3.7 %collective-permute-start.7 = (f32[128,128]{1,0:T(8,128)S(1)}, f32[128,128]{1,0:T(8,128)S(1)}, u32[]{:S(2)}, u32[]{:S(2)}) collective-permute-start(f32[128,128]{1,0:T(8,128)S(1)} %get-tuple-element.44), channel_id=1, source_target_pairs={{0,1},{1,0},{2,3},{3,2},{4,8},{5,9},{6,10},{7,11},{8,4},{9,5},{10,... | collective-permute-start | bytes 196616 | tf_op jit(solution)/shard_map/ppermute | solution.py:30
  15.0 3.2 %collective-permute-start.8 = (f32[32,128]{1,0:T(8,128)S(1)}, f32[32,128]{1,0:T(8,128)S(1)}, u32[]{:S(2)}, u32[]{:S(2)}) collective-permute-start(f32[32,128]{1,0:T(8,128)S(1)} %get-tuple-element.45), channel_id=1, source_target_pairs={{0,1},{1,0},{2,3},{3,2},{4,5},{5,4},{6,7},{7,6},{8,9},{9,8},{10,11... | collective-permute-start | bytes 49160 | tf_op jit(solution)/shard_map/ppermute | solution.py:33
  15.6 3.2 %collective-permute-start.9 = (f32[32,128]{1,0:T(8,128)S(1)}, f32[32,128]{1,0:T(8,128)S(1)}, u32[]{:S(2)}, u32[]{:S(2)}) collective-permute-start(f32[32,128]{1,0:T(8,128)S(1)} %get-tuple-element.46), channel_id=1, source_target_pairs={{0,3},{1,2},{2,1},{3,0},{4,7},{5,6},{6,5},{7,4},{8,11},{9,10},{10,... | collective-permute-start | bytes 49160 | tf_op jit(solution)/shard_map/ppermute | solution.py:33
  19.0 3.3 %collective-permute-start.10 = (f32[8,128]{1,0:T(8,128)S(1)}, f32[8,128]{1,0:T(8,128)S(1)}, u32[]{:S(2)}, u32[]{:S(2)}) collective-permute-start(f32[8,128]{1,0:T(8,128)S(1)} %moments.1), channel_id=1, source_target_pairs={{0,3},{1,2},{2,1},{3,0},{4,7},{5,6},{6,5},{7,4},{8,11},{9,10},{10,... | collective-permute-start | bytes 12296 | tf_op jit(solution)/shard_map/ppermute | solution.py:42
  20.2 3.6 %collective-permute-start.11 = (f32[8,128]{1,0:T(8,128)S(1)}, f32[8,128]{1,0:T(8,128)S(1)}, u32[]{:S(2)}, u32[]{:S(2)}) collective-permute-start(f32[8,128]{1,0:T(8,128)S(1)} %moments.1), channel_id=1, source_target_pairs={{0,2},{1,3},{2,0},{3,1},{4,6},{5,7},{6,4},{7,5},{8,10},{9,11},{10,... | collective-permute-start | bytes 12296 | tf_op jit(solution)/shard_map/ppermute | solution.py:42
  20.7 3.1 %collective-permute-start.12 = (f32[8,128]{1,0:T(8,128)S(1)}, f32[8,128]{1,0:T(8,128)S(1)}, u32[]{:S(2)}, u32[]{:S(2)}) collective-permute-start(f32[8,128]{1,0:T(8,128)S(1)} %moments.1), channel_id=1, source_target_pairs={{0,1},{1,0},{2,3},{3,2},{4,5},{5,4},{6,7},{7,6},{8,9},{9,8},{10,11... | collective-permute-start | bytes 12296 | tf_op jit(solution)/shard_map/ppermute | solution.py:42

commit v7 on v6

--- a/solution.py
+++ b/solution.py
@@ -46,9 +46,9 @@
     return [1 if lax.axis_size(axis) <= 2 else 2 for axis in axes]
 
 
-def exchange_all(faces, counts):
+def exchange_all(groups):
     halos = []
-    for axis, group in zip(axes, split_refs(faces, counts)):
+    for axis, group in zip(axes, groups):
         if lax.axis_size(axis) > 1:
             group = [swap(face, axis, odd) for odd, face in enumerate(group)]
         halos.extend(group)
@@ -57,7 +57,7 @@
 
 def sort_halos(halo_refs, held_refs, counts):
     sorted_refs, held_refs = [], list(held_refs)
-    for axis, group in zip(axes, split_refs(halo_refs, counts)):
+    for axis, group in zip(axes, split_refs(halo_refs, counts[:2])):
         if len(group) == 1:
             sorted_refs.append((group[0], group[0]))
             continue
@@ -70,10 +70,22 @@
     return sorted_refs
 
 
+def sort_ends(z_refs):
+    below = above = z_refs[0][...]
+    if len(z_refs) == 2:
+        even = lax.axis_index("gz") % 2 == 0
+        below, above = (
+            jnp.where(even, z_refs[1 - k][...], z_refs[k][...]) for k in range(2)
+        )
+    half = below.shape[1] // 2
+    lane_index = lax.broadcasted_iota(jnp.int32, below.shape, 1)
+    return pltpu.roll(jnp.where(lane_index < half, above, below), half, 1)
+
+
 def held_halos(faces, counts):
     return [
         pltpu.VMEM(face.shape, face.dtype)
-        for group in split_refs(faces, counts)
+        for group in split_refs(faces, counts[:2])
         for face in (group if len(group) == 2 else [])
     ]
 
@@ -90,9 +102,9 @@
     return flags
 
 
-def write_faces(dims, rows_ref, face_refs, z_ends, extra=None):
-    sensors, size_x, size_y, size_z = dims
-    x_refs, y_refs, z_refs = face_refs
+def write_faces(dims, rows_ref, face_refs, labels=None, beyond=None):
+    sensors, size_x, size_y, size_z = dims
+    x_refs, y_refs = face_refs
 
     def field(r):
         return rows_ref[pl.ds(pl.multiple_of(r * sensors, sensors), sensors), :]
@@ -105,40 +117,55 @@
         x = jnp.where(high, size_x - 1, 0)
         for y in range(size_y):
             ref[y * sensors : (y + 1) * sensors, :] = field(x * size_y + y)
-        if extra is not None:
-            ref[size_y * sensors : size_y * (sensors + 1), :] = jnp.where(high, extra[-1], extra[0])
+        if labels is not None:
+            ref[size_y * sensors :, :] = jnp.where(high, labels[-1], labels[0])
+        else:
+            ref[size_y * sensors :, :] = beyond
 
     for number, ref in enumerate(y_refs):
         high = high_end("gy", number)
         y = jnp.where(high, size_y - 1, 0)
         for x in range(size_x):
             ref[x * sensors : (x + 1) * sensors, :] = field(x * size_y + y)
-            if extra is not None:
+            if labels is not None:
                 row = size_x * sensors + x
-                ref[row : row + 1, :] = jnp.where(high, extra[x][size_y - 1 :, :], extra[x][0:1, :])
-
-    ends = z_ends
-    if extra is not None:
-        ends = []
-        for z, packed in zip((0, size_z - 1), z_ends):
-            labels = jnp.zeros((size_y, packed.shape[1]), jnp.float32)
-            for x in range(size_x):
-                labels = jnp.where(lanes_equal(labels.shape, x), extra[x][:, z : z + 1], labels)
-            ends.append(jnp.concatenate([packed, labels], axis=0))
-    for number, ref in enumerate(z_refs):
-        ref[...] = jnp.where(high_end("gz", number), ends[1], ends[0])
-
-
-def pack_ends(dims, rows_ref, lanes):
-    sensors, size_x, size_y, size_z = dims
-    ends = []
-    for z in (0, size_z - 1):
-        packed = jnp.zeros((sensors, lanes), jnp.float32)
-        for r in range(size_x * size_y):
-            row = rows_ref[r * sensors : (r + 1) * sensors, :]
-            packed = jnp.where(lanes_equal(packed.shape, r), row[:, z : z + 1], packed)
-        ends.append(packed)
-    return ends
+                ref[row : row + 1, :] = jnp.where(high, labels[x][size_y - 1 :, :], labels[x][0:1, :])
+        if labels is None:
+            ref[size_x * sensors :, :] = beyond
+
+
+def put_lanes(packed, row, source, target, count):
+    lanes = packed.shape[1]
+    moved = pltpu.roll(row, (target - source) % lanes, 1)
+    lane_index = lax.broadcasted_iota(jnp.int32, packed.shape, 1)
+    return jnp.where((lane_index >= target) & (lane_index < target + count), moved, packed)
+
+
+def pack_lines(dims, values, depth, low_shift):
+    size_x, size_y, size_z = dims[1:]
+    half = size_z // 2
+    packed = jnp.zeros((size_y, size_z), jnp.float32)
+    row_index = lax.broadcasted_iota(jnp.int32, packed.shape, 0)
+    for x in range(size_x):
+        line = 2 * (x * size_y + row_index)
+        for p in range(depth):
+            low, high = values[x]
+            end = size_z - depth + p
+            packed = jnp.where(lanes_equal(packed.shape, line + low_shift + p), low[:, p : p + 1], packed)
+            packed = jnp.where(lanes_equal(packed.shape, line + half + p), high[:, end : end + 1], packed)
+    return jnp.broadcast_to(jnp.sum(packed, axis=0, keepdims=True), (8, size_z))
+
+
+def pack_rows(dims, rows_ref, depth, low_shift):
+    sensors, size_x, size_y, size_z = dims
+    half = size_z // 2
+    assert 2 * size_x * size_y <= half
+    packed = jnp.zeros((sensors, size_z), jnp.float32)
+    for r in range(size_x * size_y):
+        row = rows_ref[r * sensors : (r + 1) * sensors, :]
+        packed = put_lanes(packed, row, 0, 2 * r + low_shift, depth)
+        packed = put_lanes(packed, row, size_z - depth, half + 2 * r, depth)
+    return packed
 
 
 def split_refs(refs, counts):
@@ -153,8 +180,9 @@
     sensors, size_x, size_y, size_z = dims
     small_hbm, refs = refs[:4], refs[4:]
     (rows_ref, shifted_ref, table_ref), small_refs = refs[:3], refs[3:6]
-    face_refs = refs[6 : 6 + sum(counts)]
-    staged_ref, label_vmem, level_ref, semaphores = refs[6 + sum(counts) :]
+    own_ref, refs = refs[6], refs[7:]
+    face_refs = split_refs(refs[: sum(counts[:2])], counts[:2])
+    staged_ref, label_vmem, level_ref, semaphores = refs[sum(counts[:2]) :]
     copies = [
         pltpu.make_async_copy(source_ref.at[:, x], staged_ref.at[x], semaphores.at[x])
         for x in range(size_x)
@@ -177,9 +205,9 @@
         for y in range(size_y):
             r = x * size_y + y
             rows_ref[r * sensors : (r + 1) * sensors, :] = flat[x, pl.ds(y, sensors, stride=size_y), :]
-    face_refs = split_refs(face_refs, counts)
-    z_ends = pack_ends(dims, rows_ref, face_refs[2][0].shape[1])
-    write_faces(dims, rows_ref, face_refs, z_ends, shifted)
+    write_faces(dims, rows_ref, face_refs, labels=shifted)
+    own_ref[0:sensors, :] = pack_rows(dims, rows_ref, 2, 0)
+    own_ref[sensors:, :] = pack_lines(dims, [(plane, plane) for plane in shifted], 2, 0)
 
 
 def prepare_kernel(
@@ -220,7 +248,8 @@
 def tissue(shifted, table_ref):
     conductivity = jnp.zeros_like(shifted)
     for level in range(table_ref.shape[0]):
-        conductivity = jnp.where(shifted == level + 1, table_ref[level], conductivity)
+        value = table_ref[level] if shifted.shape == table_ref.shape[1:] else table_ref[level, 0:1, 0:1]
+        conductivity = jnp.where(shifted == level + 1, value, conductivity)
     return conductivity, (shifted > 0).astype(jnp.float32)
 
 
@@ -228,10 +257,17 @@
     return 0.5 * (first[0] + second[0]) * first[1] * second[1]
 
 
-def weights(dims, shifted_ref, table_ref, halo_refs, weight_ref):
+def weights(dims, shifted_ref, table_ref, halo_refs, z_ref, weight_ref):
     sensors, size_x, size_y, size_z = dims
     flags = neighbour_flags()
-    (x_low, x_high), (y_low, y_high), (z_low, z_high) = halo_refs
+    (x_low, x_high), (y_low, y_high) = halo_refs
+    beyond = z_ref[sensors : sensors + 1, :]
+    half = size_z // 2
+
+    def beyond_end(x, first, flag):
+        line = 2 * (x * size_y + row_index) + first
+        picked = jnp.where(lanes_equal(row_index.shape, line), beyond, 0.0)
+        return masked(jnp.sum(picked, axis=1, keepdims=True), flag)
 
     def masked(value, flag):
         return jnp.where(flag, value, 0.0)
@@ -258,15 +294,14 @@
             masked(y_high[y_row : y_row + 1, :], flags[1][1]),
             pltpu.roll(shifted, size_y - 1, 0),
         )
-        z_rows = slice(sensors, sensors + size_y)
         z_before = jnp.where(
             lane_index == 0,
-            masked(z_low[z_rows, x : x + 1], flags[2][0]),
+            beyond_end(x, 1, flags[2][0]),
             pltpu.roll(shifted, 1, 1),
         )
         z_after = jnp.where(
             lane_index == size_z - 1,
-            masked(z_high[z_rows, x : x + 1], flags[2][1]),
+            beyond_end(x, half, flags[2][1]),
             pltpu.roll(shifted, size_z - 1, 1),
         )
         six = [across_x[x], across_x[x + 1]]
@@ -278,10 +313,13 @@
         weight_ref[7, x] = 0.5 * own_tissue[x][0]
 
 
-def around(dims, rows_ref, halo_refs, r, flags=None):
-    sensors, size_x, size_y, size_z = dims
-    (x_low, x_high), (y_low, y_high), (z_low, z_high) = halo_refs
+def around(dims, rows_ref, halo_refs, z_ref, r, flags=None):
+    sensors, size_x, size_y, size_z = dims
+    (x_low, x_high), (y_low, y_high) = halo_refs
     x, y = divmod(r, size_y)
+    z_low = z_ref[0:sensors, 2 * r + 1 : 2 * r + 2]
+    high_lane = size_z // 2 + 2 * r
+    z_high = z_ref[0:sensors, high_lane : high_lane + 1]
 
     def keep(value, dim, end):
         return value if flags is None else jnp.where(flags[dim][end], value, 0.0)
@@ -299,11 +337,11 @@
     y_after = row(r + 1) if y < size_y - 1 else keep(part(y_high, x), 1, 1)
     lane_index = lax.broadcasted_iota(jnp.int32, centre.shape, 1)
     z_before = jnp.where(
-        lane_index == 0, keep(z_low[0:sensors, r : r + 1], 2, 0), pltpu.roll(centre, 1, 1)
+        lane_index == 0, keep(z_low, 2, 0), pltpu.roll(centre, 1, 1)
     )
     z_after = jnp.where(
         lane_index == size_z - 1,
-        keep(z_high[0:sensors, r : r + 1], 2, 1),
+        keep(z_high, 2, 1),
         pltpu.roll(centre, size_z - 1, 1),
     )
     return centre, (x_before, x_after, y_before, y_after, z_before, z_after)
@@ -318,24 +356,20 @@
 
 def apply_kernel(dims, counts, rows_ref, shifted_ref, table_ref, *refs):
     sensors, size_x, size_y, size_z = dims
-    messages = sum(counts)
-    halo_refs = sort_halos(refs[:messages], refs[2 * messages + 3 :], counts)
-    weight_ref, end_ref, applied_ref = refs[messages : messages + 3]
-    face_refs = split_refs(refs[messages + 3 : 2 * messages + 3], counts)
-    weights(dims, shifted_ref, table_ref, halo_refs, weight_ref)
+    message_refs, refs = refs[: sum(counts)], refs[sum(counts) :]
+    weight_ref, end_ref, applied_ref, z_ref = refs[:4]
+    face_refs = split_refs(refs[4 : 4 + sum(counts[:2])], counts[:2])
+    halo_refs = sort_halos(message_refs, refs[4 + sum(counts[:2]) :], counts)
+    z_ref[...] = sort_ends(message_refs[sum(counts[:2]) :])
+    weights(dims, shifted_ref, table_ref, halo_refs, z_ref, weight_ref)
     for r in range(size_x * size_y):
         x, y = divmod(r, size_y)
-        centre, beside = around(dims, rows_ref, halo_refs, r)
+        centre, beside = around(dims, rows_ref, halo_refs, z_ref, r)
         applied_ref[r * sensors : (r + 1) * sensors, :] = combine(weight_ref, x, y, centre, beside)
-    z_ends = pack_ends(dims, applied_ref, end_ref.shape[2])
-    write_faces(dims, applied_ref, face_refs, z_ends)
-    for end, (k, z) in enumerate(((4, 0), (5, size_z - 1))):
-        packed = jnp.zeros((size_y, end_ref.shape[2]), jnp.float32)
-        row_index = lax.broadcasted_iota(jnp.int32, packed.shape, 0)
-        for x in range(size_x):
-            here = lanes_equal(packed.shape, row_index + x * size_y)
-            packed = jnp.where(here, weight_ref[k, x][:, z : z + 1], packed)
-        end_ref[end] = jnp.sum(packed, axis=0, keepdims=True) * z_ends[end]
+    write_faces(dims, applied_ref, face_refs, beyond=z_ref[...])
+    lines = [(weight_ref[4, x], weight_ref[5, x]) for x in range(size_x)]
+    outward = pack_lines(dims, lines, 1, 1)
+    end_ref[...] = outward[0:1, :] * pack_rows(dims, applied_ref, 1, 1)
 
 
 def halves(value):
@@ -369,7 +403,7 @@
     return total - weight(4) * before - weight(5) * after
 
 
-def select_columns(dims, rows_ref, weight_ref, halo_refs, chosen_ref, parts_ref):
+def select_columns(dims, rows_ref, weight_ref, halo_refs, z_ref, chosen_ref, parts_ref):
     sensors, size_x, size_y, size_z = dims
     flags = neighbour_flags()
     width = 3 * sensors
@@ -377,7 +411,7 @@
         x, y = divmod(r, size_y)
         span = slice(r * size_z, (r + 1) * size_z)
         scale = weight_ref[7, x, y : y + 1, :]
-        _, beside = around(dims, rows_ref, halo_refs, r, flags)
+        _, beside = around(dims, rows_ref, halo_refs, z_ref, r, flags)
         for c in range(3):
             high, low = halves(scale * (beside[2 * c + 1] - beside[2 * c]))
             parts_ref[c * sensors : (c + 1) * sensors, span] = high
@@ -388,9 +422,9 @@
     return found[:, :width] + found[:, width:]
 
 
-def source_kernel(dims, counts, rows_ref, applied_ref, weight_ref, chosen_ref, *refs):
-    sensors, size_x, size_y, size_z = dims
-    messages = sum(counts)
+def source_kernel(dims, counts, rows_ref, applied_ref, weight_ref, chosen_ref, z_ref, *refs):
+    sensors, size_x, size_y, size_z = dims
+    messages = sum(counts[:2])
     column_ref, sum_ref, parts_ref = refs[messages : messages + 3]
     halo_refs = sort_halos(refs[:messages], refs[messages + 3 :], counts)
     sums = [jnp.zeros((sensors, size_z), jnp.float32) for _ in range(4)]
@@ -405,16 +439,70 @@
     for k in range(4):
         sum_ref[k * sensors : (k + 1) * sensors, :] = sums[k]
     column_ref[...] = select_columns(
-        dims, rows_ref, weight_ref, halo_refs, chosen_ref, parts_ref
-    )
-
-
-def moment_kernel(dims, counts, applied_ref, weight_ref, sum_ref, end_ref, *refs):
-    sensors, size_x, size_y, size_z = dims
-    messages = sum(counts)
-    moment_ref = refs[messages]
-    halo_refs = sort_halos(refs[:messages], refs[messages + 1 :], counts)
-    (x_low, x_high), (y_low, y_high), (z_low, z_high) = halo_refs
+        dims, rows_ref, weight_ref, halo_refs, z_ref, chosen_ref, parts_ref
+    )
+
+
+def packed_beside(dims, beyond, own, along_x, along_y):
+    sensors, size_x, size_y, size_z = dims
+    half = size_z // 2
+    lane_index = lax.broadcasted_iota(jnp.int32, beyond.shape, 1)
+    in_half = lane_index % half
+    row = in_half // 2 % size_y
+
+    def moved(value, lanes):
+        return pltpu.roll(value, lanes % size_z, 1)
+
+    def either(condition, value, lanes, other, back):
+        return jnp.where(condition, moved(value, lanes), moved(other, back))
+
+    step, wrap = 2 * size_y, 2 * size_y * (size_x - 1)
+    return (
+        either(in_half >= step, beyond, step, along_x[0], -wrap),
+        either(in_half < wrap, beyond, -step, along_x[1], wrap),
+        either(row > 0, beyond, 2, along_y[0], -2 * (size_y - 1)),
+        either(row < size_y - 1, beyond, -2, along_y[1], 2 * (size_y - 1)),
+        either(lane_index < half, beyond, 1, beyond, -1),
+        either(lane_index < half, own, 1, own, -1),
+    )
+
+
+def moment_kernel(
+    dims, counts, applied_ref, weight_ref, sum_ref, end_ref, own_ref, z_ref, table_ref, *refs
+):
+    sensors, size_x, size_y, size_z = dims
+    messages = sum(counts[:2])
+    moment_ref, plane_ref = refs[messages : messages + 2]
+    halo_refs = sort_halos(refs[:messages], refs[messages + 2 :], counts)
+    (x_low, x_high), (y_low, y_high) = halo_refs
+    flags = neighbour_flags()
+
+    def forwarded(pair, dim, first, last):
+        start = (size_y, size_x)[dim] * sensors
+        return [
+            jnp.where(flags[dim][end], ref[start + first : start + last, :], 0.0)
+            for end, ref in enumerate(pair)
+        ]
+
+    def of_lines(first, last):
+        return packed_beside(
+            dims,
+            z_ref[first:last, :],
+            own_ref[first:last, :],
+            forwarded(halo_refs[0], 0, first, last),
+            forwarded(halo_refs[1], 1, first, last),
+        )
+
+    middle = tissue(z_ref[sensors:, :], table_ref)
+    six = [
+        edge_weight(middle, tissue(label, table_ref))
+        for label in of_lines(sensors, z_ref.shape[0])
+    ]
+    total = mass_term + (six[0] + six[1]) + (six[2] + six[3]) + (six[4] + six[5])
+    plane = total[0:1, :] * z_ref[0:sensors, :]
+    for weight, value in zip(six, of_lines(0, sensors)):
+        plane = plane - weight[0:1, :] * value
+    plane_ref[...] = plane
 
     def part(ref, index):
         return ref[index * sensors : (index + 1) * sensors, :]
@@ -430,13 +518,7 @@
     for x in range(size_x):
         outward = outward + crossing(2, x * size_y, part(y_low, x))
         outward = outward + crossing(3, x * size_y + size_y - 1, part(y_high, x))
-    crossed = end_ref[0] * z_low[0:sensors, :] + end_ref[1] * z_high[0:sensors, :]
-    for first in range(0, crossed.shape[1], size_z):
-        piece = crossed[:, first : first + size_z]
-        spare = size_z - piece.shape[1]
-        if spare:
-            piece = jnp.concatenate([piece, jnp.zeros((sensors, spare), jnp.float32)], axis=1)
-        outward = outward + piece
+    outward = outward + end_ref[...] * plane
     last = part(sum_ref, 3) - outward
     moment_ref[...] = lax.dot_general(
         jnp.ones((8, size_z), jnp.float32),
@@ -456,13 +538,13 @@
 
 
 def applied_kernel(
-    dims, counts, slots_each, applied_ref, weight_ref, chosen_ref, source_column_ref, *refs
+    dims, counts, slots_each, applied_ref, weight_ref, chosen_ref, source_column_ref, z_ref, *refs
 ):
-    sensors, messages = dims[0], sum(counts)
+    sensors, messages = dims[0], sum(counts[:2])
     column_ref, parts_ref = refs[messages : messages + 2]
     halo_refs = sort_halos(refs[:messages], refs[messages + 2 :], counts)
     applied_columns = select_columns(
-        dims, applied_ref, weight_ref, halo_refs, chosen_ref, parts_ref
+        dims, applied_ref, weight_ref, halo_refs, z_ref, chosen_ref, parts_ref
     )
     columns = jnp.concatenate([source_column_ref[...], applied_columns], axis=1)
     whole, rest, fold, rows, moment_rows = payload_rows(sensors, slots_each)
@@ -573,17 +655,12 @@
     return [pl.BlockSpec(memory_space=pltpu.VMEM)] * count
 
 
-def face_shapes(dims, counts, with_labels):
-    sensors, size_x, size_y, size_z = dims
-    lanes = -(-size_x * size_y // lane_tile) * lane_tile
-    shapes = (
-        (size_y * (sensors + with_labels), size_z),
-        (size_x * sensors + 8 * with_labels * -(-size_x // 8), size_z),
-        (sensors + size_y * with_labels, lanes),
-    )
+def face_shapes(dims, counts, x_rows, y_rows):
+    sensors, size_x, size_y, size_z = dims
+    rows = (size_y * sensors + x_rows, size_x * sensors + y_rows)
     return [
-        jax.ShapeDtypeStruct(shape, jnp.float32)
-        for shape, count in zip(shapes, counts)
+        jax.ShapeDtypeStruct((row, size_z), jnp.float32)
+        for row, count in zip(rows, counts)
         for _ in range(count)
     ]
 
@@ -593,7 +670,7 @@
     sensors, size_x, size_y, size_z = dims
     rows_count = size_x * size_y
     counts = face_counts()
-    messages = sum(counts)
+    messages = sum(counts[:2])
     owners = lax.axis_size("gx") * lax.axis_size("gy")
     slots = send_map.size
     slots_each = slots // owners
@@ -608,6 +685,7 @@
 
     parts = [pltpu.VMEM((6 * sensors, voxels), jnp.bfloat16)]
     field_shape = array((rows_count * sensors, size_z))
+    ends_shape = array((sensors + 8, size_z))
     levels = conductivity_table.shape[0]
     small = (
         send_map.reshape(1, slots),
@@ -619,9 +697,10 @@
         functools.partial(pack_kernel, dims, counts),
         out_shape=[field_shape, array(labels.shape), array((levels, size_y, size_z))]
         + [array(value.shape, value.dtype) for value in small[:3]]
-        + face_shapes(dims, counts, 1),
+        + [ends_shape]
+        + face_shapes(dims, counts, size_y, 8 * -(-size_x // 8)),
         in_specs=in_hbm(6),
-        out_specs=in_vmem(6 + messages),
+        out_specs=in_vmem(7 + messages),
         scratch_shapes=[
             pltpu.VMEM((size_x, sensors, size_y, size_z), jnp.float32),
             pltpu.VMEM((size_x, size_y, size_z), jnp.int32),
@@ -630,8 +709,8 @@
         ],
         name="pack",
     )(*held_in_hbm(source_term, labels, *small))
-    rows, shifted, table, voxel, owned, data, *faces = packed
-    source_halos = exchange_all(faces, counts)
+    rows, shifted, table, voxel, owned, data, own_ends, *faces = packed
+    source_halos = exchange_all([*split_refs(faces, counts[:2]), [own_ends] * counts[2]])
     chosen, owned_chosen, table = call(
         functools.partial(prepare_kernel, size_z, (slots_each, fold)),
         out_shape=[
@@ -644,46 +723,46 @@
         name="prepare",
     )(voxel, owned, table)
 
-    faces_out = face_shapes(dims, counts, 0)
-    end_shape = (2, *faces_out[-1].shape)
     result = call(
         functools.partial(apply_kernel, dims, counts),
-        out_shape=[array((8, size_x, size_y, size_z)), array(end_shape), field_shape] + faces_out,
-        in_specs=in_vmem(3 + messages),
-        out_specs=in_vmem(3 + messages),
+        out_shape=[array((8, size_x, size_y, size_z)), array((sensors, size_z)), field_shape]
+        + [ends_shape]
+        + face_shapes(dims, counts, sensors + 8, sensors + 8),
+        in_specs=in_vmem(3 + messages + counts[2]),
+        out_specs=in_vmem(4 + messages),
         scratch_shapes=held_halos(source_halos, counts),
         name="apply",
     )(rows, shifted, table, *source_halos)
-    weight, ends, applied, faces = *result[:3], result[3:]
-    applied_halos = exchange_all(faces, counts)
+    weight, ends, applied, beyond, *faces = result
+    applied_halos = exchange_all(split_refs(faces, counts[:2]))
 
     source_columns, sums = call(
         functools.partial(source_kernel, dims, counts),
         out_shape=[array((slots, 3 * sensors)), array((4 * sensors, size_z))],
-        in_specs=in_vmem(4 + messages),
+        in_specs=in_vmem(5 + messages),
         out_specs=in_vmem(2),
         scratch_shapes=parts + held_halos(source_halos, counts),
         name="source_columns",
-    )(rows, applied, weight, chosen, *source_halos)
-    moment = call(
+    )(rows, applied, weight, chosen, beyond, *source_halos[:messages])
+    moment, plane = call(
         functools.partial(moment_kernel, dims, counts),
-        out_shape=array((8, 4 * sensors)),
-        in_specs=in_vmem(4 + messages),
-        out_specs=in_vmem(1)[0],
+        out_shape=[array((8, 4 * sensors)), array((sensors, size_z))],
+        in_specs=in_vmem(7 + messages),
+        out_specs=in_vmem(2),
         scratch_shapes=held_halos(applied_halos, counts),
         name="moments",
-    )(applied, weight, sums, ends, *applied_halos)
+    )(applied, weight, sums, ends, own_ends, beyond, table, *applied_halos)
     moment = sum_over(moment, "gz")
 
     each = payload + moment_rows
     columns = call(
         functools.partial(applied_kernel, dims, counts, slots_each),
         out_shape=array((owners * each, lane_tile)),
-        in_specs=in_vmem(4 + messages),
+        in_specs=in_vmem(5 + messages),
         out_specs=in_vmem(1)[0],
         scratch_shapes=parts + held_halos(applied_halos, counts),
         name="applied_columns",
-    )(applied, weight, chosen, source_columns, *applied_halos)
+    )(applied, weight, chosen, source_columns, plane, *applied_halos)
     place = lax.broadcasted_iota(jnp.int32, columns.shape, 0) % each
     stamp = jnp.pad(moment[0], (0, moment_rows * lane_tile - 4 * sensors)).reshape(-1, lane_tile)
     for row in range(moment_rows):

time: 37.8 us -> 37.6 us (level)
  starting transfers between devices: 12.9 us -> 11.6 us
  waiting for transfers between devices: 3.39 us -> 4.15 us
  Pallas kernels: 8.02 us -> 8.47 us
    ppermute x8 -> x6, starting transfers between devices: 11 us -> 9.4 us  [swap(): return lax.ppermute(value, axis, sorted(partner.items()))]
    ppermute x8 -> x6, waiting for transfers between devices: 1.78 us -> 2.53 us  [swap(): return lax.ppermute(value, axis, sorted(partner.items()))]
  transfers between devices with their start and end apart: 13 -> 11, of which waited for: 3 -> 3; matrix products, arithmetic and copies ran while one was open for 0% -> 0% of each run, Pallas kernels for 10% -> 11%
where the time goes in v7:
time: 37.6 us; the launch traced here: 37.3 us
  blocking collectives  12.2 us (32%)
  starting transfers between devices  11.6 us (31%)
  Pallas kernels  8.47 us (23%)
  waiting for transfers between devices  4.15 us (11%)
  between operations  0.7 us (2%)
    all_to_all x1, blocking collectives, per_device(): lax.all_to_all(columns.reshape(owners, 1, each * lane_tile), ('gx', 'gy')...  12.2 us
    ppermute x6, starting transfers between devices, swap(): return lax.ppermute(value, axis, sorted(partner.items()))  9.4 us
    ppermute x6, waiting for transfers between devices, swap(): return lax.ppermute(value, axis, sorted(partner.items()))  2.53 us
    ppermute x3, starting transfers between devices, sum_over(): return value + sum((lax.ppermute(value, axis, table) for table in tables))  2.17 us
    pallas_call x1, Pallas kernels, per_device(): call(functools.partial(source_kernel, dims, counts), out_shape=[array((sl...  1.68 us
    pallas_call x1, Pallas kernels, per_device(): call(functools.partial(pack_kernel, dims, counts), out_shape=[field_shape...  1.64 us
    ppermute x3, waiting for transfers between devices, sum_over(): return value + sum((lax.ppermute(value, axis, table) for table in tables))  1.61 us
    pallas_call x1, Pallas kernels, per_device(): call(functools.partial(applied_kernel, dims, counts, slots_each), out_sha...  1.44 us
  transfers between devices with their start and end apart: 11, of which 3 were waited for; matrix products, arithmetic and copies ran while one was open for 0% of the time, Pallas kernels for 11%

profile of v7, /device:TPU:0, one launch (start us, length us, event | category | flops | bytes accessed | tf_op | source)
XLA Modules:
  0.0 37.3 jit_solution(16798449417751804305)
XLA Ops:
  0.6 1.6 %pack.1 = (f32[1024,128]{1,0:T(8,128)S(1)}, f32[4,8,128]{2,1,0:T(8,128)S(1)}, f32[6,8,128]{2,1,0:T(8,128)S(1)}, s32[1,256]{1,0:T(1,128)S(1)}, s32[1,128]{1,0:T(1...) custom-call(f32[32,4,8,128]{3,2,1,0:T(8,128)} %source_ref.1, ...), custom_call_target="tpu_custom_call" | custom-call | tf_op jit(solution)/shard_map/pack/pallas_call | solution.py:696
  2.3 3.1 %collective-permute-start = (f32[264,128]{1,0:T(8,128)S(1)}, f32[264,128]{1,0:T(8,128)S(1)}, u32[]{:S(2)}, u32[]{:S(2)}) collective-permute-start(f32[264,128]{1,0:T(8,128)S(1)} %get-tuple-element.32), channel_id=1, source_target_pairs={{0,16},{16,0},{1,17},{17,1},{2,18},{18,2},{3,19},{19,3},{4,20},{20... | collective-permute-start | bytes 405512 | tf_op jit(solution)/shard_map/ppermute | solution.py:33
  5.3 1.6 %collective-permute-start.1 = (f32[136,128]{1,0:T(8,128)S(1)}, f32[136,128]{1,0:T(8,128)S(1)}, u32[]{:S(2)}, u32[]{:S(2)}) collective-permute-start(f32[136,128]{1,0:T(8,128)S(1)} %get-tuple-element.33), channel_id=1, source_target_pairs={{0,4},{4,0},{8,12},{12,8},{1,5},{5,1},{9,13},{13,9},{2,6},{6,2},{1... | collective-permute-start | bytes 208904 | tf_op jit(solution)/shard_map/ppermute | solution.py:33
  6.9 0.0 collective-permute-start.2
  6.9 0.5 %collective-permute-start.3 = (f32[40,128]{1,0:T(8,128)S(1)}, f32[40,128]{1,0:T(8,128)S(1)}, u32[]{:S(2)}, u32[]{:S(2)}) collective-permute-start(f32[40,128]{1,0:T(8,128)S(1)} %get-tuple-element.35.own_ref), channel_id=1, source_target_pairs={{0,1},{1,0},{2,3},{3,2},{4,5},{5,4},{6,7},{7,6},{8,9},{9,8},{10,11... | collective-permute-start | bytes 61448 | tf_op jit(solution)/shard_map/ppermute | solution.py:33
  7.4 1.1 %collective-permute-start.4 = (f32[40,128]{1,0:T(8,128)S(1)}, f32[40,128]{1,0:T(8,128)S(1)}, u32[]{:S(2)}, u32[]{:S(2)}) collective-permute-start(f32[40,128]{1,0:T(8,128)S(1)} %get-tuple-element.35.own_ref), channel_id=1, source_target_pairs={{0,3},{1,2},{2,1},{3,0},{4,7},{5,6},{6,5},{7,4},{8,11},{9,10},{10,... | collective-permute-start | bytes 61448 | tf_op jit(solution)/shard_map/ppermute | solution.py:33
  8.5 0.8 %prepare.1 = (bf16[256,4096]{1,0:T(8,128)(2,1)S(1)}, bf16[512,128]{1,0:T(8,128)(2,1)S(1)}, f32[6,8,128]{2,1,0:T(8,128)S(1)}) custom-call(s32[1,256]{1,0:T(1,128)S(1)} %get-tuple-element.28.voxel_ref, s32[1,128]{1,0:T(1,128)S(1)} %get-tuple-element.29.owned_ref, f32[6,8,128]{2,1,0:T(8,128)S(1)} %get-tuple-element.30.level_ref), custom_call_target="tpu_custom_call" | custom-call | tf_op jit(solution)/shard_map/prepare/pallas_call | solution.py:714
  9.4 0.0 collective-permute-done.3.refs_3_
  9.4 1.3 %collective-permute-done.4.refs_4_ = f32[40,128]{1,0:T(8,128)S(1)} collective-permute-done((f32[40,128]{1,0:T(8,128)S(1)}, f32[40,128]{1,0:T(8,128)S(1)}, u32[]{:S(2)}, u32[]{:S(2)}) %collective-permute-start.4) | collective-permute-done | bytes 20512 | tf_op jit(solution)/shard_map/ppermute | solution.py:33
  10.7 0.0 collective-permute-done.1.refs_1_
  10.7 0.0 collective-permute-done.2.refs_2_
  10.7 0.0 collective-permute-done.refs_0_
  10.7 1.4 %apply.1 = (f32[8,4,8,128]{3,2,1,0:T(8,128)S(1)}, f32[32,128]{1,0:T(8,128)S(1)}, f32[1024,128]{1,0:T(8,128)S(1)}, f32[40,128]{1,0:T(8,128)S(1)}, f32[296,128]{1,...) custom-call(f32[1024,128]{1,0:T(8,128)S(1)} %get-tuple-element.26.rows_ref, ...), custom_call_target="tpu_custom_call" | custom-call | tf_op jit(solution)/shard_map/apply/pallas_call | solution.py:726
  12.0 0.6 %collective-permute-start.5 = (f32[296,128]{1,0:T(8,128)S(1)}, f32[296,128]{1,0:T(8,128)S(1)}, u32[]{:S(2)}, u32[]{:S(2)}) collective-permute-start(f32[296,128]{1,0:T(8,128)S(1)} %get-tuple-element.42), channel_id=1, source_target_pairs={{0,16},{16,0},{1,17},{17,1},{2,18},{18,2},{3,19},{19,3},{4,20},{20... | collective-permute-start | bytes 454664 | tf_op jit(solution)/shard_map/ppermute | solution.py:33
  12.6 2.6 %collective-permute-start.6 = (f32[168,128]{1,0:T(8,128)S(1)}, f32[168,128]{1,0:T(8,128)S(1)}, u32[]{:S(2)}, u32[]{:S(2)}) collective-permute-start(f32[168,128]{1,0:T(8,128)S(1)} %get-tuple-element.43), channel_id=1, source_target_pairs={{0,4},{4,0},{8,12},{12,8},{1,5},{5,1},{9,13},{13,9},{2,6},{6,2},{1... | collective-permute-start | bytes 258056 | tf_op jit(solution)/shard_map/ppermute | solution.py:33
  15.2 0.0 collective-permute-start.7
  15.2 1.7 %source_columns.1 = (f32[256,96]{1,0:T(8,128)S(1)}, f32[128,128]{1,0:T(8,128)S(1)}) custom-call(f32[1024,128]{1,0:T(8,128)S(1)} %get-tuple-element.26.rows_ref, f32[1024,128]{1,0:T(8,128)S(1)} %get-tuple-element.36.applied_ref, f32[8,4,8,128]{3,2,1,0:T(8,128)S(1)} %get-tuple-element.37.weight_ref, bf16[256,4096]{1,0:T(8,128)(2,1)S(1)} %get-tuple-element.38.chosen_ref, ...), custom_call_target="tpu_custom_call" | custom-call | tf_op jit(solution)/shard_map/source_columns/pallas_call | solution.py:739
  16.9 1.2 %collective-permute-done.6.refs_1_ = f32[168,128]{1,0:T(8,128)S(1)} collective-permute-done((f32[168,128]{1,0:T(8,128)S(1)}, f32[168,128]{1,0:T(8,128)S(1)}, u32[]{:S(2)}, u32[]{:S(2)}) %collective-permute-start.6) | collective-permute-done | bytes 86048 | tf_op jit(solution)/shard_map/ppermute | solution.py:33
  18.1 0.0 collective-permute-done.7.refs_2_
  18.1 0.0 collective-permute-done.5.refs_0_
  18.1 0.3 moments.1
  18.4 0.0 collective-permute-start.10
  18.4 1.6 %collective-permute-start.8 = (f32[8,128]{1,0:T(8,128)S(1)}, f32[8,128]{1,0:T(8,128)S(1)}, u32[]{:S(2)}, u32[]{:S(2)}) collective-permute-start(f32[8,128]{1,0:T(8,128)S(1)} %get-tuple-element.45), channel_id=1, source_target_pairs={{0,3},{1,2},{2,1},{3,0},{4,7},{5,6},{6,5},{7,4},{8,11},{9,10},{10,... | collective-permute-start | bytes 12296 | tf_op jit(solution)/shard_map/ppermute | solution.py:42
  20.1 0.5 %collective-permute-start.9 = (f32[8,128]{1,0:T(8,128)S(1)}, f32[8,128]{1,0:T(8,128)S(1)}, u32[]{:S(2)}, u32[]{:S(2)}) collective-permute-start(f32[8,128]{1,0:T(8,128)S(1)} %get-tuple-element.45), channel_id=1, source_target_pairs={{0,2},{1,3},{2,0},{3,1},{4,6},{5,7},{6,4},{7,5},{8,10},{9,11},{10,... | collective-permute-start | bytes 12296 | tf_op jit(solution)/shard_map/ppermute | solution.py:42
  20.6 1.4 %applied_columns.1 = f32[392,128]{1,0:T(8,128)S(1)} custom-call(f32[1024,128]{1,0:T(8,128)S(1)} %get-tuple-element.36.applied_ref, f32[8,4,8,128]{3,2,1,0:T(8,128)S(1)} %get-tuple-element.37.weight_ref, bf16[256,4096]{1,0:T(8,128)(2,1)S(1)} %get-tuple-element.38.chosen_ref, f32[256,96]{1,0:T(8,128)S(1)} %get-tuple-element.46.source_column_ref, ...), custom_call_target="tpu_custom_call" | custom-call | tf_op jit(solution)/shard_map/applied_columns/pallas_call | solution.py:758
  22.0 0.0 collective-permute-done.10
  22.1 0.0 collective-permute-done.8
  22.1 1.6 %collective-permute-done.9 = f32[8,128]{1,0:T(8,128)S(1)} collective-permute-done((f32[8,128]{1,0:T(8,128)S(1)}, f32[8,128]{1,0:T(8,128)S(1)}, u32[]{:S(2)}, u32[]{:S(2)}) %collective-permute-start.9) | collective-permute-done | bytes 4128 | tf_op jit(solution)/shard_map/ppermute | solution.py:42
  23.7 0.2 fusion
  23.9 12.2 %all_to_all.5 = f32[8,1,6272]{2,1,0:T(1,128)S(1)} all-to-all(f32[8,1,6272]{2,1,0:T(1,128)S(1)} %bitcast.7), channel_id=1, replica_groups=mesh['gx'=2,'gy'=4,'gz'=4] {'gx','gy'}, dimensions={0} | all-to-all | bytes 401408 | tf_op jit(solution)/shard_map/all_to_all | solution.py:770
  36.1 1.2 %owner.1 = (f32[3,128,128]{2,1,0:T(8,128)}, f32[6,128]{1,0:T(8,128)}) custom-call(f32[392,128]{1,0:T(8,128)S(1)} %bitcast.6, bf16[512,128]{1,0:T(8,128)(2,1)S(1)} %get-tuple-element.48.chosen_ref, f32[32,128]{1,0:T(8,128)S(1)} %get-tuple-element.49.data_ref), custom_call_target="tpu_custom_call" | custom-call | tf_op jit(solution)/shard_map/owner/pallas_call | solution.py:773
  (4 shorter events, 0.0 us)
Async XLA Ops:
  2.3 8.4 %collective-permute-start = (f32[264,128]{1,0:T(8,128)S(1)}, f32[264,128]{1,0:T(8,128)S(1)}, u32[]{:S(2)}, u32[]{:S(2)}) collective-permute-start(f32[264,128]{1,0:T(8,128)S(1)} %get-tuple-element.32), channel_id=1, source_target_pairs={{0,16},{16,0},{1,17},{17,1},{2,18},{18,2},{3,19},{19,3},{4,20},{20... | collective-permute-start | bytes 405512 | tf_op jit(solution)/shard_map/ppermute | solution.py:33
  5.3 5.3 %collective-permute-start.1 = (f32[136,128]{1,0:T(8,128)S(1)}, f32[136,128]{1,0:T(8,128)S(1)}, u32[]{:S(2)}, u32[]{:S(2)}) collective-permute-start(f32[136,128]{1,0:T(8,128)S(1)} %get-tuple-element.33), channel_id=1, source_target_pairs={{0,4},{4,0},{8,12},{12,8},{1,5},{5,1},{9,13},{13,9},{2,6},{6,2},{1... | collective-permute-start | bytes 208904 | tf_op jit(solution)/shard_map/ppermute | solution.py:33
  6.9 3.8 %collective-permute-start.2 = (f32[136,128]{1,0:T(8,128)S(1)}, f32[136,128]{1,0:T(8,128)S(1)}, u32[]{:S(2)}, u32[]{:S(2)}) collective-permute-start(f32[136,128]{1,0:T(8,128)S(1)} %get-tuple-element.34), channel_id=1, source_target_pairs={{0,1},{1,0},{2,3},{3,2},{4,8},{5,9},{6,10},{7,11},{8,4},{9,5},{10,... | collective-permute-start | bytes 208904 | tf_op jit(solution)/shard_map/ppermute | solution.py:30
  6.9 2.4 %collective-permute-start.3 = (f32[40,128]{1,0:T(8,128)S(1)}, f32[40,128]{1,0:T(8,128)S(1)}, u32[]{:S(2)}, u32[]{:S(2)}) collective-permute-start(f32[40,128]{1,0:T(8,128)S(1)} %get-tuple-element.35.own_ref), channel_id=1, source_target_pairs={{0,1},{1,0},{2,3},{3,2},{4,5},{5,4},{6,7},{7,6},{8,9},{9,8},{10,11... | collective-permute-start | bytes 61448 | tf_op jit(solution)/shard_map/ppermute | solution.py:33
  7.4 3.2 %collective-permute-start.4 = (f32[40,128]{1,0:T(8,128)S(1)}, f32[40,128]{1,0:T(8,128)S(1)}, u32[]{:S(2)}, u32[]{:S(2)}) collective-permute-start(f32[40,128]{1,0:T(8,128)S(1)} %get-tuple-element.35.own_ref), channel_id=1, source_target_pairs={{0,3},{1,2},{2,1},{3,0},{4,7},{5,6},{6,5},{7,4},{8,11},{9,10},{10,... | collective-permute-start | bytes 61448 | tf_op jit(solution)/shard_map/ppermute | solution.py:33
  12.0 6.1 %collective-permute-start.5 = (f32[296,128]{1,0:T(8,128)S(1)}, f32[296,128]{1,0:T(8,128)S(1)}, u32[]{:S(2)}, u32[]{:S(2)}) collective-permute-start(f32[296,128]{1,0:T(8,128)S(1)} %get-tuple-element.42), channel_id=1, source_target_pairs={{0,16},{16,0},{1,17},{17,1},{2,18},{18,2},{3,19},{19,3},{4,20},{20... | collective-permute-start | bytes 454664 | tf_op jit(solution)/shard_map/ppermute | solution.py:33
  12.6 5.5 %collective-permute-start.6 = (f32[168,128]{1,0:T(8,128)S(1)}, f32[168,128]{1,0:T(8,128)S(1)}, u32[]{:S(2)}, u32[]{:S(2)}) collective-permute-start(f32[168,128]{1,0:T(8,128)S(1)} %get-tuple-element.43), channel_id=1, source_target_pairs={{0,4},{4,0},{8,12},{12,8},{1,5},{5,1},{9,13},{13,9},{2,6},{6,2},{1... | collective-permute-start | bytes 258056 | tf_op jit(solution)/shard_map/ppermute | solution.py:33
  15.2 2.9 %collective-permute-start.7 = (f32[168,128]{1,0:T(8,128)S(1)}, f32[168,128]{1,0:T(8,128)S(1)}, u32[]{:S(2)}, u32[]{:S(2)}) collective-permute-start(f32[168,128]{1,0:T(8,128)S(1)} %get-tuple-element.44), channel_id=1, source_target_pairs={{0,1},{1,0},{2,3},{3,2},{4,8},{5,9},{6,10},{7,11},{8,4},{9,5},{10,... | collective-permute-start | bytes 258056 | tf_op jit(solution)/shard_map/ppermute | solution.py:30
  18.4 3.6 %collective-permute-start.10 = (f32[8,128]{1,0:T(8,128)S(1)}, f32[8,128]{1,0:T(8,128)S(1)}, u32[]{:S(2)}, u32[]{:S(2)}) collective-permute-start(f32[8,128]{1,0:T(8,128)S(1)} %get-tuple-element.45), channel_id=1, source_target_pairs={{0,1},{1,0},{2,3},{3,2},{4,5},{5,4},{6,7},{7,6},{8,9},{9,8},{10,11... | collective-permute-start | bytes 12296 | tf_op jit(solution)/shard_map/ppermute | solution.py:42
  18.4 3.6 %collective-permute-start.8 = (f32[8,128]{1,0:T(8,128)S(1)}, f32[8,128]{1,0:T(8,128)S(1)}, u32[]{:S(2)}, u32[]{:S(2)}) collective-permute-start(f32[8,128]{1,0:T(8,128)S(1)} %get-tuple-element.45), channel_id=1, source_target_pairs={{0,3},{1,2},{2,1},{3,0},{4,7},{5,6},{6,5},{7,4},{8,11},{9,10},{10,... | collective-permute-start | bytes 12296 | tf_op jit(solution)/shard_map/ppermute | solution.py:42
  20.1 3.6 %collective-permute-start.9 = (f32[8,128]{1,0:T(8,128)S(1)}, f32[8,128]{1,0:T(8,128)S(1)}, u32[]{:S(2)}, u32[]{:S(2)}) collective-permute-start(f32[8,128]{1,0:T(8,128)S(1)} %get-tuple-element.45), channel_id=1, source_target_pairs={{0,2},{1,3},{2,0},{3,1},{4,6},{5,7},{6,4},{7,5},{8,10},{9,11},{10,... | collective-permute-start | bytes 12296 | tf_op jit(solution)/shard_map/ppermute | solution.py:42

commit v8 on v7

--- a/solution.py
+++ b/solution.py
@@ -35,10 +35,11 @@
 
 def sum_over(value, axis):
     count = lax.axis_size(axis)
+    steps = [count - 1, *range(1, count - 1)][: count - 1]
     if count & (count - 1) == 0:
-        tables = [[(i, i ^ d) for i in range(count)] for d in range(count - 1, 0, -1)]
+        tables = [[(i, i ^ d) for i in range(count)] for d in steps]
     else:
-        tables = [[(i, (i + d) % count) for i in range(count)] for d in range(count - 1, 0, -1)]
+        tables = [[(i, (i + d) % count) for i in range(count)] for d in steps]
     return value + sum(lax.ppermute(value, axis, table) for table in tables)
 
 

time: 37.6 us -> 37.1 us (0.987)
  waiting for transfers between devices: 4.15 us -> 3.47 us
    ppermute x3, waiting for transfers between devices: 1.61 us -> 0.93 us  [sum_over(): return value + sum((lax.ppermute(value, axis, table) for table in tables))]
where the time goes in v8:
time: 37.1 us; the launch traced here: 36.8 us
  blocking collectives  12.3 us (33%)
  starting transfers between devices  11.6 us (31%)
  Pallas kernels  8.47 us (23%)
  waiting for transfers between devices  3.47 us (9%)
  between operations  0.7 us (2%)
    all_to_all x1, blocking collectives, per_device(): lax.all_to_all(columns.reshape(owners, 1, each * lane_tile), ('gx', 'gy')...  12.3 us
    ppermute x6, starting transfers between devices, swap(): return lax.ppermute(value, axis, sorted(partner.items()))  9.4 us
    ppermute x6, waiting for transfers between devices, swap(): return lax.ppermute(value, axis, sorted(partner.items()))  2.53 us
    ppermute x3, starting transfers between devices, sum_over(): return value + sum((lax.ppermute(value, axis, table) for table in tables))  2.17 us
    pallas_call x1, Pallas kernels, per_device(): call(functools.partial(source_kernel, dims, counts), out_shape=[array((sl...  1.68 us
    pallas_call x1, Pallas kernels, per_device(): call(functools.partial(pack_kernel, dims, counts), out_shape=[field_shape...  1.64 us
    pallas_call x1, Pallas kernels, per_device(): call(functools.partial(applied_kernel, dims, counts, slots_each), out_sha...  1.44 us
    pallas_call x1, Pallas kernels, per_device(): call(functools.partial(apply_kernel, dims, counts), out_shape=[array((8,...  1.35 us
  transfers between devices with their start and end apart: 11, of which 3 were waited for; matrix products, arithmetic and copies ran while one was open for 0% of the time, Pallas kernels for 11%

profile of v8, /device:TPU:0, one launch (start us, length us, event | category | flops | bytes accessed | tf_op | source)
XLA Modules:
  0.0 36.8 jit_solution(5079828018122189220)
XLA Ops:
  0.6 1.6 %pack.1 = (f32[1024,128]{1,0:T(8,128)S(1)}, f32[4,8,128]{2,1,0:T(8,128)S(1)}, f32[6,8,128]{2,1,0:T(8,128)S(1)}, s32[1,256]{1,0:T(1,128)S(1)}, s32[1,128]{1,0:T(1...) custom-call(f32[32,4,8,128]{3,2,1,0:T(8,128)} %source_ref.1, ...), custom_call_target="tpu_custom_call" | custom-call | tf_op jit(solution)/shard_map/pack/pallas_call | solution.py:697
  2.3 3.1 %collective-permute-start = (f32[264,128]{1,0:T(8,128)S(1)}, f32[264,128]{1,0:T(8,128)S(1)}, u32[]{:S(2)}, u32[]{:S(2)}) collective-permute-start(f32[264,128]{1,0:T(8,128)S(1)} %get-tuple-element.32), channel_id=1, source_target_pairs={{0,16},{16,0},{1,17},{17,1},{2,18},{18,2},{3,19},{19,3},{4,20},{20... | collective-permute-start | bytes 405512 | tf_op jit(solution)/shard_map/ppermute | solution.py:33
  5.3 1.6 %collective-permute-start.1 = (f32[136,128]{1,0:T(8,128)S(1)}, f32[136,128]{1,0:T(8,128)S(1)}, u32[]{:S(2)}, u32[]{:S(2)}) collective-permute-start(f32[136,128]{1,0:T(8,128)S(1)} %get-tuple-element.33), channel_id=1, source_target_pairs={{0,4},{4,0},{8,12},{12,8},{1,5},{5,1},{9,13},{13,9},{2,6},{6,2},{1... | collective-permute-start | bytes 208904 | tf_op jit(solution)/shard_map/ppermute | solution.py:33
  6.9 0.0 collective-permute-start.2
  6.9 0.5 %collective-permute-start.3 = (f32[40,128]{1,0:T(8,128)S(1)}, f32[40,128]{1,0:T(8,128)S(1)}, u32[]{:S(2)}, u32[]{:S(2)}) collective-permute-start(f32[40,128]{1,0:T(8,128)S(1)} %get-tuple-element.35.own_ref), channel_id=1, source_target_pairs={{0,1},{1,0},{2,3},{3,2},{4,5},{5,4},{6,7},{7,6},{8,9},{9,8},{10,11... | collective-permute-start | bytes 61448 | tf_op jit(solution)/shard_map/ppermute | solution.py:33
  7.4 1.1 %collective-permute-start.4 = (f32[40,128]{1,0:T(8,128)S(1)}, f32[40,128]{1,0:T(8,128)S(1)}, u32[]{:S(2)}, u32[]{:S(2)}) collective-permute-start(f32[40,128]{1,0:T(8,128)S(1)} %get-tuple-element.35.own_ref), channel_id=1, source_target_pairs={{0,3},{1,2},{2,1},{3,0},{4,7},{5,6},{6,5},{7,4},{8,11},{9,10},{10,... | collective-permute-start | bytes 61448 | tf_op jit(solution)/shard_map/ppermute | solution.py:33
  8.5 0.8 %prepare.1 = (bf16[256,4096]{1,0:T(8,128)(2,1)S(1)}, bf16[512,128]{1,0:T(8,128)(2,1)S(1)}, f32[6,8,128]{2,1,0:T(8,128)S(1)}) custom-call(s32[1,256]{1,0:T(1,128)S(1)} %get-tuple-element.28.voxel_ref, s32[1,128]{1,0:T(1,128)S(1)} %get-tuple-element.29.owned_ref, f32[6,8,128]{2,1,0:T(8,128)S(1)} %get-tuple-element.30.level_ref), custom_call_target="tpu_custom_call" | custom-call | tf_op jit(solution)/shard_map/prepare/pallas_call | solution.py:715
  9.4 0.0 collective-permute-done.3.refs_3_
  9.4 1.3 %collective-permute-done.4.refs_4_ = f32[40,128]{1,0:T(8,128)S(1)} collective-permute-done((f32[40,128]{1,0:T(8,128)S(1)}, f32[40,128]{1,0:T(8,128)S(1)}, u32[]{:S(2)}, u32[]{:S(2)}) %collective-permute-start.4) | collective-permute-done | bytes 20512 | tf_op jit(solution)/shard_map/ppermute | solution.py:33
  10.7 0.0 collective-permute-done.1.refs_1_
  10.7 0.0 collective-permute-done.2.refs_2_
  10.7 0.0 collective-permute-done.refs_0_
  10.7 1.4 %apply.1 = (f32[8,4,8,128]{3,2,1,0:T(8,128)S(1)}, f32[32,128]{1,0:T(8,128)S(1)}, f32[1024,128]{1,0:T(8,128)S(1)}, f32[40,128]{1,0:T(8,128)S(1)}, f32[296,128]{1,...) custom-call(f32[1024,128]{1,0:T(8,128)S(1)} %get-tuple-element.26.rows_ref, ...), custom_call_target="tpu_custom_call" | custom-call | tf_op jit(solution)/shard_map/apply/pallas_call | solution.py:727
  12.0 0.6 %collective-permute-start.5 = (f32[296,128]{1,0:T(8,128)S(1)}, f32[296,128]{1,0:T(8,128)S(1)}, u32[]{:S(2)}, u32[]{:S(2)}) collective-permute-start(f32[296,128]{1,0:T(8,128)S(1)} %get-tuple-element.42), channel_id=1, source_target_pairs={{0,16},{16,0},{1,17},{17,1},{2,18},{18,2},{3,19},{19,3},{4,20},{20... | collective-permute-start | bytes 454664 | tf_op jit(solution)/shard_map/ppermute | solution.py:33
  12.6 2.6 %collective-permute-start.6 = (f32[168,128]{1,0:T(8,128)S(1)}, f32[168,128]{1,0:T(8,128)S(1)}, u32[]{:S(2)}, u32[]{:S(2)}) collective-permute-start(f32[168,128]{1,0:T(8,128)S(1)} %get-tuple-element.43), channel_id=1, source_target_pairs={{0,4},{4,0},{8,12},{12,8},{1,5},{5,1},{9,13},{13,9},{2,6},{6,2},{1... | collective-permute-start | bytes 258056 | tf_op jit(solution)/shard_map/ppermute | solution.py:33
  15.2 0.0 collective-permute-start.7
  15.2 1.7 %source_columns.1 = (f32[256,96]{1,0:T(8,128)S(1)}, f32[128,128]{1,0:T(8,128)S(1)}) custom-call(f32[1024,128]{1,0:T(8,128)S(1)} %get-tuple-element.26.rows_ref, f32[1024,128]{1,0:T(8,128)S(1)} %get-tuple-element.36.applied_ref, f32[8,4,8,128]{3,2,1,0:T(8,128)S(1)} %get-tuple-element.37.weight_ref, bf16[256,4096]{1,0:T(8,128)(2,1)S(1)} %get-tuple-element.38.chosen_ref, ...), custom_call_target="tpu_custom_call" | custom-call | tf_op jit(solution)/shard_map/source_columns/pallas_call | solution.py:740
  16.9 1.2 %collective-permute-done.6.refs_1_ = f32[168,128]{1,0:T(8,128)S(1)} collective-permute-done((f32[168,128]{1,0:T(8,128)S(1)}, f32[168,128]{1,0:T(8,128)S(1)}, u32[]{:S(2)}, u32[]{:S(2)}) %collective-permute-start.6) | collective-permute-done | bytes 86048 | tf_op jit(solution)/shard_map/ppermute | solution.py:33
  18.1 0.0 collective-permute-done.7.refs_2_
  18.1 0.0 collective-permute-done.5.refs_0_
  18.1 0.3 moments.1
  18.4 1.5 %collective-permute-start.10 = (f32[8,128]{1,0:T(8,128)S(1)}, f32[8,128]{1,0:T(8,128)S(1)}, u32[]{:S(2)}, u32[]{:S(2)}) collective-permute-start(f32[8,128]{1,0:T(8,128)S(1)} %get-tuple-element.45), channel_id=1, source_target_pairs={{0,2},{1,3},{2,0},{3,1},{4,6},{5,7},{6,4},{7,5},{8,10},{9,11},{10,... | collective-permute-start | bytes 12296 | tf_op jit(solution)/shard_map/ppermute | solution.py:43
  19.9 0.0 collective-permute-start.8
  19.9 0.6 %collective-permute-start.9 = (f32[8,128]{1,0:T(8,128)S(1)}, f32[8,128]{1,0:T(8,128)S(1)}, u32[]{:S(2)}, u32[]{:S(2)}) collective-permute-start(f32[8,128]{1,0:T(8,128)S(1)} %get-tuple-element.45), channel_id=1, source_target_pairs={{0,1},{1,0},{2,3},{3,2},{4,5},{5,4},{6,7},{7,6},{8,9},{9,8},{10,11... | collective-permute-start | bytes 12296 | tf_op jit(solution)/shard_map/ppermute | solution.py:43
  20.6 1.4 %applied_columns.1 = f32[392,128]{1,0:T(8,128)S(1)} custom-call(f32[1024,128]{1,0:T(8,128)S(1)} %get-tuple-element.36.applied_ref, f32[8,4,8,128]{3,2,1,0:T(8,128)S(1)} %get-tuple-element.37.weight_ref, bf16[256,4096]{1,0:T(8,128)(2,1)S(1)} %get-tuple-element.38.chosen_ref, f32[256,96]{1,0:T(8,128)S(1)} %get-tuple-element.46.source_column_ref, ...), custom_call_target="tpu_custom_call" | custom-call | tf_op jit(solution)/shard_map/applied_columns/pallas_call | solution.py:759
  22.0 0.0 collective-permute-done.10
  22.1 0.9 %collective-permute-done.8 = f32[8,128]{1,0:T(8,128)S(1)} collective-permute-done((f32[8,128]{1,0:T(8,128)S(1)}, f32[8,128]{1,0:T(8,128)S(1)}, u32[]{:S(2)}, u32[]{:S(2)}) %collective-permute-start.8) | collective-permute-done | bytes 4128 | tf_op jit(solution)/shard_map/ppermute | solution.py:43
  23.0 0.0 collective-permute-done.9
  23.0 0.2 fusion
  23.2 12.3 %all_to_all.5 = f32[8,1,6272]{2,1,0:T(1,128)S(1)} all-to-all(f32[8,1,6272]{2,1,0:T(1,128)S(1)} %bitcast.7), channel_id=1, replica_groups=mesh['gx'=2,'gy'=4,'gz'=4] {'gx','gy'}, dimensions={0} | all-to-all | bytes 401408 | tf_op jit(solution)/shard_map/all_to_all | solution.py:771
  35.6 1.2 %owner.1 = (f32[3,128,128]{2,1,0:T(8,128)}, f32[6,128]{1,0:T(8,128)}) custom-call(f32[392,128]{1,0:T(8,128)S(1)} %bitcast.6, bf16[512,128]{1,0:T(8,128)(2,1)S(1)} %get-tuple-element.48.chosen_ref, f32[32,128]{1,0:T(8,128)S(1)} %get-tuple-element.49.data_ref), custom_call_target="tpu_custom_call" | custom-call | tf_op jit(solution)/shard_map/owner/pallas_call | solution.py:774
  (4 shorter events, 0.0 us)
Async XLA Ops:
  2.3 8.4 %collective-permute-start = (f32[264,128]{1,0:T(8,128)S(1)}, f32[264,128]{1,0:T(8,128)S(1)}, u32[]{:S(2)}, u32[]{:S(2)}) collective-permute-start(f32[264,128]{1,0:T(8,128)S(1)} %get-tuple-element.32), channel_id=1, source_target_pairs={{0,16},{16,0},{1,17},{17,1},{2,18},{18,2},{3,19},{19,3},{4,20},{20... | collective-permute-start | bytes 405512 | tf_op jit(solution)/shard_map/ppermute | solution.py:33
  5.3 5.3 %collective-permute-start.1 = (f32[136,128]{1,0:T(8,128)S(1)}, f32[136,128]{1,0:T(8,128)S(1)}, u32[]{:S(2)}, u32[]{:S(2)}) collective-permute-start(f32[136,128]{1,0:T(8,128)S(1)} %get-tuple-element.33), channel_id=1, source_target_pairs={{0,4},{4,0},{8,12},{12,8},{1,5},{5,1},{9,13},{13,9},{2,6},{6,2},{1... | collective-permute-start | bytes 208904 | tf_op jit(solution)/shard_map/ppermute | solution.py:33
  6.9 3.8 %collective-permute-start.2 = (f32[136,128]{1,0:T(8,128)S(1)}, f32[136,128]{1,0:T(8,128)S(1)}, u32[]{:S(2)}, u32[]{:S(2)}) collective-permute-start(f32[136,128]{1,0:T(8,128)S(1)} %get-tuple-element.34), channel_id=1, source_target_pairs={{0,1},{1,0},{2,3},{3,2},{4,8},{5,9},{6,10},{7,11},{8,4},{9,5},{10,... | collective-permute-start | bytes 208904 | tf_op jit(solution)/shard_map/ppermute | solution.py:30
  6.9 2.4 %collective-permute-start.3 = (f32[40,128]{1,0:T(8,128)S(1)}, f32[40,128]{1,0:T(8,128)S(1)}, u32[]{:S(2)}, u32[]{:S(2)}) collective-permute-start(f32[40,128]{1,0:T(8,128)S(1)} %get-tuple-element.35.own_ref), channel_id=1, source_target_pairs={{0,1},{1,0},{2,3},{3,2},{4,5},{5,4},{6,7},{7,6},{8,9},{9,8},{10,11... | collective-permute-start | bytes 61448 | tf_op jit(solution)/shard_map/ppermute | solution.py:33
  7.4 3.2 %collective-permute-start.4 = (f32[40,128]{1,0:T(8,128)S(1)}, f32[40,128]{1,0:T(8,128)S(1)}, u32[]{:S(2)}, u32[]{:S(2)}) collective-permute-start(f32[40,128]{1,0:T(8,128)S(1)} %get-tuple-element.35.own_ref), channel_id=1, source_target_pairs={{0,3},{1,2},{2,1},{3,0},{4,7},{5,6},{6,5},{7,4},{8,11},{9,10},{10,... | collective-permute-start | bytes 61448 | tf_op jit(solution)/shard_map/ppermute | solution.py:33
  12.0 6.1 %collective-permute-start.5 = (f32[296,128]{1,0:T(8,128)S(1)}, f32[296,128]{1,0:T(8,128)S(1)}, u32[]{:S(2)}, u32[]{:S(2)}) collective-permute-start(f32[296,128]{1,0:T(8,128)S(1)} %get-tuple-element.42), channel_id=1, source_target_pairs={{0,16},{16,0},{1,17},{17,1},{2,18},{18,2},{3,19},{19,3},{4,20},{20... | collective-permute-start | bytes 454664 | tf_op jit(solution)/shard_map/ppermute | solution.py:33
  12.6 5.5 %collective-permute-start.6 = (f32[168,128]{1,0:T(8,128)S(1)}, f32[168,128]{1,0:T(8,128)S(1)}, u32[]{:S(2)}, u32[]{:S(2)}) collective-permute-start(f32[168,128]{1,0:T(8,128)S(1)} %get-tuple-element.43), channel_id=1, source_target_pairs={{0,4},{4,0},{8,12},{12,8},{1,5},{5,1},{9,13},{13,9},{2,6},{6,2},{1... | collective-permute-start | bytes 258056 | tf_op jit(solution)/shard_map/ppermute | solution.py:33
  15.2 2.9 %collective-permute-start.7 = (f32[168,128]{1,0:T(8,128)S(1)}, f32[168,128]{1,0:T(8,128)S(1)}, u32[]{:S(2)}, u32[]{:S(2)}) collective-permute-start(f32[168,128]{1,0:T(8,128)S(1)} %get-tuple-element.44), channel_id=1, source_target_pairs={{0,1},{1,0},{2,3},{3,2},{4,8},{5,9},{6,10},{7,11},{8,4},{9,5},{10,... | collective-permute-start | bytes 258056 | tf_op jit(solution)/shard_map/ppermute | solution.py:30
  18.4 3.6 %collective-permute-start.10 = (f32[8,128]{1,0:T(8,128)S(1)}, f32[8,128]{1,0:T(8,128)S(1)}, u32[]{:S(2)}, u32[]{:S(2)}) collective-permute-start(f32[8,128]{1,0:T(8,128)S(1)} %get-tuple-element.45), channel_id=1, source_target_pairs={{0,2},{1,3},{2,0},{3,1},{4,6},{5,7},{6,4},{7,5},{8,10},{9,11},{10,... | collective-permute-start | bytes 12296 | tf_op jit(solution)/shard_map/ppermute | solution.py:43
  19.9 3.0 %collective-permute-start.8 = (f32[8,128]{1,0:T(8,128)S(1)}, f32[8,128]{1,0:T(8,128)S(1)}, u32[]{:S(2)}, u32[]{:S(2)}) collective-permute-start(f32[8,128]{1,0:T(8,128)S(1)} %get-tuple-element.45), channel_id=1, source_target_pairs={{0,3},{1,2},{2,1},{3,0},{4,7},{5,6},{6,5},{7,4},{8,11},{9,10},{10,... | collective-permute-start | bytes 12296 | tf_op jit(solution)/shard_map/ppermute | solution.py:43
  19.9 3.0 %collective-permute-start.9 = (f32[8,128]{1,0:T(8,128)S(1)}, f32[8,128]{1,0:T(8,128)S(1)}, u32[]{:S(2)}, u32[]{:S(2)}) collective-permute-start(f32[8,128]{1,0:T(8,128)S(1)} %get-tuple-element.45), channel_id=1, source_target_pairs={{0,1},{1,0},{2,3},{3,2},{4,5},{5,4},{6,7},{7,6},{8,9},{9,8},{10,11... | collective-permute-start | bytes 12296 | tf_op jit(solution)/shard_map/ppermute | solution.py:43

commit v9 on v8

--- a/solution.py
+++ b/solution.py
@@ -103,31 +103,34 @@
     return flags
 
 
-def write_faces(dims, rows_ref, face_refs, labels=None, beyond=None):
-    sensors, size_x, size_y, size_z = dims
-    x_refs, y_refs = face_refs
-
-    def field(r):
-        return rows_ref[pl.ds(pl.multiple_of(r * sensors, sensors), sensors), :]
-
-    def high_end(axis, number):
-        return lax.axis_index(axis) % 2 == number
-
-    for number, ref in enumerate(x_refs):
+def high_end(axis, number):
+    return lax.axis_index(axis) % 2 == number
+
+
+def line_of(dims, rows_ref, r):
+    sensors = dims[0]
+    return rows_ref[pl.ds(pl.multiple_of(r * sensors, sensors), sensors), :]
+
+
+def write_x(dims, rows_ref, refs, labels=None, beyond=None):
+    sensors, size_x, size_y, size_z = dims
+    last = rows_ref.shape[0] // (sensors * size_y) - 1
+    for number, ref in enumerate(refs):
         high = high_end("gx", number)
-        x = jnp.where(high, size_x - 1, 0)
+        x = jnp.where(high, last, 0)
         for y in range(size_y):
-            ref[y * sensors : (y + 1) * sensors, :] = field(x * size_y + y)
-        if labels is not None:
-            ref[size_y * sensors :, :] = jnp.where(high, labels[-1], labels[0])
-        else:
-            ref[size_y * sensors :, :] = beyond
-
-    for number, ref in enumerate(y_refs):
+            ref[y * sensors : (y + 1) * sensors, :] = line_of(dims, rows_ref, x * size_y + y)
+        behind = beyond if labels is None else jnp.where(high, labels[-1], labels[0])
+        ref[size_y * sensors :, :] = behind
+
+
+def write_y(dims, rows_ref, refs, labels=None, beyond=None):
+    sensors, size_x, size_y, size_z = dims
+    for number, ref in enumerate(refs):
         high = high_end("gy", number)
         y = jnp.where(high, size_y - 1, 0)
         for x in range(size_x):
-            ref[x * sensors : (x + 1) * sensors, :] = field(x * size_y + y)
+            ref[x * sensors : (x + 1) * sensors, :] = line_of(dims, rows_ref, x * size_y + y)
             if labels is not None:
                 row = size_x * sensors + x
                 ref[row : row + 1, :] = jnp.where(high, labels[x][size_y - 1 :, :], labels[x][0:1, :])
@@ -206,7 +209,8 @@
         for y in range(size_y):
             r = x * size_y + y
             rows_ref[r * sensors : (r + 1) * sensors, :] = flat[x, pl.ds(y, sensors, stride=size_y), :]
-    write_faces(dims, rows_ref, face_refs, labels=shifted)
+    write_x(dims, rows_ref, face_refs[0], labels=shifted)
+    write_y(dims, rows_ref, face_refs[1], labels=shifted)
     own_ref[0:sensors, :] = pack_rows(dims, rows_ref, 2, 0)
     own_ref[sensors:, :] = pack_lines(dims, [(plane, plane) for plane in shifted], 2, 0)
 
@@ -355,19 +359,43 @@
     return total
 
 
-def apply_kernel(dims, counts, rows_ref, shifted_ref, table_ref, *refs):
-    sensors, size_x, size_y, size_z = dims
+def x_ends(size_x):
+    return sorted({0, size_x - 1})
+
+
+def apply_rows(dims, rows_ref, weight_ref, halo_refs, z_ref, x, target_ref, place):
+    sensors, size_y = dims[0], dims[2]
+    for y in range(size_y):
+        centre, beside = around(dims, rows_ref, halo_refs, z_ref, x * size_y + y)
+        first = (place * size_y + y) * sensors
+        target_ref[first : first + sensors, :] = combine(weight_ref, x, y, centre, beside)
+
+
+def apply_ends_kernel(dims, counts, rows_ref, shifted_ref, table_ref, *refs):
     message_refs, refs = refs[: sum(counts)], refs[sum(counts) :]
-    weight_ref, end_ref, applied_ref, z_ref = refs[:4]
-    face_refs = split_refs(refs[4 : 4 + sum(counts[:2])], counts[:2])
-    halo_refs = sort_halos(message_refs, refs[4 + sum(counts[:2]) :], counts)
+    weight_ref, z_ref, edge_ref = refs[:3]
+    halo_refs = sort_halos(message_refs, refs[3 + counts[0] :], counts)
     z_ref[...] = sort_ends(message_refs[sum(counts[:2]) :])
     weights(dims, shifted_ref, table_ref, halo_refs, z_ref, weight_ref)
-    for r in range(size_x * size_y):
-        x, y = divmod(r, size_y)
-        centre, beside = around(dims, rows_ref, halo_refs, z_ref, r)
-        applied_ref[r * sensors : (r + 1) * sensors, :] = combine(weight_ref, x, y, centre, beside)
-    write_faces(dims, applied_ref, face_refs, beyond=z_ref[...])
+    for place, x in enumerate(x_ends(dims[1])):
+        apply_rows(dims, rows_ref, weight_ref, halo_refs, z_ref, x, edge_ref, place)
+    write_x(dims, edge_ref, refs[3 : 3 + counts[0]], beyond=z_ref[...])
+
+
+def apply_kernel(dims, counts, rows_ref, weight_ref, z_ref, edge_ref, *refs):
+    sensors, size_x, size_y, size_z = dims
+    message_refs, refs = refs[: sum(counts[:2])], refs[sum(counts[:2]) :]
+    end_ref, applied_ref = refs[:2]
+    halo_refs = sort_halos(message_refs, refs[2 + counts[1] :], counts)
+    plane = size_y * sensors
+    ends = x_ends(size_x)
+    for x in range(size_x):
+        if x in ends:
+            place = ends.index(x)
+            applied_ref[x * plane : (x + 1) * plane, :] = edge_ref[place * plane : (place + 1) * plane, :]
+        else:
+            apply_rows(dims, rows_ref, weight_ref, halo_refs, z_ref, x, applied_ref, x)
+    write_y(dims, applied_ref, refs[2 : 2 + counts[1]], beyond=z_ref[...])
     lines = [(weight_ref[4, x], weight_ref[5, x]) for x in range(size_x)]
     outward = pack_lines(dims, lines, 1, 1)
     end_ref[...] = outward[0:1, :] * pack_rows(dims, applied_ref, 1, 1)
@@ -724,18 +752,26 @@
         name="prepare",
     )(voxel, owned, table)
 
-    result = call(
+    face_out = face_shapes(dims, counts, sensors + 8, sensors + 8)
+    weight, beyond, edges, *x_faces = call(
+        functools.partial(apply_ends_kernel, dims, counts),
+        out_shape=[array((8, size_x, size_y, size_z)), ends_shape]
+        + [array((len(x_ends(size_x)) * size_y * sensors, size_z))]
+        + face_out[: counts[0]],
+        in_specs=in_vmem(3 + messages + counts[2]),
+        out_specs=in_vmem(3 + counts[0]),
+        scratch_shapes=held_halos(source_halos, counts),
+        name="apply_ends",
+    )(rows, shifted, table, *source_halos)
+    ends, applied, *y_faces = call(
         functools.partial(apply_kernel, dims, counts),
-        out_shape=[array((8, size_x, size_y, size_z)), array((sensors, size_z)), field_shape]
-        + [ends_shape]
-        + face_shapes(dims, counts, sensors + 8, sensors + 8),
-        in_specs=in_vmem(3 + messages + counts[2]),
-        out_specs=in_vmem(4 + messages),
+        out_shape=[array((sensors, size_z)), field_shape] + face_out[counts[0] :],
+        in_specs=in_vmem(4 + messages),
+        out_specs=in_vmem(2 + counts[1]),
         scratch_shapes=held_halos(source_halos, counts),
         name="apply",
-    )(rows, shifted, table, *source_halos)
-    weight, ends, applied, beyond, *faces = result
-    applied_halos = exchange_all(split_refs(faces, counts[:2]))
+    )(rows, weight, beyond, edges, *source_halos[:messages])
+    applied_halos = exchange_all([x_faces, y_faces])
 
     source_columns, sums = call(
         functools.partial(source_kernel, dims, counts),

time: 37.1 us -> 37.2 us (level)
    pallas_call x1 -> x2, Pallas kernels: 1.35 us -> 1.34 us  [the longest x1 0.74 us: per_device(): call(functools.partial(apply_kernel, dims, counts), out_shape=[array((sen...]
  transfers between devices with their start and end apart: 11 -> 11, of which waited for: 3 -> 3; matrix products, arithmetic and copies ran while one was open for 0% -> 0% of each run, Pallas kernels for 11% -> 12%
where the time goes in v9:
time: 37.2 us; the launch traced here: 36.9 us
  blocking collectives  12.4 us (33%)
  starting transfers between devices  11.6 us (31%)
  Pallas kernels  8.33 us (22%)
  waiting for transfers between devices  3.58 us (10%)
  between operations  0.7 us (2%)
    all_to_all x1, blocking collectives, per_device(): lax.all_to_all(columns.reshape(owners, 1, each * lane_tile), ('gx', 'gy')...  12.4 us
    ppermute x6, starting transfers between devices, swap(): return lax.ppermute(value, axis, sorted(partner.items()))  9.47 us
    ppermute x6, waiting for transfers between devices, swap(): return lax.ppermute(value, axis, sorted(partner.items()))  2.62 us
    ppermute x3, starting transfers between devices, sum_over(): return value + sum((lax.ppermute(value, axis, table) for table in tables))  2.17 us
    pallas_call x1, Pallas kernels, per_device(): call(functools.partial(pack_kernel, dims, counts), out_shape=[field_shape...  1.63 us
    pallas_call x1, Pallas kernels, per_device(): call(functools.partial(source_kernel, dims, counts), out_shape=[array((sl...  1.59 us
    pallas_call x1, Pallas kernels, per_device(): call(functools.partial(applied_kernel, dims, counts, slots_each), out_sha...  1.42 us
    pallas_call x1, Pallas kernels, per_device(): call(functools.partial(owner_kernel, sensors, slots_each), out_shape=[arr...  1.23 us
  transfers between devices with their start and end apart: 11, of which 3 were waited for; matrix products, arithmetic and copies ran while one was open for 0% of the time, Pallas kernels for 12%

profile of v9, /device:TPU:0, one launch (start us, length us, event | category | flops | bytes accessed | tf_op | source)
XLA Modules:
  0.0 36.9 jit_solution(5741034198013456848)
XLA Ops:
  0.6 1.6 %pack.1 = (f32[1024,128]{1,0:T(8,128)S(1)}, f32[4,8,128]{2,1,0:T(8,128)S(1)}, f32[6,8,128]{2,1,0:T(8,128)S(1)}, s32[1,256]{1,0:T(1,128)S(1)}, s32[1,128]{1,0:T(1...) custom-call(f32[32,4,8,128]{3,2,1,0:T(8,128)} %source_ref.1, ...), custom_call_target="tpu_custom_call" | custom-call | tf_op jit(solution)/shard_map/pack/pallas_call | solution.py:725
  2.3 3.1 %collective-permute-start = (f32[264,128]{1,0:T(8,128)S(1)}, f32[264,128]{1,0:T(8,128)S(1)}, u32[]{:S(2)}, u32[]{:S(2)}) collective-permute-start(f32[264,128]{1,0:T(8,128)S(1)} %get-tuple-element.33), channel_id=1, source_target_pairs={{0,16},{16,0},{1,17},{17,1},{2,18},{18,2},{3,19},{19,3},{4,20},{20... | collective-permute-start | bytes 405512 | tf_op jit(solution)/shard_map/ppermute | solution.py:33
  5.3 1.6 %collective-permute-start.1 = (f32[136,128]{1,0:T(8,128)S(1)}, f32[136,128]{1,0:T(8,128)S(1)}, u32[]{:S(2)}, u32[]{:S(2)}) collective-permute-start(f32[136,128]{1,0:T(8,128)S(1)} %get-tuple-element.34), channel_id=1, source_target_pairs={{0,4},{4,0},{8,12},{12,8},{1,5},{5,1},{9,13},{13,9},{2,6},{6,2},{1... | collective-permute-start | bytes 208904 | tf_op jit(solution)/shard_map/ppermute | solution.py:33
  6.9 0.0 collective-permute-start.2
  6.9 0.5 %collective-permute-start.3 = (f32[40,128]{1,0:T(8,128)S(1)}, f32[40,128]{1,0:T(8,128)S(1)}, u32[]{:S(2)}, u32[]{:S(2)}) collective-permute-start(f32[40,128]{1,0:T(8,128)S(1)} %get-tuple-element.36.own_ref), channel_id=1, source_target_pairs={{0,1},{1,0},{2,3},{3,2},{4,5},{5,4},{6,7},{7,6},{8,9},{9,8},{10,11... | collective-permute-start | bytes 61448 | tf_op jit(solution)/shard_map/ppermute | solution.py:33
  7.4 1.1 %collective-permute-start.4 = (f32[40,128]{1,0:T(8,128)S(1)}, f32[40,128]{1,0:T(8,128)S(1)}, u32[]{:S(2)}, u32[]{:S(2)}) collective-permute-start(f32[40,128]{1,0:T(8,128)S(1)} %get-tuple-element.36.own_ref), channel_id=1, source_target_pairs={{0,3},{1,2},{2,1},{3,0},{4,7},{5,6},{6,5},{7,4},{8,11},{9,10},{10,... | collective-permute-start | bytes 61448 | tf_op jit(solution)/shard_map/ppermute | solution.py:33
  8.5 0.8 %prepare.1 = (bf16[256,4096]{1,0:T(8,128)(2,1)S(1)}, bf16[512,128]{1,0:T(8,128)(2,1)S(1)}, f32[6,8,128]{2,1,0:T(8,128)S(1)}) custom-call(s32[1,256]{1,0:T(1,128)S(1)} %get-tuple-element.29.voxel_ref, s32[1,128]{1,0:T(1,128)S(1)} %get-tuple-element.30.owned_ref, f32[6,8,128]{2,1,0:T(8,128)S(1)} %get-tuple-element.31.level_ref), custom_call_target="tpu_custom_call" | custom-call | tf_op jit(solution)/shard_map/prepare/pallas_call | solution.py:743
  9.3 0.0 collective-permute-done.3.refs_3_
  9.4 1.3 %collective-permute-done.4.refs_4_ = f32[40,128]{1,0:T(8,128)S(1)} collective-permute-done((f32[40,128]{1,0:T(8,128)S(1)}, f32[40,128]{1,0:T(8,128)S(1)}, u32[]{:S(2)}, u32[]{:S(2)}) %collective-permute-start.4) | collective-permute-done | bytes 20512 | tf_op jit(solution)/shard_map/ppermute | solution.py:33
  10.7 0.0 collective-permute-done.1.refs_1_
  10.7 0.0 collective-permute-done.2.refs_2_
  10.7 0.0 collective-permute-done.refs_0_
  10.7 0.6 %apply_ends.1 = (f32[8,4,8,128]{3,2,1,0:T(8,128)S(1)}, f32[40,128]{1,0:T(8,128)S(1)}, f32[512,128]{1,0:T(8,128)S(1)}, f32[296,128]{1,0:T(8,128)S(1)}) custom-call(f32[1024,128]{1,0:T(8,128)S(1)} %get-tuple-element.27.rows_ref, f32[4,8,128]{2,1,0:T(8,128)S(1)} %get-tuple-element.28.shifted_ref, f32[6,8,128]{2,1,0:T(8,128)S(1)} %get-tuple-element.32.table_ref, ...), custom_call_target="tpu_custom_call" | custom-call | tf_op jit(solution)/shard_map/apply_ends/pallas_call | solution.py:756
  11.3 0.6 %collective-permute-start.5 = (f32[296,128]{1,0:T(8,128)S(1)}, f32[296,128]{1,0:T(8,128)S(1)}, u32[]{:S(2)}, u32[]{:S(2)}) collective-permute-start(f32[296,128]{1,0:T(8,128)S(1)} %get-tuple-element.44), channel_id=1, source_target_pairs={{0,16},{16,0},{1,17},{17,1},{2,18},{18,2},{3,19},{19,3},{4,20},{20... | collective-permute-start | bytes 454664 | tf_op jit(solution)/shard_map/ppermute | solution.py:33
  11.8 0.7 %apply.1 = (f32[32,128]{1,0:T(8,128)S(1)}, f32[1024,128]{1,0:T(8,128)S(1)}, f32[168,128]{1,0:T(8,128)S(1)}, f32[168,128]{1,0:T(8,128)S(1)}) custom-call(f32[1024,128]{1,0:T(8,128)S(1)} %get-tuple-element.27.rows_ref, f32[8,4,8,128]{3,2,1,0:T(8,128)S(1)} %get-tuple-element.37.weight_ref, f32[40,128]{1,0:T(8,128)S(1)} %get-tuple-element.38.z_ref, ...), custom_call_target="tpu_custom_call" | custom-call | tf_op jit(solution)/shard_map/apply/pallas_call | solution.py:766
  12.6 2.7 %collective-permute-start.6 = (f32[168,128]{1,0:T(8,128)S(1)}, f32[168,128]{1,0:T(8,128)S(1)}, u32[]{:S(2)}, u32[]{:S(2)}) collective-permute-start(f32[168,128]{1,0:T(8,128)S(1)} %get-tuple-element.45), channel_id=1, source_target_pairs={{0,4},{4,0},{8,12},{12,8},{1,5},{5,1},{9,13},{13,9},{2,6},{6,2},{1... | collective-permute-start | bytes 258056 | tf_op jit(solution)/shard_map/ppermute | solution.py:33
  15.2 0.0 collective-permute-start.7
  15.3 1.6 %source_columns.1 = (f32[256,96]{1,0:T(8,128)S(1)}, f32[128,128]{1,0:T(8,128)S(1)}) custom-call(f32[1024,128]{1,0:T(8,128)S(1)} %get-tuple-element.27.rows_ref, f32[1024,128]{1,0:T(8,128)S(1)} %get-tuple-element.40.applied_ref, f32[8,4,8,128]{3,2,1,0:T(8,128)S(1)} %get-tuple-element.37.weight_ref, bf16[256,4096]{1,0:T(8,128)(2,1)S(1)} %get-tuple-element.41.chosen_ref, ...), custom_call_target="tpu_custom_call" | custom-call | tf_op jit(solution)/shard_map/source_columns/pallas_call | solution.py:776
  16.9 1.3 %collective-permute-done.6.refs_1_ = f32[168,128]{1,0:T(8,128)S(1)} collective-permute-done((f32[168,128]{1,0:T(8,128)S(1)}, f32[168,128]{1,0:T(8,128)S(1)}, u32[]{:S(2)}, u32[]{:S(2)}) %collective-permute-start.6) | collective-permute-done | bytes 86048 | tf_op jit(solution)/shard_map/ppermute | solution.py:33
  18.2 0.0 collective-permute-done.7.refs_2_
  18.2 0.0 collective-permute-done.5.refs_0_
  18.2 0.3 moments.1
  18.5 1.5 %collective-permute-start.10 = (f32[8,128]{1,0:T(8,128)S(1)}, f32[8,128]{1,0:T(8,128)S(1)}, u32[]{:S(2)}, u32[]{:S(2)}) collective-permute-start(f32[8,128]{1,0:T(8,128)S(1)} %get-tuple-element.47), channel_id=1, source_target_pairs={{0,2},{1,3},{2,0},{3,1},{4,6},{5,7},{6,4},{7,5},{8,10},{9,11},{10,... | collective-permute-start | bytes 12296 | tf_op jit(solution)/shard_map/ppermute | solution.py:43
  20.0 0.0 collective-permute-start.8
  20.0 0.6 %collective-permute-start.9 = (f32[8,128]{1,0:T(8,128)S(1)}, f32[8,128]{1,0:T(8,128)S(1)}, u32[]{:S(2)}, u32[]{:S(2)}) collective-permute-start(f32[8,128]{1,0:T(8,128)S(1)} %get-tuple-element.47), channel_id=1, source_target_pairs={{0,1},{1,0},{2,3},{3,2},{4,5},{5,4},{6,7},{7,6},{8,9},{9,8},{10,11... | collective-permute-start | bytes 12296 | tf_op jit(solution)/shard_map/ppermute | solution.py:43
  20.7 1.4 %applied_columns.1 = f32[392,128]{1,0:T(8,128)S(1)} custom-call(f32[1024,128]{1,0:T(8,128)S(1)} %get-tuple-element.40.applied_ref, f32[8,4,8,128]{3,2,1,0:T(8,128)S(1)} %get-tuple-element.37.weight_ref, bf16[256,4096]{1,0:T(8,128)(2,1)S(1)} %get-tuple-element.41.chosen_ref, f32[256,96]{1,0:T(8,128)S(1)} %get-tuple-element.48.source_column_ref, ...), custom_call_target="tpu_custom_call" | custom-call | tf_op jit(solution)/shard_map/applied_columns/pallas_call | solution.py:795
  22.1 0.0 collective-permute-done.10
  22.1 0.9 %collective-permute-done.8 = f32[8,128]{1,0:T(8,128)S(1)} collective-permute-done((f32[8,128]{1,0:T(8,128)S(1)}, f32[8,128]{1,0:T(8,128)S(1)}, u32[]{:S(2)}, u32[]{:S(2)}) %collective-permute-start.8) | collective-permute-done | bytes 4128 | tf_op jit(solution)/shard_map/ppermute | solution.py:43
  23.0 0.0 collective-permute-done.9
  23.1 0.2 fusion
  23.3 12.4 %all_to_all.5 = f32[8,1,6272]{2,1,0:T(1,128)S(1)} all-to-all(f32[8,1,6272]{2,1,0:T(1,128)S(1)} %bitcast.7), channel_id=1, replica_groups=mesh['gx'=2,'gy'=4,'gz'=4] {'gx','gy'}, dimensions={0} | all-to-all | bytes 401408 | tf_op jit(solution)/shard_map/all_to_all | solution.py:807
  35.7 1.2 %owner.1 = (f32[3,128,128]{2,1,0:T(8,128)}, f32[6,128]{1,0:T(8,128)}) custom-call(f32[392,128]{1,0:T(8,128)S(1)} %bitcast.6, bf16[512,128]{1,0:T(8,128)(2,1)S(1)} %get-tuple-element.50.chosen_ref, f32[32,128]{1,0:T(8,128)S(1)} %get-tuple-element.51.data_ref), custom_call_target="tpu_custom_call" | custom-call | tf_op jit(solution)/shard_map/owner/pallas_call | solution.py:810
  (4 shorter events, 0.0 us)
Async XLA Ops:
  2.3 8.4 %collective-permute-start = (f32[264,128]{1,0:T(8,128)S(1)}, f32[264,128]{1,0:T(8,128)S(1)}, u32[]{:S(2)}, u32[]{:S(2)}) collective-permute-start(f32[264,128]{1,0:T(8,128)S(1)} %get-tuple-element.33), channel_id=1, source_target_pairs={{0,16},{16,0},{1,17},{17,1},{2,18},{18,2},{3,19},{19,3},{4,20},{20... | collective-permute-start | bytes 405512 | tf_op jit(solution)/shard_map/ppermute | solution.py:33
  5.3 5.3 %collective-permute-start.1 = (f32[136,128]{1,0:T(8,128)S(1)}, f32[136,128]{1,0:T(8,128)S(1)}, u32[]{:S(2)}, u32[]{:S(2)}) collective-permute-start(f32[136,128]{1,0:T(8,128)S(1)} %get-tuple-element.34), channel_id=1, source_target_pairs={{0,4},{4,0},{8,12},{12,8},{1,5},{5,1},{9,13},{13,9},{2,6},{6,2},{1... | collective-permute-start | bytes 208904 | tf_op jit(solution)/shard_map/ppermute | solution.py:33
  6.9 3.8 %collective-permute-start.2 = (f32[136,128]{1,0:T(8,128)S(1)}, f32[136,128]{1,0:T(8,128)S(1)}, u32[]{:S(2)}, u32[]{:S(2)}) collective-permute-start(f32[136,128]{1,0:T(8,128)S(1)} %get-tuple-element.35), channel_id=1, source_target_pairs={{0,1},{1,0},{2,3},{3,2},{4,8},{5,9},{6,10},{7,11},{8,4},{9,5},{10,... | collective-permute-start | bytes 208904 | tf_op jit(solution)/shard_map/ppermute | solution.py:30
  6.9 2.4 %collective-permute-start.3 = (f32[40,128]{1,0:T(8,128)S(1)}, f32[40,128]{1,0:T(8,128)S(1)}, u32[]{:S(2)}, u32[]{:S(2)}) collective-permute-start(f32[40,128]{1,0:T(8,128)S(1)} %get-tuple-element.36.own_ref), channel_id=1, source_target_pairs={{0,1},{1,0},{2,3},{3,2},{4,5},{5,4},{6,7},{7,6},{8,9},{9,8},{10,11... | collective-permute-start | bytes 61448 | tf_op jit(solution)/shard_map/ppermute | solution.py:33
  7.4 3.2 %collective-permute-start.4 = (f32[40,128]{1,0:T(8,128)S(1)}, f32[40,128]{1,0:T(8,128)S(1)}, u32[]{:S(2)}, u32[]{:S(2)}) collective-permute-start(f32[40,128]{1,0:T(8,128)S(1)} %get-tuple-element.36.own_ref), channel_id=1, source_target_pairs={{0,3},{1,2},{2,1},{3,0},{4,7},{5,6},{6,5},{7,4},{8,11},{9,10},{10,... | collective-permute-start | bytes 61448 | tf_op jit(solution)/shard_map/ppermute | solution.py:33
  11.3 6.9 %collective-permute-start.5 = (f32[296,128]{1,0:T(8,128)S(1)}, f32[296,128]{1,0:T(8,128)S(1)}, u32[]{:S(2)}, u32[]{:S(2)}) collective-permute-start(f32[296,128]{1,0:T(8,128)S(1)} %get-tuple-element.44), channel_id=1, source_target_pairs={{0,16},{16,0},{1,17},{17,1},{2,18},{18,2},{3,19},{19,3},{4,20},{20... | collective-permute-start | bytes 454664 | tf_op jit(solution)/shard_map/ppermute | solution.py:33
  12.6 5.6 %collective-permute-start.6 = (f32[168,128]{1,0:T(8,128)S(1)}, f32[168,128]{1,0:T(8,128)S(1)}, u32[]{:S(2)}, u32[]{:S(2)}) collective-permute-start(f32[168,128]{1,0:T(8,128)S(1)} %get-tuple-element.45), channel_id=1, source_target_pairs={{0,4},{4,0},{8,12},{12,8},{1,5},{5,1},{9,13},{13,9},{2,6},{6,2},{1... | collective-permute-start | bytes 258056 | tf_op jit(solution)/shard_map/ppermute | solution.py:33
  15.2 2.9 %collective-permute-start.7 = (f32[168,128]{1,0:T(8,128)S(1)}, f32[168,128]{1,0:T(8,128)S(1)}, u32[]{:S(2)}, u32[]{:S(2)}) collective-permute-start(f32[168,128]{1,0:T(8,128)S(1)} %get-tuple-element.46), channel_id=1, source_target_pairs={{0,1},{1,0},{2,3},{3,2},{4,8},{5,9},{6,10},{7,11},{8,4},{9,5},{10,... | collective-permute-start | bytes 258056 | tf_op jit(solution)/shard_map/ppermute | solution.py:30
  18.5 3.6 %collective-permute-start.10 = (f32[8,128]{1,0:T(8,128)S(1)}, f32[8,128]{1,0:T(8,128)S(1)}, u32[]{:S(2)}, u32[]{:S(2)}) collective-permute-start(f32[8,128]{1,0:T(8,128)S(1)} %get-tuple-element.47), channel_id=1, source_target_pairs={{0,2},{1,3},{2,0},{3,1},{4,6},{5,7},{6,4},{7,5},{8,10},{9,11},{10,... | collective-permute-start | bytes 12296 | tf_op jit(solution)/shard_map/ppermute | solution.py:43
  20.0 3.0 %collective-permute-start.8 = (f32[8,128]{1,0:T(8,128)S(1)}, f32[8,128]{1,0:T(8,128)S(1)}, u32[]{:S(2)}, u32[]{:S(2)}) collective-permute-start(f32[8,128]{1,0:T(8,128)S(1)} %get-tuple-element.47), channel_id=1, source_target_pairs={{0,3},{1,2},{2,1},{3,0},{4,7},{5,6},{6,5},{7,4},{8,11},{9,10},{10,... | collective-permute-start | bytes 12296 | tf_op jit(solution)/shard_map/ppermute | solution.py:43
  20.0 3.0 %collective-permute-start.9 = (f32[8,128]{1,0:T(8,128)S(1)}, f32[8,128]{1,0:T(8,128)S(1)}, u32[]{:S(2)}, u32[]{:S(2)}) collective-permute-start(f32[8,128]{1,0:T(8,128)S(1)} %get-tuple-element.47), channel_id=1, source_target_pairs={{0,1},{1,0},{2,3},{3,2},{4,5},{5,4},{6,7},{7,6},{8,9},{9,8},{10,11... | collective-permute-start | bytes 12296 | tf_op jit(solution)/shard_map/ppermute | solution.py:43

commit v10 on v8

--- a/solution.py
+++ b/solution.py
@@ -191,7 +191,7 @@
     moves = [(label_ref, label_vmem), *zip(small_hbm, (*small_refs, level_ref))]
     for k, move in enumerate(moves):
         copies.append(pltpu.make_async_copy(*move, semaphores.at[size_x + k]))
-    for copy in copies[size_x:] + copies[:size_x]:
+    for copy in copies:
         copy.start()
     for copy in copies[size_x:]:
         copy.wait()
@@ -565,7 +565,18 @@
         column_ref[at : at + moment_rows, :] = jnp.zeros((moment_rows, lane_tile), jnp.float32)
 
 
-def owner_kernel(sensors, slots_each, received_ref, chosen_ref, data_ref, projection_ref, gram_ref):
+def owner_kernel(
+    sensors,
+    slots_each,
+    received_ref,
+    chosen_ref,
+    data_ref,
+    projection_hbm,
+    gram_hbm,
+    projection_ref,
+    gram_ref,
+    semaphores,
+):
     whole, rest, fold, rows, moment_rows = payload_rows(sensors, slots_each)
     each = rows + moment_rows
     sources = received_ref.shape[0] // each
@@ -622,7 +633,7 @@
             others = others + found[k * rest : (k + 1) * rest, :]
         owned.append(others)
     owned = jnp.concatenate(owned, axis=0)
-    lead = []
+    lead, copies = [], []
     for c in range(3):
         source_part = owned[c * sensors : (c + 1) * sensors, :]
         applied_part = owned[(3 + c) * sensors : (4 + c) * sensors, :]
@@ -634,8 +645,16 @@
             precision=lax.Precision.HIGHEST,
             preferred_element_type=jnp.float32,
         )
+        copies.append(
+            pltpu.make_async_copy(projection_ref.at[c], projection_hbm.at[c], semaphores.at[c])
+        )
+        copies[c].start()
     for k, (first, second) in enumerate(entry_pairs):
         gram_ref[k : k + 1, :] = jnp.sum(lead[first] * lead[second], axis=0, keepdims=True)
+    copies.append(pltpu.make_async_copy(gram_ref, gram_hbm, semaphores.at[3]))
+    copies[3].start()
+    for copy in copies:
+        copy.wait()
 
 
 def call(body, **arguments):
@@ -775,7 +794,12 @@
         functools.partial(owner_kernel, sensors, slots_each),
         out_shape=[array((3, times, positions)), array((6, positions))],
         in_specs=in_vmem(3),
-        out_specs=in_vmem(2),
+        out_specs=in_hbm(2),
+        scratch_shapes=[
+            pltpu.VMEM((3, times, positions), jnp.float32),
+            pltpu.VMEM((6, positions), jnp.float32),
+            pltpu.SemaphoreType.DMA((4,)),
+        ],
         name="owner",
     )(received, owned_chosen, data)
 

time: 37.1 us -> 36.9 us (level)
  no operation moved by 1% of the time
where the time goes in v10:
time: 36.9 us; the launch traced here: 36.8 us
  blocking collectives  12.3 us (33%)
  starting transfers between devices  11.6 us (31%)
  Pallas kernels  8.41 us (23%)
  waiting for transfers between devices  3.46 us (9%)
  between operations  0.7 us (2%)
    all_to_all x1, blocking collectives, per_device(): lax.all_to_all(columns.reshape(owners, 1, each * lane_tile), ('gx', 'gy')...  12.3 us
    ppermute x6, starting transfers between devices, swap(): return lax.ppermute(value, axis, sorted(partner.items()))  9.4 us
    ppermute x6, waiting for transfers between devices, swap(): return lax.ppermute(value, axis, sorted(partner.items()))  2.53 us
    ppermute x3, starting transfers between devices, sum_over(): return value + sum((lax.ppermute(value, axis, table) for table in tables))  2.17 us
    pallas_call x1, Pallas kernels, per_device(): call(functools.partial(source_kernel, dims, counts), out_shape=[array((sl...  1.68 us
    pallas_call x1, Pallas kernels, per_device(): call(functools.partial(pack_kernel, dims, counts), out_shape=[field_shape...  1.59 us
    pallas_call x1, Pallas kernels, per_device(): call(functools.partial(applied_kernel, dims, counts, slots_each), out_sha...  1.44 us
    pallas_call x1, Pallas kernels, per_device(): call(functools.partial(apply_kernel, dims, counts), out_shape=[array((8,...  1.35 us
  transfers between devices with their start and end apart: 11, of which 3 were waited for; matrix products, arithmetic and copies ran while one was open for 0% of the time, Pallas kernels for 11%

profile of v10, /device:TPU:0, one launch (start us, length us, event | category | flops | bytes accessed | tf_op | source)
XLA Modules:
  0.0 36.8 jit_solution(16828411558699224158)
XLA Ops:
  0.6 1.6 %pack.1 = (f32[1024,128]{1,0:T(8,128)S(1)}, f32[4,8,128]{2,1,0:T(8,128)S(1)}, f32[6,8,128]{2,1,0:T(8,128)S(1)}, s32[1,256]{1,0:T(1,128)S(1)}, s32[1,128]{1,0:T(1...) custom-call(f32[32,4,8,128]{3,2,1,0:T(8,128)} %source_ref.1, ...), custom_call_target="tpu_custom_call" | custom-call | tf_op jit(solution)/shard_map/pack/pallas_call | solution.py:716
  2.2 3.1 %collective-permute-start = (f32[264,128]{1,0:T(8,128)S(1)}, f32[264,128]{1,0:T(8,128)S(1)}, u32[]{:S(2)}, u32[]{:S(2)}) collective-permute-start(f32[264,128]{1,0:T(8,128)S(1)} %get-tuple-element.32), channel_id=1, source_target_pairs={{0,16},{16,0},{1,17},{17,1},{2,18},{18,2},{3,19},{19,3},{4,20},{20... | collective-permute-start | bytes 405512 | tf_op jit(solution)/shard_map/ppermute | solution.py:33
  5.3 1.6 %collective-permute-start.1 = (f32[136,128]{1,0:T(8,128)S(1)}, f32[136,128]{1,0:T(8,128)S(1)}, u32[]{:S(2)}, u32[]{:S(2)}) collective-permute-start(f32[136,128]{1,0:T(8,128)S(1)} %get-tuple-element.33), channel_id=1, source_target_pairs={{0,4},{4,0},{8,12},{12,8},{1,5},{5,1},{9,13},{13,9},{2,6},{6,2},{1... | collective-permute-start | bytes 208904 | tf_op jit(solution)/shard_map/ppermute | solution.py:33
  6.9 0.0 collective-permute-start.2
  6.9 0.5 %collective-permute-start.3 = (f32[40,128]{1,0:T(8,128)S(1)}, f32[40,128]{1,0:T(8,128)S(1)}, u32[]{:S(2)}, u32[]{:S(2)}) collective-permute-start(f32[40,128]{1,0:T(8,128)S(1)} %get-tuple-element.35.own_ref), channel_id=1, source_target_pairs={{0,1},{1,0},{2,3},{3,2},{4,5},{5,4},{6,7},{7,6},{8,9},{9,8},{10,11... | collective-permute-start | bytes 61448 | tf_op jit(solution)/shard_map/ppermute | solution.py:33
  7.4 1.1 %collective-permute-start.4 = (f32[40,128]{1,0:T(8,128)S(1)}, f32[40,128]{1,0:T(8,128)S(1)}, u32[]{:S(2)}, u32[]{:S(2)}) collective-permute-start(f32[40,128]{1,0:T(8,128)S(1)} %get-tuple-element.35.own_ref), channel_id=1, source_target_pairs={{0,3},{1,2},{2,1},{3,0},{4,7},{5,6},{6,5},{7,4},{8,11},{9,10},{10,... | collective-permute-start | bytes 61448 | tf_op jit(solution)/shard_map/ppermute | solution.py:33
  8.5 0.8 %prepare.1 = (bf16[256,4096]{1,0:T(8,128)(2,1)S(1)}, bf16[512,128]{1,0:T(8,128)(2,1)S(1)}, f32[6,8,128]{2,1,0:T(8,128)S(1)}) custom-call(s32[1,256]{1,0:T(1,128)S(1)} %get-tuple-element.28.voxel_ref, s32[1,128]{1,0:T(1,128)S(1)} %get-tuple-element.29.owned_ref, f32[6,8,128]{2,1,0:T(8,128)S(1)} %get-tuple-element.30.level_ref), custom_call_target="tpu_custom_call" | custom-call | tf_op jit(solution)/shard_map/prepare/pallas_call | solution.py:734
  9.3 0.0 collective-permute-done.3.refs_3_
  9.3 1.3 %collective-permute-done.4.refs_4_ = f32[40,128]{1,0:T(8,128)S(1)} collective-permute-done((f32[40,128]{1,0:T(8,128)S(1)}, f32[40,128]{1,0:T(8,128)S(1)}, u32[]{:S(2)}, u32[]{:S(2)}) %collective-permute-start.4) | collective-permute-done | bytes 20512 | tf_op jit(solution)/shard_map/ppermute | solution.py:33
  10.6 0.0 collective-permute-done.1.refs_1_
  10.6 0.0 collective-permute-done.2.refs_2_
  10.6 0.0 collective-permute-done.refs_0_
  10.6 1.4 %apply.1 = (f32[8,4,8,128]{3,2,1,0:T(8,128)S(1)}, f32[32,128]{1,0:T(8,128)S(1)}, f32[1024,128]{1,0:T(8,128)S(1)}, f32[40,128]{1,0:T(8,128)S(1)}, f32[296,128]{1,...) custom-call(f32[1024,128]{1,0:T(8,128)S(1)} %get-tuple-element.26.rows_ref, ...), custom_call_target="tpu_custom_call" | custom-call | tf_op jit(solution)/shard_map/apply/pallas_call | solution.py:746
  12.0 0.6 %collective-permute-start.5 = (f32[296,128]{1,0:T(8,128)S(1)}, f32[296,128]{1,0:T(8,128)S(1)}, u32[]{:S(2)}, u32[]{:S(2)}) collective-permute-start(f32[296,128]{1,0:T(8,128)S(1)} %get-tuple-element.42), channel_id=1, source_target_pairs={{0,16},{16,0},{1,17},{17,1},{2,18},{18,2},{3,19},{19,3},{4,20},{20... | collective-permute-start | bytes 454664 | tf_op jit(solution)/shard_map/ppermute | solution.py:33
  12.5 2.6 %collective-permute-start.6 = (f32[168,128]{1,0:T(8,128)S(1)}, f32[168,128]{1,0:T(8,128)S(1)}, u32[]{:S(2)}, u32[]{:S(2)}) collective-permute-start(f32[168,128]{1,0:T(8,128)S(1)} %get-tuple-element.43), channel_id=1, source_target_pairs={{0,4},{4,0},{8,12},{12,8},{1,5},{5,1},{9,13},{13,9},{2,6},{6,2},{1... | collective-permute-start | bytes 258056 | tf_op jit(solution)/shard_map/ppermute | solution.py:33
  15.1 0.0 collective-permute-start.7
  15.2 1.7 %source_columns.1 = (f32[256,96]{1,0:T(8,128)S(1)}, f32[128,128]{1,0:T(8,128)S(1)}) custom-call(f32[1024,128]{1,0:T(8,128)S(1)} %get-tuple-element.26.rows_ref, f32[1024,128]{1,0:T(8,128)S(1)} %get-tuple-element.36.applied_ref, f32[8,4,8,128]{3,2,1,0:T(8,128)S(1)} %get-tuple-element.37.weight_ref, bf16[256,4096]{1,0:T(8,128)(2,1)S(1)} %get-tuple-element.38.chosen_ref, ...), custom_call_target="tpu_custom_call" | custom-call | tf_op jit(solution)/shard_map/source_columns/pallas_call | solution.py:759
  16.8 1.2 %collective-permute-done.6.refs_1_ = f32[168,128]{1,0:T(8,128)S(1)} collective-permute-done((f32[168,128]{1,0:T(8,128)S(1)}, f32[168,128]{1,0:T(8,128)S(1)}, u32[]{:S(2)}, u32[]{:S(2)}) %collective-permute-start.6) | collective-permute-done | bytes 86048 | tf_op jit(solution)/shard_map/ppermute | solution.py:33
  18.1 0.0 collective-permute-done.7.refs_2_
  18.1 0.0 collective-permute-done.5.refs_0_
  18.1 0.3 moments.1
  18.4 1.5 %collective-permute-start.10 = (f32[8,128]{1,0:T(8,128)S(1)}, f32[8,128]{1,0:T(8,128)S(1)}, u32[]{:S(2)}, u32[]{:S(2)}) collective-permute-start(f32[8,128]{1,0:T(8,128)S(1)} %get-tuple-element.45), channel_id=1, source_target_pairs={{0,2},{1,3},{2,0},{3,1},{4,6},{5,7},{6,4},{7,5},{8,10},{9,11},{10,... | collective-permute-start | bytes 12296 | tf_op jit(solution)/shard_map/ppermute | solution.py:43
  19.9 0.0 collective-permute-start.8
  19.9 0.6 %collective-permute-start.9 = (f32[8,128]{1,0:T(8,128)S(1)}, f32[8,128]{1,0:T(8,128)S(1)}, u32[]{:S(2)}, u32[]{:S(2)}) collective-permute-start(f32[8,128]{1,0:T(8,128)S(1)} %get-tuple-element.45), channel_id=1, source_target_pairs={{0,1},{1,0},{2,3},{3,2},{4,5},{5,4},{6,7},{7,6},{8,9},{9,8},{10,11... | collective-permute-start | bytes 12296 | tf_op jit(solution)/shard_map/ppermute | solution.py:43
  20.6 1.4 %applied_columns.1 = f32[392,128]{1,0:T(8,128)S(1)} custom-call(f32[1024,128]{1,0:T(8,128)S(1)} %get-tuple-element.36.applied_ref, f32[8,4,8,128]{3,2,1,0:T(8,128)S(1)} %get-tuple-element.37.weight_ref, bf16[256,4096]{1,0:T(8,128)(2,1)S(1)} %get-tuple-element.38.chosen_ref, f32[256,96]{1,0:T(8,128)S(1)} %get-tuple-element.46.source_column_ref, ...), custom_call_target="tpu_custom_call" | custom-call | tf_op jit(solution)/shard_map/applied_columns/pallas_call | solution.py:778
  22.0 0.0 collective-permute-done.10
  22.0 0.9 %collective-permute-done.8 = f32[8,128]{1,0:T(8,128)S(1)} collective-permute-done((f32[8,128]{1,0:T(8,128)S(1)}, f32[8,128]{1,0:T(8,128)S(1)}, u32[]{:S(2)}, u32[]{:S(2)}) %collective-permute-start.8) | collective-permute-done | bytes 4128 | tf_op jit(solution)/shard_map/ppermute | solution.py:43
  22.9 0.0 collective-permute-done.9
  23.0 0.2 fusion
  23.2 12.3 %all_to_all.5 = f32[8,1,6272]{2,1,0:T(1,128)S(1)} all-to-all(f32[8,1,6272]{2,1,0:T(1,128)S(1)} %bitcast.7), channel_id=1, replica_groups=mesh['gx'=2,'gy'=4,'gz'=4] {'gx','gy'}, dimensions={0} | all-to-all | bytes 401408 | tf_op jit(solution)/shard_map/all_to_all | solution.py:790
  35.5 1.2 %owner.1 = (f32[3,128,128]{2,1,0:T(8,128)}, f32[6,128]{1,0:T(8,128)}) custom-call(f32[392,128]{1,0:T(8,128)S(1)} %bitcast.6, bf16[512,128]{1,0:T(8,128)(2,1)S(1)} %get-tuple-element.48.chosen_ref, f32[32,128]{1,0:T(8,128)S(1)} %get-tuple-element.49.data_ref), custom_call_target="tpu_custom_call" | custom-call | tf_op jit(solution)/shard_map/owner/pallas_call | solution.py:793
  (4 shorter events, 0.0 us)
Async XLA Ops:
  2.2 8.4 %collective-permute-start = (f32[264,128]{1,0:T(8,128)S(1)}, f32[264,128]{1,0:T(8,128)S(1)}, u32[]{:S(2)}, u32[]{:S(2)}) collective-permute-start(f32[264,128]{1,0:T(8,128)S(1)} %get-tuple-element.32), channel_id=1, source_target_pairs={{0,16},{16,0},{1,17},{17,1},{2,18},{18,2},{3,19},{19,3},{4,20},{20... | collective-permute-start | bytes 405512 | tf_op jit(solution)/shard_map/ppermute | solution.py:33
  5.3 5.3 %collective-permute-start.1 = (f32[136,128]{1,0:T(8,128)S(1)}, f32[136,128]{1,0:T(8,128)S(1)}, u32[]{:S(2)}, u32[]{:S(2)}) collective-permute-start(f32[136,128]{1,0:T(8,128)S(1)} %get-tuple-element.33), channel_id=1, source_target_pairs={{0,4},{4,0},{8,12},{12,8},{1,5},{5,1},{9,13},{13,9},{2,6},{6,2},{1... | collective-permute-start | bytes 208904 | tf_op jit(solution)/shard_map/ppermute | solution.py:33
  6.9 3.8 %collective-permute-start.2 = (f32[136,128]{1,0:T(8,128)S(1)}, f32[136,128]{1,0:T(8,128)S(1)}, u32[]{:S(2)}, u32[]{:S(2)}) collective-permute-start(f32[136,128]{1,0:T(8,128)S(1)} %get-tuple-element.34), channel_id=1, source_target_pairs={{0,1},{1,0},{2,3},{3,2},{4,8},{5,9},{6,10},{7,11},{8,4},{9,5},{10,... | collective-permute-start | bytes 208904 | tf_op jit(solution)/shard_map/ppermute | solution.py:30
  6.9 2.4 %collective-permute-start.3 = (f32[40,128]{1,0:T(8,128)S(1)}, f32[40,128]{1,0:T(8,128)S(1)}, u32[]{:S(2)}, u32[]{:S(2)}) collective-permute-start(f32[40,128]{1,0:T(8,128)S(1)} %get-tuple-element.35.own_ref), channel_id=1, source_target_pairs={{0,1},{1,0},{2,3},{3,2},{4,5},{5,4},{6,7},{7,6},{8,9},{9,8},{10,11... | collective-permute-start | bytes 61448 | tf_op jit(solution)/shard_map/ppermute | solution.py:33
  7.4 3.2 %collective-permute-start.4 = (f32[40,128]{1,0:T(8,128)S(1)}, f32[40,128]{1,0:T(8,128)S(1)}, u32[]{:S(2)}, u32[]{:S(2)}) collective-permute-start(f32[40,128]{1,0:T(8,128)S(1)} %get-tuple-element.35.own_ref), channel_id=1, source_target_pairs={{0,3},{1,2},{2,1},{3,0},{4,7},{5,6},{6,5},{7,4},{8,11},{9,10},{10,... | collective-permute-start | bytes 61448 | tf_op jit(solution)/shard_map/ppermute | solution.py:33
  12.0 6.1 %collective-permute-start.5 = (f32[296,128]{1,0:T(8,128)S(1)}, f32[296,128]{1,0:T(8,128)S(1)}, u32[]{:S(2)}, u32[]{:S(2)}) collective-permute-start(f32[296,128]{1,0:T(8,128)S(1)} %get-tuple-element.42), channel_id=1, source_target_pairs={{0,16},{16,0},{1,17},{17,1},{2,18},{18,2},{3,19},{19,3},{4,20},{20... | collective-permute-start | bytes 454664 | tf_op jit(solution)/shard_map/ppermute | solution.py:33
  12.5 5.5 %collective-permute-start.6 = (f32[168,128]{1,0:T(8,128)S(1)}, f32[168,128]{1,0:T(8,128)S(1)}, u32[]{:S(2)}, u32[]{:S(2)}) collective-permute-start(f32[168,128]{1,0:T(8,128)S(1)} %get-tuple-element.43), channel_id=1, source_target_pairs={{0,4},{4,0},{8,12},{12,8},{1,5},{5,1},{9,13},{13,9},{2,6},{6,2},{1... | collective-permute-start | bytes 258056 | tf_op jit(solution)/shard_map/ppermute | solution.py:33
  15.1 2.9 %collective-permute-start.7 = (f32[168,128]{1,0:T(8,128)S(1)}, f32[168,128]{1,0:T(8,128)S(1)}, u32[]{:S(2)}, u32[]{:S(2)}) collective-permute-start(f32[168,128]{1,0:T(8,128)S(1)} %get-tuple-element.44), channel_id=1, source_target_pairs={{0,1},{1,0},{2,3},{3,2},{4,8},{5,9},{6,10},{7,11},{8,4},{9,5},{10,... | collective-permute-start | bytes 258056 | tf_op jit(solution)/shard_map/ppermute | solution.py:30
  18.4 3.6 %collective-permute-start.10 = (f32[8,128]{1,0:T(8,128)S(1)}, f32[8,128]{1,0:T(8,128)S(1)}, u32[]{:S(2)}, u32[]{:S(2)}) collective-permute-start(f32[8,128]{1,0:T(8,128)S(1)} %get-tuple-element.45), channel_id=1, source_target_pairs={{0,2},{1,3},{2,0},{3,1},{4,6},{5,7},{6,4},{7,5},{8,10},{9,11},{10,... | collective-permute-start | bytes 12296 | tf_op jit(solution)/shard_map/ppermute | solution.py:43
  19.9 3.0 %collective-permute-start.8 = (f32[8,128]{1,0:T(8,128)S(1)}, f32[8,128]{1,0:T(8,128)S(1)}, u32[]{:S(2)}, u32[]{:S(2)}) collective-permute-start(f32[8,128]{1,0:T(8,128)S(1)} %get-tuple-element.45), channel_id=1, source_target_pairs={{0,3},{1,2},{2,1},{3,0},{4,7},{5,6},{6,5},{7,4},{8,11},{9,10},{10,... | collective-permute-start | bytes 12296 | tf_op jit(solution)/shard_map/ppermute | solution.py:43
  19.9 3.0 %collective-permute-start.9 = (f32[8,128]{1,0:T(8,128)S(1)}, f32[8,128]{1,0:T(8,128)S(1)}, u32[]{:S(2)}, u32[]{:S(2)}) collective-permute-start(f32[8,128]{1,0:T(8,128)S(1)} %get-tuple-element.45), channel_id=1, source_target_pairs={{0,1},{1,0},{2,3},{3,2},{4,5},{5,4},{6,7},{7,6},{8,9},{9,8},{10,11... | collective-permute-start | bytes 12296 | tf_op jit(solution)/shard_map/ppermute | solution.py:43
